TPU v7x, 32 devices: a whole 2x2x4 slice. The times are simulated.
32 devices in a mesh: dp: 16 (over z, y, x), fsdp: 2 (over core).
Axes of the slice: x: 2, y: 2, z: 4, core: 2. Of those that a mesh axis runs over, the one named last changes fastest.
Arguments:
- block_input: float32 [2, 2048, 768], P(None, ('dp', 'fsdp')), may hold values from -6 to 6
- out_grad: float32 [2, 2048, 768], P(None, ('dp', 'fsdp')), may hold values from -6 to 6
- seg_ids: int32 [2, 2048], P(None, ('dp', 'fsdp')), may hold values from -1 to 7, as said below
- params: float32 [7087872], P(('dp', 'fsdp')), as said below
- first_moment: float32 [7087872], P(('dp', 'fsdp')), may hold values from -6 to 6
- second_moment: float32 [7087872], P(('dp', 'fsdp')), may hold values from 1 to 10
Outputs:
- block_output: float32 [2, 2048, 768], P(None, ('dp', 'fsdp'))
- input_grad: float32 [2, 2048, 768], P(None, ('dp', 'fsdp'))
- param_grad: float32 [7087872], P(('dp', 'fsdp'))
- new_params: float32 [7087872], P(('dp', 'fsdp'))
- new_first: float32 [7087872], P(('dp', 'fsdp'))
- new_second: float32 [7087872], P(('dp', 'fsdp'))
Inputs may be any that keep to these rules, and one draw needn't show every extreme that they name: `seg_ids`: in each block of 64 slots, ids count the sequences 0, 1, 2, ... in order from the block's first slot, each sequence contiguous, at most 8 sequences a block; the block ends in padding with id -1, at least one slot of it; blocks differ in how much is padding. `params`: laid out as the steps read it.
All inputs are finite; a program needn't handle non-finite values.
Results may differ from a plain program's by a relative error of at most 0.012.
Values may be sent and summed in bfloat16 or wider, within the bound.
No kernel may reach another device: no remote copies, remote signals or barrier semaphores. Data moves between devices by JAX's collectives and lax.ppermute only.
A program may use at most 256 MiB of HBM per device.

v0:
```python
import math

import jax
import jax.numpy as jnp
from jax import lax
from jax.sharding import PartitionSpec as P

D = 768
FF = 3072
HEADS = 12
HEAD_DIM = 64
ROT = 16
STEP = 3


NORM_EPS = 1e-05
BETA_ONE = 0.9
BETA_TWO = 0.95
LEARN_RATE = 0.05
WEIGHT_DECAY = 0.1
ADAM_EPS = 1e-08


def layout_shapes():
    return [
        (D, 3 * D),
        (D, D),
        (D, FF),
        (FF, D),
        (3 * D,),
        (D,),
        (FF,),
        (D,),
        (D,),
        (D,),
        (D,),
        (D,),
    ]


def unpack_flat(flat_vec):
    pieces_out = []
    offset = 0
    for item_shape in layout_shapes():
        length = math.prod(item_shape)
        pieces_out.append(flat_vec[offset : offset + length].reshape(item_shape))
        offset += length
    return pieces_out


def product(form, left, right):
    return jnp.einsum(form, left, right, preferred_element_type=jnp.float32)


def block_tables(seg_rows):
    row_count = seg_rows.shape[1]
    row_idx = jnp.arange(row_count)
    same_seq = seg_rows[:, :, None] == seg_rows[:, None, :]
    earlier = row_idx[None, :] < row_idx[:, None]
    diagonal = row_idx[None, :] == row_idx[:, None]
    causal = row_idx[None, :] <= row_idx[:, None]
    allowed = same_seq & causal[None] & ((seg_rows[:, :, None] >= 0) | diagonal[None])
    position = jnp.sum(jnp.where(same_seq & earlier[None], 1, 0), axis=2).astype(jnp.float32)
    inv_freq = 10000.0 ** (-(jnp.arange(ROT // 2, dtype=jnp.float32) * 2.0) / ROT)
    angles = position[:, :, None] * inv_freq[None, None, :]
    return (allowed, jnp.cos(angles)[:, :, None, :], jnp.sin(angles)[:, :, None, :])


def rotate(vecs, cos_t, sin_t):
    half_rot = ROT // 2
    first = vecs[..., :half_rot]
    second = vecs[..., half_rot:ROT]
    return jnp.concatenate(
        [first * cos_t - second * sin_t, second * cos_t + first * sin_t, vecs[..., ROT:]], axis=-1
    )


def unrotate(vecs, cos_t, sin_t):
    half_rot = ROT // 2
    first = vecs[..., :half_rot]
    second = vecs[..., half_rot:ROT]
    return jnp.concatenate(
        [first * cos_t + second * sin_t, second * cos_t - first * sin_t, vecs[..., ROT:]], axis=-1
    )


def layer_norm(flat_x, gain, shift):
    row_mean = jnp.mean(flat_x, axis=-1, keepdims=True)
    centred = flat_x - row_mean
    row_var = jnp.mean(centred * centred, axis=-1, keepdims=True)
    inv_std = lax.rsqrt(row_var + NORM_EPS)
    normed = centred * inv_std
    return (
        normed,
        inv_std,
        (normed * gain.astype(jnp.float32) + shift.astype(jnp.float32)).astype(jnp.bfloat16),
    )


def norm_back(grad_act, normed, inv_std, gain):
    grad_gain = jnp.sum(grad_act * normed, axis=0)
    grad_shift = jnp.sum(grad_act, axis=0)
    scaled = grad_act * gain.astype(jnp.float32)
    grad_in = inv_std * (
        scaled
        - jnp.mean(scaled, axis=-1, keepdims=True)
        - normed * jnp.mean(scaled * normed, axis=-1, keepdims=True)
    )
    return (grad_gain, grad_shift, grad_in)


def softmax_rows(query_bf, key_bf, allowed, log_total):
    scores = product("gqhd,gkhd->ghqk", query_bf, key_bf) * HEAD_DIM ** (-0.5)
    mask_b = allowed[:, None]
    masked = jnp.where(mask_b, scores, -jnp.inf)
    if log_total is None:
        top_score = jnp.max(masked, axis=-1, keepdims=True)
        expo = jnp.where(mask_b, jnp.exp(masked - top_score), 0.0)
        log_total = top_score + jnp.log(jnp.sum(expo, axis=-1, keepdims=True))
    prob_rows = jnp.where(mask_b, jnp.exp(masked - log_total), 0.0)
    return (prob_rows, log_total)


def forward(x_rows, seg_rows, weights):
    (
        w_qkv,
        w_out,
        w_up,
        w_down,
        b_qkv,
        b_out,
        b_up,
        b_down,
        gain_one,
        shift_one,
        gain_two,
        shift_two,
    ) = weights
    group_count, row_count = seg_rows.shape
    allowed, cos_t, sin_t = block_tables(seg_rows)
    flat_x = x_rows.reshape(group_count * row_count, D)
    normed_one, inv_one, act_one = layer_norm(flat_x, gain_one, shift_one)
    normed_two, inv_two, act_two = layer_norm(flat_x, gain_two, shift_two)
    qkv_rows = jnp.dot(act_one, w_qkv, preferred_element_type=jnp.float32) + b_qkv.astype(
        jnp.float32
    )
    qkv_rows = qkv_rows.reshape(group_count, row_count, 3, HEADS, HEAD_DIM)
    query_bf = rotate(qkv_rows[:, :, 0], cos_t, sin_t).astype(jnp.bfloat16)
    key_bf = rotate(qkv_rows[:, :, 1], cos_t, sin_t).astype(jnp.bfloat16)
    value_bf = qkv_rows[:, :, 2].astype(jnp.bfloat16)
    prob_rows, log_total = softmax_rows(query_bf, key_bf, allowed, None)
    prob_bf = prob_rows.astype(jnp.bfloat16)
    attn_bf = (
        product("ghqk,gkhd->gqhd", prob_bf, value_bf)
        .astype(jnp.bfloat16)
        .reshape(group_count * row_count, D)
    )
    attn_out = jnp.dot(attn_bf, w_out, preferred_element_type=jnp.float32) + b_out.astype(
        jnp.float32
    )
    up_rows = jnp.dot(act_two, w_up, preferred_element_type=jnp.float32) + b_up.astype(jnp.float32)
    hidden_bf = jax.nn.gelu(up_rows, approximate=False).astype(jnp.bfloat16)
    mlp_out = jnp.dot(hidden_bf, w_down, preferred_element_type=jnp.float32) + b_down.astype(
        jnp.float32
    )
    result = flat_x + attn_out + mlp_out
    kept_state = (
        normed_one,
        inv_one,
        act_one,
        normed_two,
        inv_two,
        act_two,
        query_bf,
        key_bf,
        value_bf,
        log_total,
        attn_bf,
        up_rows,
        hidden_bf,
        allowed,
        cos_t,
        sin_t,
        seg_rows,
    )
    return (result.reshape(group_count, row_count, D), kept_state)


def backward(kept_state, grad_rows, weights):
    (
        w_qkv,
        w_out,
        w_up,
        w_down,
        b_qkv,
        b_out,
        b_up,
        b_down,
        gain_one,
        shift_one,
        gain_two,
        shift_two,
    ) = weights
    (
        normed_one,
        inv_one,
        act_one,
        normed_two,
        inv_two,
        act_two,
        query_bf,
        key_bf,
        value_bf,
        log_total,
        attn_bf,
        up_rows,
        hidden_bf,
        allowed,
        cos_t,
        sin_t,
        seg_rows,
    ) = kept_state
    group_count, row_count = seg_rows.shape
    valid = (seg_rows >= 0).astype(jnp.float32).reshape(group_count * row_count, 1)
    grad_y = grad_rows.reshape(group_count * row_count, D) * valid
    grad_y_bf = grad_y.astype(jnp.bfloat16)
    grad_bias = jnp.sum(grad_y, axis=0)
    grad_w_down = jnp.dot(hidden_bf.T, grad_y_bf, preferred_element_type=jnp.float32)
    grad_w_out = jnp.dot(attn_bf.T, grad_y_bf, preferred_element_type=jnp.float32)
    grad_hidden = jnp.dot(grad_y_bf, w_down.T, preferred_element_type=jnp.float32)
    cdf_part = 0.5 * (1.0 + jax.scipy.special.erf(up_rows * 0.7071067811865476))
    pdf_part = jnp.exp(-0.5 * up_rows * up_rows) * 0.3989422804014327
    grad_up = grad_hidden * (cdf_part + up_rows * pdf_part)
    grad_b_up = jnp.sum(grad_up, axis=0)
    grad_up_bf = grad_up.astype(jnp.bfloat16)
    grad_w_up = jnp.dot(act_two.T, grad_up_bf, preferred_element_type=jnp.float32)
    grad_act_two = jnp.dot(grad_up_bf, w_up.T, preferred_element_type=jnp.float32)
    grad_attn = jnp.dot(grad_y_bf, w_out.T, preferred_element_type=jnp.float32).astype(jnp.bfloat16)
    grad_attn = grad_attn.reshape(group_count, row_count, HEADS, HEAD_DIM)
    prob_rows, unused_total = softmax_rows(query_bf, key_bf, allowed, log_total)
    prob_bf = prob_rows.astype(jnp.bfloat16)
    grad_value = product("ghqk,gqhd->gkhd", prob_bf, grad_attn)
    grad_prob = product("gqhd,gkhd->ghqk", grad_attn, value_bf)
    delta_rows = jnp.sum(prob_rows * grad_prob, axis=-1, keepdims=True)
    grad_score_bf = (prob_rows * (grad_prob - delta_rows) * HEAD_DIM ** (-0.5)).astype(jnp.bfloat16)
    grad_query = unrotate(product("ghqk,gkhd->gqhd", grad_score_bf, key_bf), cos_t, sin_t)
    grad_key = unrotate(product("ghqk,gqhd->gkhd", grad_score_bf, query_bf), cos_t, sin_t)
    grad_qkv = jnp.stack([grad_query, grad_key, grad_value], axis=2).reshape(
        group_count * row_count, 3 * D
    )
    grad_b_qkv = jnp.sum(grad_qkv, axis=0)
    grad_qkv_bf = grad_qkv.astype(jnp.bfloat16)
    grad_w_qkv = jnp.dot(act_one.T, grad_qkv_bf, preferred_element_type=jnp.float32)
    grad_act_one = jnp.dot(grad_qkv_bf, w_qkv.T, preferred_element_type=jnp.float32)
    grad_gain_one, grad_shift_one, back_one = norm_back(grad_act_one, normed_one, inv_one, gain_one)
    grad_gain_two, grad_shift_two, back_two = norm_back(grad_act_two, normed_two, inv_two, gain_two)
    input_grad = (grad_y + back_one + back_two).reshape(group_count, row_count, D)
    grads = (
        grad_w_qkv,
        grad_w_out,
        grad_w_up,
        grad_w_down,
        grad_b_qkv,
        grad_bias,
        grad_b_up,
        grad_bias,
        grad_gain_one,
        grad_shift_one,
        grad_gain_two,
        grad_shift_two,
    )
    return (input_grad, grads)


def adam_update(params, grads, first_moment, second_moment):
    new_first = BETA_ONE * first_moment + (1.0 - BETA_ONE) * grads
    new_second = BETA_TWO * second_moment + (1.0 - BETA_TWO) * grads * grads
    first_hat = new_first / (1.0 - BETA_ONE**STEP)
    second_hat = new_second / (1.0 - BETA_TWO**STEP)
    new_params = params - LEARN_RATE * (
        first_hat / (jnp.sqrt(second_hat) + ADAM_EPS) + WEIGHT_DECAY * params
    )
    return (new_params, new_first, new_second)


def flatten_grads(grads):
    return jnp.concatenate([part.reshape(-1) for part in grads])


def body(block_input, out_grad, seg_ids, params, first_moment, second_moment):
    micro_count = block_input.shape[0]
    sent_params = params.astype(jnp.bfloat16)
    grad_total = None
    owned_grads = None
    outputs = []
    input_grads = []
    for batch_index in range(micro_count):
        weights = unpack_flat(lax.all_gather(sent_params, ("dp", "fsdp"), axis=0, tiled=True))
        result, kept_state = forward(
            block_input[batch_index][None], seg_ids[batch_index][None], weights
        )
        back_x, grads = backward(kept_state, out_grad[batch_index][None], weights)
        outputs.append(result[0])
        input_grads.append(back_x[0])
        flat_grads = flatten_grads(grads)
        grad_total = flat_grads if grad_total is None else grad_total + flat_grads
    owned_grads = lax.psum_scatter(grad_total, ("dp", "fsdp"), scatter_dimension=0, tiled=True)
    new_params, new_first, new_second = adam_update(
        params, owned_grads, first_moment, second_moment
    )
    return (
        jnp.stack(outputs),
        jnp.stack(input_grads),
        owned_grads,
        new_params,
        new_first,
        new_second,
    )


def solution(mesh):
    in_specs = (
        P(None, ("dp", "fsdp"), None),
        P(None, ("dp", "fsdp"), None),
        P(None, ("dp", "fsdp")),
        P(("dp", "fsdp")),
        P(("dp", "fsdp")),
        P(("dp", "fsdp")),
    )
    out_specs = (
        P(None, ("dp", "fsdp"), None),
        P(None, ("dp", "fsdp"), None),
        P(("dp", "fsdp")),
        P(("dp", "fsdp")),
        P(("dp", "fsdp")),
        P(("dp", "fsdp")),
    )
    return jax.shard_map(body, mesh=mesh, in_specs=in_specs, out_specs=out_specs, check_vma=False)
```

profile of v0, /device:TPU:0, one launch (start us, length us, event | category | flops | bytes accessed | tf_op | source)
XLA Modules:
  0.0 1064.9 jit_solution(10413537687920511585)
XLA Ops:
  8.4 5.3 broadcast.732
  13.7 7.7 dynamic-update-slice
  27.8 246.4 %all-reduce.5.cloned.1.call-done = bf16[7087872]{0:T(1024)(128)(2,1)} async-done(((bf16[7087872]{0:T(1024)(128)(2,1)}), bf16[7087872]{0:T(1024)(128)(2,1)}) %all-reduce.5.cloned.1.call-update) | async-done | bytes 14175760
  277.6 6.3 reshape.1148
  295.7 8.2 fusion.174
  303.9 8.2 reshape.1151
  406.2 5.2 fusion.162
  420.0 5.5 fusion.159
  425.5 9.3 slice.205
  434.8 6.7 fusion.170
  447.4 5.2 convolution_bitcast_fusion
  452.6 6.6 fusion.167
  467.8 7.9 reshape.1156
  475.7 5.1 constant_dynamic-update-slice_fusion.22
  485.2 9.4 copy.176
  494.6 10.7 %reshape.1159 = f32[2359296]{0:T(1024)} reshape(f32[3072,768]{1,0:T(8,128)} %fusion.170) | data formatting | bytes 18874368 | tf_op jit(solution)/shard_map/reshape | solution.py:287
  507.0 9.7 constant_dynamic-update-slice_fusion.18
  525.9 7.9 reshape.1160
  533.9 5.2 constant_dynamic-update-slice_fusion.23
  543.3 9.6 copy.177
  552.9 10.7 %reshape.1163 = f32[2359296]{0:T(1024)} reshape(f32[3072,768]{1,0:T(8,128)} %fusion.167) | data formatting | bytes 18874368 | tf_op jit(solution)/shard_map/reshape | solution.py:287
  565.2 9.7 constant_dynamic-update-slice_fusion.19
  592.4 28.8 %add.255 = f32[7087872]{0:T(1024)} add(f32[7087872]{0:T(1024)} %constant_dynamic-update-slice_fusion, f32[7087872]{0:T(1024)} %constant_dynamic-update-slice_fusion.1) | non-fusion elementwise | flops 7087872 | bytes 85054464 | tf_op jit(solution)/shard_map/add | solution.py:306
  634.5 419.1 %all-reduce.7.cloned.1.call-done = f32[7087872]{0:T(1024)} async-done(((f32[7087872]{0:T(1024)}), f32[7087872]{0:T(1024)}) %all-reduce.7.cloned.1.call-update) | async-done | bytes 28351504
  (333 shorter events, 194.9 us)
Async XLA Ops:
  7.2 267.1 %all-reduce.5.cloned.1.call-start = ((), (), s32[]{:S(2)}) async-start(), calls=%async_computation | async-start | bytes 28352512
  13.7 10.9 %copy-start.1 = (f32[2,64,768]{2,1,0:T(8,128)S(1)}, f32[2,64,768]{2,1,0:T(8,128)}, u32[]{:S(2)}) copy-start(f32[2,64,768]{2,1,0:T(8,128)} %param.6) | copy-start | bytes 1179652
  13.7 13.3 %copy-start.7 = (f32[2,64,768]{2,1,0:T(8,128)S(1)}, f32[2,64,768]{2,1,0:T(8,128)}, u32[]{:S(2)}) copy-start(f32[2,64,768]{2,1,0:T(8,128)} %param.7) | copy-start | bytes 1179652
  21.4 1032.3 %all-reduce.7.cloned.1.call-start = ((), (), s32[]{:S(2)}) async-start(), calls=%async_computation.1 | async-start | bytes 56705024
  26.3 247.9 %copy-start.80 = (f32[64]{0:T(128)}, f32[64]{0:T(128)S(1)}, u32[]{:S(2)}) copy-start(f32[64]{0:T(128)S(1)} %get-tuple-element.79) | copy-start | bytes 772
  420.0 14.8 %copy-start.21 = (f32[64,3072]{1,0:T(8,128)S(1)}, f32[64,3072]{1,0:T(8,128)}, u32[]{:S(2)}) copy-start(f32[64,3072]{1,0:T(8,128)} %convolution_add_fusion.3) | copy-start | bytes 2359300
  420.0 14.8 %copy-start.41 = (bf16[64,768]{1,0:T(8,128)(2,1)S(1)}, bf16[64,768]{1,0:T(8,128)(2,1)}, u32[]{:S(2)}) copy-start(bf16[64,768]{1,0:T(8,128)(2,1)} %get-tuple-element.69) | copy-start | bytes 294916
  425.5 20.3 %slice-start = ((s8[4718592]{0:T(1024)(128)(4,1)}), s8[524288]{0:T(1024)(128)(4,1)S(1)}, s32[]{:S(2)}) async-start(s8[4718592]{0:T(1024)(128)(4,1)} %bitcast.228), calls=%async_computation.2 | async-start | bytes 1048576
  434.8 11.0 %slice-start.1 = ((s8[4718592]{0:T(1024)(128)(4,1)}), s8[4194304]{0:T(1024)(128)(4,1)S(1)}, s32[]{:S(2)}) async-start(s8[4718592]{0:T(1024)(128)(4,1)} %bitcast.228), calls=%async_computation.3 | async-start | bytes 8388608
  447.4 17.1 %copy-start.28 = (f32[64,768]{1,0:T(8,128)}, f32[64,768]{1,0:T(8,128)S(1)}, u32[]{:S(2)}) copy-start(f32[64,768]{1,0:T(8,128)S(1)} %fusion.78) | copy-start | bytes 589828
  494.6 10.7 %copy-start.58 = (f32[3,12,64]{2,1,0:T(8,128)S(1)}, f32[3,12,64]{2,1,0:T(8,128)}, u32[]{:S(2)}) copy-start(f32[3,12,64]{2,1,0:T(8,128)} %fusion.21) | copy-start | bytes 27652
  505.4 11.3 %slice-start.2 = ((s8[9437184]{0:T(1024)(128)(4,1)}), s8[4194304]{0:T(1024)(128)(4,1)S(1)}, s32[]{:S(2)}) async-start(s8[9437184]{0:T(1024)(128)(4,1)} %bitcast.230), calls=%async_computation.4 | async-start | bytes 8388608
  507.0 9.7 slice-start.3
  507.0 9.7 slice-start.4
  563.7 11.2 %slice-start.5 = ((s8[9437184]{0:T(1024)(128)(4,1)}), s8[4194304]{0:T(1024)(128)(4,1)S(1)}, s32[]{:S(2)}) async-start(s8[9437184]{0:T(1024)(128)(4,1)} %bitcast.232), calls=%async_computation.7 | async-start | bytes 8388608
  565.2 9.7 slice-start.7
  574.9 9.8 copy-start.75
  574.9 11.1 %copy-start.74 = (f32[768]{0:T(1024)S(1)}, f32[768]{0:T(1024)}, u32[]{:S(2)}) copy-start(f32[768]{0:T(1024)} %get-tuple-element.10) | copy-start | bytes 9220
  574.9 12.4 %copy-start.73 = (f32[768]{0:T(1024)S(1)}, f32[768]{0:T(1024)}, u32[]{:S(2)}) copy-start(f32[768]{0:T(1024)} %get-tuple-element.35) | copy-start | bytes 9220
  575.0 12.9 %copy-start.72 = (f32[768]{0:T(1024)S(1)}, f32[768]{0:T(1024)}, u32[]{:S(2)}) copy-start(f32[768]{0:T(1024)} %get-tuple-element.18) | copy-start | bytes 9220
  575.0 14.2 %copy-start.71 = (f32[768]{0:T(1024)S(1)}, f32[768]{0:T(1024)}, u32[]{:S(2)}) copy-start(f32[768]{0:T(1024)} %get-tuple-element.32) | copy-start | bytes 9220
  575.0 15.5 %copy-start.70 = (f32[768]{0:T(1024)S(1)}, f32[768]{0:T(1024)}, u32[]{:S(2)}) copy-start(f32[768]{0:T(1024)} %get-tuple-element.17) | copy-start | bytes 9220
  627.5 426.1 %copy-start.9 = (f32[221496]{0:T(1024)S(1)}, f32[221496]{0:T(1024)}, u32[]{:S(2)}) copy-start(f32[221496]{0:T(1024)} %param.9) | copy-start | bytes 2657956
  627.5 426.1 %copy-start.39 = (f32[221496]{0:T(1024)S(1)}, f32[221496]{0:T(1024)}, u32[]{:S(2)}) copy-start(f32[221496]{0:T(1024)} %param.10) | copy-start | bytes 2657956
  (73 other events, 400.9 us)
Sparse Core Ops, SparseCore 0:
  21.5 252.6 all-reduce.4
  621.3 432.2 all-reduce.6
where the time goes:
time: 1080 us; the launch traced here: 1060 us
  waiting for transfers between devices  666 us (62%)
  local copies, waits for them, and re-layouts  221 us (20%)
  matrix products  107 us (10%)
  other arithmetic  55.6 us (5%)
  between operations  15.6 us (1%)
    unnamed x4, waiting for transfers between devices  666 us
    unnamed x222, local copies, waits for them, and re-layouts  103 us
    reshape x6, local copies, waits for them, and re-layouts, flatten_grads(): return jnp.concatenate([part.reshape(-1) for part in grads])  42 us
    add x1, other arithmetic, body(): grad_total = flat_grads if grad_total is None else grad_total + flat_grads  28.8 us
    slice x5, local copies, waits for them, and re-layouts, unpack_flat(): pieces_out.append(flat_vec[offset:offset + length].reshape(item_shape))  27 us
    dot_general x12, matrix products, product(): return jnp.einsum(form, left, right, preferred_element_type=jnp.float32)  26 us
  transfers between devices with their start and end apart: 2, of which 2 were waited for; matrix products, arithmetic and copies ran while one was open for 2% of the time, Pallas kernels for 0%

commit v1 on v0

--- a/solution.py
+++ b/solution.py
@@ -1,3 +1,4 @@
+import functools
 import math
 
 import jax
@@ -283,39 +284,48 @@
     return (new_params, new_first, new_second)
 
 
-def flatten_grads(grads):
-    return jnp.concatenate([part.reshape(-1) for part in grads])
-
-
-def body(block_input, out_grad, seg_ids, params, first_moment, second_moment):
-    micro_count = block_input.shape[0]
-    sent_params = params.astype(jnp.bfloat16)
-    grad_total = None
-    owned_grads = None
-    outputs = []
-    input_grads = []
-    for batch_index in range(micro_count):
-        weights = unpack_flat(lax.all_gather(sent_params, ("dp", "fsdp"), axis=0, tiled=True))
-        result, kept_state = forward(
-            block_input[batch_index][None], seg_ids[batch_index][None], weights
-        )
-        back_x, grads = backward(kept_state, out_grad[batch_index][None], weights)
-        outputs.append(result[0])
-        input_grads.append(back_x[0])
-        flat_grads = flatten_grads(grads)
-        grad_total = flat_grads if grad_total is None else grad_total + flat_grads
-    owned_grads = lax.psum_scatter(grad_total, ("dp", "fsdp"), scatter_dimension=0, tiled=True)
-    new_params, new_first, new_second = adam_update(
-        params, owned_grads, first_moment, second_moment
-    )
-    return (
-        jnp.stack(outputs),
-        jnp.stack(input_grads),
-        owned_grads,
-        new_params,
-        new_first,
-        new_second,
-    )
+AXES = ("dp", "fsdp")
+MATRIX_ROWS = 9 * D + 3 * D
+TAIL = 13 * D
+
+
+def rows_from_flat(flat, spread, count):
+    me = lax.axis_index(AXES)
+    tail = flat[flat.shape[0] - TAIL :]
+    before = lax.ppermute(tail, AXES, [(i, (i + 1) % count) for i in range(count)])
+    joined = jnp.concatenate([before, flat])
+    rows = lax.dynamic_slice(joined, (TAIL - spread * me,), (flat.shape[0] - spread,))
+    return rows.reshape(-1, D), tail.reshape(-1, D)
+
+
+def flat_from_rows(rows, tail, spread, count):
+    me = lax.axis_index(AXES)
+    head = rows.reshape(-1)[:TAIL]
+    after = lax.ppermute(head, AXES, [(i, (i - 1) % count) for i in range(count)])
+    after = jnp.where(me == count - 1, tail.reshape(-1), after)
+    joined = jnp.concatenate([rows.reshape(-1), after])
+    return lax.dynamic_slice(joined, (spread * me,), (rows.size + spread,))
+
+
+def body(count, block_input, out_grad, seg_ids, params, first_moment, second_moment):
+    spread = TAIL // count
+    row_count = (params.shape[0] - spread) // D
+    rows, tail = rows_from_flat(params.astype(jnp.bfloat16), spread, count)
+    sent = jnp.concatenate([rows, jnp.pad(tail, ((0, 3), (0, 0)))])
+    whole = lax.all_gather(sent, AXES, axis=0, tiled=False)
+    matrices = whole[:, :row_count].reshape(-1)
+    weights = unpack_flat(jnp.concatenate([matrices, whole[count - 1, row_count : row_count + 13].reshape(-1)]))
+    result, kept_state = forward(block_input, seg_ids, weights)
+    back_x, grads = backward(kept_state, out_grad, weights)
+    big = jnp.concatenate([g.astype(jnp.bfloat16).reshape(-1, D) for g in grads[:4]])
+    small = jnp.concatenate([g.astype(jnp.bfloat16).reshape(-1, D) for g in grads[4:]])
+    small = jnp.pad(small, ((0, 3), (0, 0)))
+    spots = jnp.where(jnp.arange(count)[:, None, None] == count - 1, small[None], jnp.zeros((), jnp.bfloat16))
+    out = jnp.concatenate([big.reshape(count, row_count, D), spots], axis=1)
+    owned = lax.psum_scatter(out, AXES, scatter_dimension=0, tiled=False).astype(jnp.float32)
+    owned_grads = flat_from_rows(owned[:row_count], owned[row_count : row_count + 13], spread, count)
+    new_params, new_first, new_second = adam_update(params, owned_grads, first_moment, second_moment)
+    return (result, back_x, owned_grads, new_params, new_first, new_second)
 
 
 def solution(mesh):
@@ -335,4 +345,5 @@
         P(("dp", "fsdp")),
         P(("dp", "fsdp")),
     )
-    return jax.shard_map(body, mesh=mesh, in_specs=in_specs, out_specs=out_specs, check_vma=False)
+    count = mesh.shape["dp"] * mesh.shape["fsdp"]
+    return jax.shard_map(functools.partial(body, count), mesh=mesh, in_specs=in_specs, out_specs=out_specs, check_vma=False)

time: 1080 us -> 512 us (0.47)
  waiting for transfers between devices: 666 us -> 265 us
  local copies, waits for them, and re-layouts: 221 us -> 103 us
  matrix products: 107 us -> 58.2 us
    unnamed x4 -> x2, waiting for transfers between devices: 666 us -> 0.03 us
    reduce_scatter x0 -> x1, waiting for transfers between devices: none -> 159 us  [body(): lax.psum_scatter(out, AXES, scatter_dimension=0, tiled=False)]
    all_gather x0 -> x1, waiting for transfers between devices: none -> 98.4 us  [body(): whole = lax.all_gather(sent, AXES, axis=0, tiled=False)]
    unnamed x222 -> x116, local copies, waits for them, and re-layouts: 103 us -> 7.86 us
    concatenate x2 -> x4, other arithmetic: 2.35 us -> 35 us  [the longest x1 27.5 us: body(): jnp.concatenate([g.astype(jnp.bfloat16).reshape(-1, D) for g in grads[:4]])]
    add x1, other arithmetic: 28.8 us -> 1.01 us  [backward(): grad_y + back_one + back_two]
    reshape x6 -> x8, local copies, waits for them, and re-layouts: 42 us -> 17.6 us  [the longest x2 13.5 us: body(): g.astype(jnp.bfloat16).reshape(-1, D)]
    slice x0 -> x7, local copies, waits for them, and re-layouts: none -> 15.7 us  [the longest x1 10.7 us: body(): matrices = whole[:, :row_count].reshape(-1)]
  transfers between devices with their start and end apart: 2 -> 4, of which waited for: 2 -> 4; matrix products, arithmetic and copies ran while one was open for 2% -> 3% of each run, Pallas kernels for 0% -> 0%
where the time goes in v1:
time: 512 us; the launch traced here: 502 us
  waiting for transfers between devices  265 us (52%)
  local copies, waits for them, and re-layouts  103 us (20%)
  other arithmetic  58.5 us (11%)
  matrix products  58.2 us (11%)
  between operations  15.1 us (3%)
    reduce_scatter x1, waiting for transfers between devices, body(): lax.psum_scatter(out, AXES, scatter_dimension=0, tiled=False)  159 us
    all_gather x1, waiting for transfers between devices, body(): whole = lax.all_gather(sent, AXES, axis=0, tiled=False)  98.4 us
    concatenate x1, other arithmetic, body(): jnp.concatenate([g.astype(jnp.bfloat16).reshape(-1, D) for g in grads[:4]])  27.5 us
    slice x2, local copies, waits for them, and re-layouts, unpack_flat(): pieces_out.append(flat_vec[offset:offset + length].reshape(item_shape))  26.6 us
    dot_general x6, matrix products, product(): return jnp.einsum(form, left, right, preferred_element_type=jnp.float32)  14.1 us
    reshape x2, local copies, waits for them, and re-layouts, body(): g.astype(jnp.bfloat16).reshape(-1, D)  13.5 us
    slice x1, local copies, waits for them, and re-layouts, body(): matrices = whole[:, :row_count].reshape(-1)  10.7 us
  transfers between devices with their start and end apart: 4, of which 4 were waited for; matrix products, arithmetic and copies ran while one was open for 3% of the time, Pallas kernels for 0%

profile of v1, /device:TPU:0, one launch (start us, length us, event | category | flops | bytes accessed | tf_op | source)
XLA Modules:
  0.0 502.4 jit_solution(11054215431606291464)
XLA Ops:
  9.1 7.3 %collective-permute-done = bf16[9984]{0:T(1024)(128)(2,1)S(1)} collective-permute-done((bf16[9984]{0:T(1024)(128)(2,1)S(1)}, bf16[9984]{0:T(1024)(128)(2,1)S(1)}, u32[]{:S(2)}, u32[]{:S(2)}) %collective-permute-start) | collective-permute-done | bytes 20000 | tf_op jit(solution)/shard_map/ppermute | solution.py:295
  23.8 98.4 %all-gather.3.cloned.1.call-done = bf16[9728,768]{1,0:T(8,128)(2,1)} async-done(((bf16[304,768]{1,0:T(8,128)(2,1)}), bf16[9728,768]{1,0:T(8,128)(2,1)}) %all-gather.3.cloned.1.call-update) | async-done | bytes 14942224 | tf_op jit(solution)/shard_map/all_gather | solution.py:315
  125.8 4.0 slice.170
  129.7 10.7 %slice.181 = bf16[32,288,768]{2,1,0:T(8,128)(2,1)} slice(bf16[32,304,768]{2,1,0:T(8,128)(2,1)} %bitcast.70), slice={[0:32], [0:288], [0:768]} | slice | bytes 28311552 | tf_op jit(solution)/shard_map/slice | solution.py:316
  141.0 5.1 %reshape.388 = bf16[768,2304]{1,0:T(8,128)(2,1)S(1)} reshape(bf16[8,288,768]{2,1,0:T(8,128)(2,1)} %slice.170) | data formatting | bytes 7077888 | tf_op jit(solution)/shard_map/reshape | solution.py:47
  153.0 3.6 reshape.389
  180.0 4.0 convolution_bitcast_fusion.2
  184.0 4.0 convolution_bitcast_fusion.1
  196.0 3.7 copy.41
  199.7 3.4 convert_element_type.287
  203.1 3.2 fusion.90
  209.2 22.7 %slice.152 = bf16[2304,3072]{1,0:T(8,128)(2,1)} reshape(bf16[32,288,768]{2,1,0:T(8,128)(2,1)} %slice.181) | data formatting | bytes 28311552 | tf_op jit(solution)/shard_map/slice | solution.py:47
  234.4 5.1 %reshape.395 = bf16[2304,768]{1,0:T(8,128)(2,1)S(1)} reshape(bf16[768,2304]{1,0:T(8,128)(2,1)} %convolution_convert_fusion.2) | data formatting | bytes 7077888 | tf_op jit(solution)/shard_map/reshape | solution.py:320
  239.5 7.4 %fusion.19 = (bf16[128,3072]{1,0:T(8,128)(2,1)}, f32[128,3072]{1,0:T(8,128)S(1)}) fusion(f32[3072]{0:T(1024)} %reshape.406, bf16[2304,3072]{1,0:T(8,128)(2,1)} %slice.152, f32[128,768]{1,0:T(8,128)} %fusion.54, f32[768]{0:T(1024)S(1)} %copy-done.38, f32[768]{0:T(1024)S(1)} %copy-done.36), kind=kOutput, calls=%fused_computation.24 | convolution fusion | flops 630226944 | bytes 7489536 | tf_op jit(solution)/shard_map/dot_general | solution.py:162
  247.0 4.7 fusion.89
  251.7 3.6 convolution_convert_fusion.1
  255.2 5.5 %multiply_reduce_fusion.1 = (bf16[768]{0:T(1024)(128)(2,1)}, f32[128]{0:T(128)}, f32[128]{0:T(128)}, bf16[768]{0:T(1024)(128)(2,1)}, f32[128]{0:T(128)}, /*index...) fusion(f32[128,768]{1,0:T(8,128)S(1)} %copy-done.13, ...), kind=kOutput, calls=%fused_computation.101 | convolution fusion | flops 605352448 | bytes 6699008 | tf_op jit(solution)/shard_map/dot_general | solution.py:238
  265.7 8.5 %reshape.396 = bf16[3072,768]{1,0:T(8,128)(2,1)} reshape(bf16[768,3072]{1,0:T(8,128)(2,1)} %convolution_convert_fusion.1) | data formatting | bytes 9437184 | tf_op jit(solution)/shard_map/reshape | solution.py:320
  274.1 4.8 convolution_convert_fusion
  284.7 27.5 %pad_maximum_fusion.1 = bf16[9216,768]{1,0:T(8,128)(2,1)S(1)} fusion(bf16[3072,768]{1,0:T(8,128)(2,1)} %convolution_convert_fusion, bf16[3072,768]{1,0:T(8,128)(2,1)} %reshape.396, bf16[768,768]{1,0:T(8,128)(2,1)} %convolution_convert_fusion.3, bf16[2304,768]{1,0:T(8,128)(2,1)S(1)} %reshape.395), kind=kLoop, calls=%fused_computation.2 | loop fusion | flops 56623104 | bytes 28311552 | tf_op jit(solution)/shard_map/concatenate | solution.py:320
  312.2 6.3 %pad_maximum_fusion = bf16[32,304,768]{2,1,0:T(8,128)(2,1)} fusion(bf16[32,16,768]{2,1,0:T(8,128)(2,1)S(1)} %broadcast_select_fusion, bf16[32,288,768]{2,1,0:T(8,128)(2,1)S(1)} %bitcast.65), kind=kLoop, calls=%fused_computation.1 | loop fusion | flops 29884416 | bytes 29884416 | tf_op jit(solution)/shard_map/concatenate | solution.py:324
  319.6 3.2 fusion.39
  325.5 159.4 %reduce-scatter.2.cloned.1.call-done = bf16[1,304,768]{2,1,0:T(8,128)(2,1)} async-done(((bf16[32,304,768]{2,1,0:T(8,128)(2,1)}), bf16[1,304,768]{2,1,0:T(8,128)(2,1)}) %reduce-scatter.2.cloned.1.call-update) | async-done | bytes 466960 | tf_op jit(solution)/shard_map/reduce_scatter | solution.py:325
  491.0 4.1 multiply_subtract_fusion
  (202 shorter events, 77.2 us)
Async XLA Ops:
  7.2 115.0 %all-gather.3.cloned.1.call-start = ((), (), s32[]{:S(2)}) async-start(), calls=%async_computation.2 | async-start | bytes 15409152 | tf_op jit(solution)/shard_map/all_gather | solution.py:315
  8.5 7.9 %collective-permute-start = (bf16[9984]{0:T(1024)(128)(2,1)S(1)}, bf16[9984]{0:T(1024)(128)(2,1)S(1)}, u32[]{:S(2)}, u32[]{:S(2)}) collective-permute-start(bf16[9984]{0:T(1024)(128)(2,1)S(1)} %slice.167), channel_id=1, source_target_pairs={{0,1},{1,2},{2,3},{3,4},{4,5},{5,6},{6,7},{7,8},{8,9},{9,10},{10,1... | collective-permute-start | bytes 59912 | tf_op jit(solution)/shard_map/ppermute | solution.py:295
  9.1 9.1 %copy-start = (f32[2,64,768]{2,1,0:T(8,128)S(1)}, f32[2,64,768]{2,1,0:T(8,128)}, u32[]{:S(2)}) copy-start(f32[2,64,768]{2,1,0:T(8,128)} %param.6) | copy-start | bytes 1179652
  18.1 466.8 %reduce-scatter.2.cloned.1.call-start = ((), (), s32[]{:S(2)}) async-start(), calls=%async_computation.1 | async-start | bytes 15409152 | tf_op jit(solution)/shard_map/reduce_scatter | solution.py:325
  18.3 111.4 %copy-start.47 = (f32[128]{0:T(128)}, f32[128]{0:T(128)S(1)}, u32[]{:S(2)}) copy-start(f32[128]{0:T(128)S(1)} %div.43) | copy-start | bytes 1540
  18.6 111.1 %copy-start.49 = (f32[128]{0:T(128)}, f32[128]{0:T(128)S(1)}, u32[]{:S(2)}) copy-start(f32[128]{0:T(128)S(1)} %rsqrt.14) | copy-start | bytes 1540
  18.7 111.0 %copy-start.51 = (f32[128]{0:T(128)}, f32[128]{0:T(128)S(1)}, u32[]{:S(2)}) copy-start(f32[128]{0:T(128)S(1)} %mul.351) | copy-start | bytes 1540
  188.1 3.8 copy-start.6
  209.2 22.7 %copy-start.39 = (f32[1,4,768]{2,1,0:T(4,128)S(1)}, f32[1,4,768]{2,1,0:T(4,128)}, u32[]{:S(2)}) copy-start(f32[1,4,768]{2,1,0:T(4,128)} %slice_convert_fusion.2) | copy-start | bytes 36868
  209.2 23.3 %copy-start.28 = (bf16[2,64,12,64]{1,3,2,0:T(8,128)(2,1)S(1)}, bf16[2,64,12,64]{1,3,2,0:T(8,128)(2,1)}, u32[]{:S(2)}) copy-start(bf16[2,64,12,64]{1,3,2,0:T(8,128)(2,1)} %fusion.36) | copy-start | bytes 589828
  234.4 5.1 %copy-start.36 = (f32[768]{0:T(1024)S(1)}, f32[768]{0:T(1024)}, u32[]{:S(2)}) copy-start(f32[768]{0:T(1024)} %get-tuple-element.9) | copy-start | bytes 9220
  234.4 5.1 %copy-start.38 = (f32[768]{0:T(1024)S(1)}, f32[768]{0:T(1024)}, u32[]{:S(2)}) copy-start(f32[768]{0:T(1024)} %get-tuple-element.8) | copy-start | bytes 9220
  239.5 7.4 %copy-start.32 = (bf16[128,768]{1,0:T(8,128)(2,1)S(1)}, bf16[128,768]{1,0:T(8,128)(2,1)}, u32[]{:S(2)}) copy-start(bf16[128,768]{1,0:T(8,128)(2,1)} %fusion.59) | copy-start | bytes 589828
  247.0 4.7 copy-start.13
  274.1 4.8 copy-start.18
  274.1 4.8 copy-start.30
  322.8 165.1 %copy-start.10 = (f32[2,64,768]{2,1,0:T(8,128)S(1)}, f32[2,64,768]{2,1,0:T(8,128)}, u32[]{:S(2)}) copy-start(f32[2,64,768]{2,1,0:T(8,128)} %param.7) | copy-start | bytes 1179652
  322.8 165.1 %copy-start.25 = (f32[128,768]{1,0:T(8,128)S(1)}, f32[128,768]{1,0:T(8,128)}, u32[]{:S(2)}) copy-start(f32[128,768]{1,0:T(8,128)} %fusion.90) | copy-start | bytes 1179652
  322.8 165.1 %copy-start.35 = (f32[128,768]{1,0:T(8,128)S(1)}, f32[128,768]{1,0:T(8,128)}, u32[]{:S(2)}) copy-start(f32[128,768]{1,0:T(8,128)} %get-tuple-element.53) | copy-start | bytes 1179652
  322.8 165.0 %copy-start.48 = (f32[128]{0:T(128)S(1)}, f32[128]{0:T(128)}, u32[]{:S(2)}) copy-start(f32[128]{0:T(128)} %copy-done.47) | copy-start | bytes 1540
  322.8 165.0 %copy-start.50 = (f32[128]{0:T(128)S(1)}, f32[128]{0:T(128)}, u32[]{:S(2)}) copy-start(f32[128]{0:T(128)} %copy-done.49) | copy-start | bytes 1540
  322.9 165.0 %copy-start.52 = (f32[128]{0:T(128)S(1)}, f32[128]{0:T(128)}, u32[]{:S(2)}) copy-start(f32[128]{0:T(128)} %copy-done.51) | copy-start | bytes 1540
  484.9 4.7 copy-start.15
  486.3 3.5 collective-permute-start.1
  (37 other events, 67.6 us)
Sparse Core Ops, SparseCore 0:
  18.2 103.9 all-gather.2
  318.6 166.2 reduce-scatter.1

commit v2 on v1

--- a/solution.py
+++ b/solution.py
@@ -4,6 +4,8 @@
 import jax
 import jax.numpy as jnp
 from jax import lax
+from jax.experimental import pallas as pl
+from jax.experimental.pallas import tpu as pltpu
 from jax.sharding import PartitionSpec as P
 
 D = 768
@@ -328,22 +330,641 @@
     return (result, back_x, owned_grads, new_params, new_first, new_second)
 
 
+BF = jnp.bfloat16
+F32 = jnp.float32
+PLANES = 4
+PART = D // PLANES
+SPOT = 96
+SLAB = 352
+STARTS = (0, 80, 176, 256)
+
+
+def dot_nn(a, b):
+    return lax.dot_general(a, b, (((1,), (0,)), ((), ())), preferred_element_type=F32)
+
+
+def dot_nt(a, b):
+    return lax.dot_general(a, b, (((1,), (1,)), ((), ())), preferred_element_type=F32)
+
+
+def dot_tn(a, b):
+    return lax.dot_general(a, b, (((0,), (0,)), ((), ())), preferred_element_type=F32)
+
+
+def lanes_of(width):
+    return lax.broadcasted_iota(jnp.int32, (1, width), 1)
+
+
+def group_mask(index, width=D, size=PART):
+    lane = lanes_of(width)
+    return (lane >= index * size) & (lane < (index + 1) * size)
+
+
+def turned(value, shift):
+    shift = shift % value.shape[-1]
+    return value if shift == 0 else pltpu.roll(value, shift, value.ndim - 1)
+
+
+def spread_groups(parts, first):
+    total = None
+    for group, part in enumerate(parts):
+        moved = jnp.where(group_mask(group), turned(part, PART * (group - first)), 0.0)
+        total = moved if total is None else total + moved
+    return total
+
+
+def every(size, stride, first):
+    row = lax.broadcasted_iota(jnp.int32, (size, SPOT), 0)
+    col = lax.broadcasted_iota(jnp.int32, (size, SPOT), 1)
+    return jnp.where(col == stride * row + first, 1.0, 0.0).astype(BF)
+
+
+def permutations():
+    place = jnp.arange(D)
+    part, inner = place // PART, place % PART
+    hidden_from = SPOT * (inner // 24) + 24 * part + inner % 24
+    kind = inner // HEAD_DIM
+    head = jnp.where(
+        part < 3,
+        part + jnp.where(kind == 0, 0, jnp.where(kind == 1, 5, 9)),
+        jnp.where(kind == 0, 3, jnp.where(kind == 1, 4, 8)),
+    )
+    head_from = HEAD_DIM * head + inner % HEAD_DIM
+    rows = place[:, None]
+    return (
+        (rows == head_from[None]).astype(BF),
+        (rows == hidden_from[None]).astype(BF),
+    )
+
+
+def pack_kernel(where_ref, rows_ref, tail_ref, heads_ref, hidden_ref, *outs):
+    out_refs, spot = outs[:PLANES], outs[PLANES]
+    plane, place = where_ref[0], where_ref[1]
+    device = 8 * plane + place
+    spot[...] = jnp.zeros_like(spot)
+    for i in range(3):
+        block = 3 * device + i
+
+        @pl.when(block < 24)
+        def _():
+            for j in range(3):
+                picked = dot_nn(every(32, 3, j), rows_ref[SPOT * i : SPOT * i + SPOT, :].astype(BF))
+                sorted_ = dot_nn(picked.astype(BF), heads_ref[...])
+                parts = [sorted_[8 * g : 8 * g + 8] for g in range(4)]
+                for s in range(PLANES):
+                    spot[s, 24 * i + 8 * j : 24 * i + 8 * j + 8, :] = spread_groups(parts, s)
+
+        @pl.when((block >= 32) & (block < 64))
+        def _():
+            source = rows_ref[SPOT * i : SPOT * i + SPOT, :].astype(BF)
+            parts = [
+                dot_nn(dot_nn(every(24, 4, j), source).astype(BF), hidden_ref[...])
+                for j in range(4)
+            ]
+            for s in range(PLANES):
+                value = spread_groups(parts, s)
+                if i < 2:
+                    spot[s, 24 * i : 24 * i + 24, :] = value
+                else:
+                    mixed = block == 32
+
+                    @pl.when(mixed)
+                    def _():
+                        spot[s, 0:24, :] = value
+
+                    @pl.when(jnp.logical_not(mixed))
+                    def _():
+                        spot[s, 48:72, :] = value
+
+        @pl.when(block >= 64)
+        def _():
+            for s in range(PLANES):
+                spot[s, 24 * i : 24 * i + 24, :] = rows_ref[
+                    SPOT * i + 24 * s : SPOT * i + 24 * s + 24, :
+                ]
+
+    @pl.when(device == 8)
+    def _():
+        for s in range(3):
+            spot[s, 0:64, :] = rows_ref[64 * s : 64 * s + 64, :]
+        spot[3, 0:96, :] = rows_ref[192:288, :]
+
+    @pl.when(device == 9)
+    def _():
+        for s in range(3):
+            spot[s, 0:64, :] = rows_ref[32 + 64 * s : 96 + 64 * s, :]
+        spot[3, 0:32, :] = rows_ref[0:32, :]
+        spot[3, 32:96, :] = rows_ref[224:288, :]
+
+    @pl.when(device == 10)
+    def _():
+        for s in range(3):
+            spot[s, 24:88, :] = rows_ref[64 * s : 64 * s + 64, :]
+
+    @pl.when(device == 31)
+    def _():
+        upper = tail_ref[0:8, :].astype(BF)
+        by_head = dot_nn(upper, heads_ref[...])
+        by_hidden = dot_nn(upper, hidden_ref[...])
+        for s in range(PLANES):
+            spot[s, 72:73, :] = spread_groups([by_hidden[4 + j : 5 + j] for j in range(4)], s)
+            spot[s, 73:74, :] = spread_groups([by_head[j : j + 1] for j in range(3)], s)
+            spot[s, 74:75, :] = tail_ref[3:4, :]
+            spot[s, 80:88, :] = tail_ref[8:16, :]
+
+    for r in range(PLANES):
+        out_refs[r][...] = spot[plane ^ r].astype(BF)
+
+
+def unpack_kernel(where_ref, *refs):
+    in_refs, (heads_ref, hidden_ref, rows_ref, tail_ref, spot) = refs[:PLANES], refs[PLANES:]
+    plane, place = where_ref[0], where_ref[1]
+    device = 8 * plane + place
+    for r in range(PLANES):
+        spot[plane ^ r] = in_refs[r][...].astype(F32)
+    for i in range(3):
+        block = 3 * device + i
+
+        @pl.when(block < 24)
+        def _():
+            total = None
+            for j in range(3):
+                base = 24 * i + 8 * j
+                parts = [spot[s, base : base + 8, :] for s in range(PLANES)]
+                sorted_ = jnp.concatenate([spread_groups(parts, g) for g in range(4)], axis=0)
+                picked = dot_nt(sorted_.astype(BF), heads_ref[...]).astype(BF)
+                value = dot_tn(every(32, 3, j), picked)
+                total = value if total is None else total + value
+            rows_ref[SPOT * i : SPOT * i + SPOT, :] = total
+
+        @pl.when((block >= 32) & (block < 64))
+        def _():
+            start = 24 * i
+            if i == 2:
+                start = pl.multiple_of(jnp.where(block == 32, 0, 48), 8)
+            parts = [spot[s, pl.ds(start, 24), :] for s in range(PLANES)]
+            total = None
+            for j in range(4):
+                picked = dot_nt(spread_groups(parts, j).astype(BF), hidden_ref[...]).astype(BF)
+                value = dot_tn(every(24, 4, j), picked)
+                total = value if total is None else total + value
+            rows_ref[SPOT * i : SPOT * i + SPOT, :] = total
+
+        @pl.when(block >= 64)
+        def _():
+            for s in range(PLANES):
+                rows_ref[SPOT * i + 24 * s : SPOT * i + 24 * s + 24, :] = spot[
+                    s, 24 * i : 24 * i + 24, :
+                ]
+
+    @pl.when(device == 8)
+    def _():
+        for s in range(3):
+            rows_ref[64 * s : 64 * s + 64, :] = spot[s, 0:64, :]
+        rows_ref[192:288, :] = spot[3, 0:96, :]
+
+    @pl.when(device == 9)
+    def _():
+        for s in range(3):
+            rows_ref[32 + 64 * s : 96 + 64 * s, :] = spot[s, 0:64, :]
+        rows_ref[0:32, :] = spot[3, 0:32, :]
+        rows_ref[224:288, :] = spot[3, 32:96, :]
+
+    @pl.when(device == 10)
+    def _():
+        for s in range(3):
+            rows_ref[64 * s : 64 * s + 64, :] = spot[s, 24:88, :]
+
+    tail_ref[...] = jnp.zeros_like(tail_ref)
+
+    @pl.when(device == 31)
+    def _():
+        whole = [spot[s, 72:73, :] for s in range(PLANES)]
+        for j in range(4):
+            row = jnp.broadcast_to(spread_groups(whole, j), (8, D)).astype(BF)
+            tail_ref[4 + j : 5 + j, :] = dot_nt(row, hidden_ref[...])[0:1]
+        whole = [spot[s, 73:74, :] for s in range(PLANES)]
+        for j in range(3):
+            row = jnp.broadcast_to(spread_groups(whole, j), (8, D)).astype(BF)
+            tail_ref[j : j + 1, :] = dot_nt(row, heads_ref[...])[0:1]
+        tail_ref[3:4, :] = sum(spot[s, 74:75, :] for s in range(PLANES))
+        tail_ref[8:16, :] = sum(spot[s, 80:88, :] for s in range(PLANES))
+
+
+def slab_start(plane):
+    start = jnp.where(plane == 1, STARTS[1], jnp.where(plane == 2, STARTS[2], STARTS[3]))
+    return pl.multiple_of(jnp.where(plane == 0, 0, start), 16)
+
+
+def slab_kernel(where_ref, a_ref, b_ref, c_ref, d_ref, out_ref):
+    for r, ref in enumerate((a_ref, b_ref, c_ref, d_ref)):
+        source = where_ref[0] ^ r
+        out_ref[pl.ds(slab_start(source), 80), :] = ref[0:80, :]
+
+        @pl.when((source == 1) | (source == 3))
+        def _():
+            out_ref[pl.ds(slab_start(source) + 80, 16), :] = ref[80:96, :]
+
+
+def split_kernel(where_ref, a_ref, b_ref, c_ref, d_ref, *outs):
+    out_refs, total = outs[:PLANES], outs[PLANES]
+    total[...] = (a_ref[...].astype(F32) + b_ref[...].astype(F32)) + (
+        c_ref[...].astype(F32) + d_ref[...].astype(F32)
+    )
+    for r in range(PLANES):
+        out_refs[r][...] = total[pl.ds(slab_start(where_ref[0] ^ r), SPOT), :].astype(BF)
+
+
+def layer_kernel(where_ref, *refs):
+    act_refs, slab_refs = refs[:4], refs[4:12]
+    grad_refs, back_refs = refs[12:20], refs[20:24]
+    (w_up, w_down, w_out, packed, w_qkv, tails, bf_up, bf_down, bf_out, bf_qkv, normed, grad_y,
+     qkv, attn, g_qkv, g_attn, up, slab) = refs[24:]
+    plane, spot, core = where_ref[0], where_ref[1], where_ref[2]
+    lane = lanes_of(D)
+
+    def place_of(index):
+        return 2 * (spot ^ (index % 4)) + (core if index < 4 else 1 - core)
+
+    w_out[...] = jnp.zeros_like(w_out)
+    for index, ref in enumerate(slab_refs):
+        q = place_of(index)
+        for i in range(3):
+            for j in range(3):
+                packed[j, pl.ds(pl.multiple_of(24 * q + 8 * i, 8), 8), :] = ref[0:80, :][
+                    24 * i + 8 * j : 24 * i + 8 * j + 8
+                ].astype(F32)
+        one = ref[80:176, :].astype(F32)
+        two = ref[176:256, :].astype(F32)
+        three = ref[256:352, :].astype(F32)
+
+        @pl.when(q >= 3)
+        def _():
+            w_up[pl.ds(pl.multiple_of(72 * q - 192, 8), 72), :] = one[0:72]
+
+        @pl.when(q == 2)
+        def _():
+            w_up[0:24, :] = one[0:24]
+
+            @pl.when(plane < 3)
+            def _():
+                w_out[128:192, :] = one[24:88]
+
+        @pl.when((q < 2) & (plane < 3))
+        def _():
+            w_out[pl.ds(pl.multiple_of(64 * q, 8), 64), :] = one[0:64]
+
+        @pl.when((q < 2) & (plane == 3))
+        def _():
+            w_out[pl.ds(pl.multiple_of(96 * q, 8), 96), :] = one[0:96]
+
+        @pl.when(q < 5)
+        def _():
+            w_up[pl.ds(pl.multiple_of(384 + 72 * q, 8), 72), :] = two[0:72]
+
+        @pl.when(q == 5)
+        def _():
+            w_up[744:768, :] = two[0:24]
+            w_down[0:48, :] = two[24:72]
+
+        @pl.when(q > 5)
+        def _():
+            w_down[pl.ds(pl.multiple_of(72 * q - 384, 8), 72), :] = two[0:72]
+
+        w_down[pl.ds(pl.multiple_of(192 + 72 * q, 8), 72), :] = three[0:72]
+
+        @pl.when(q == 7)
+        def _():
+            tails[...] = three[72:88]
+
+    for j in range(3):
+        for i in range(4):
+            moved = turned(packed[j], -PART * i)[:, 0:256]
+            moved = jnp.where(lanes_of(256) < PART, moved, 0.0)
+            w_qkv[:, i, :, 256 * j : 256 * j + 256] = moved.reshape(24, 8, 256)
+    bf_up[...] = w_up[...].astype(BF)
+    bf_down[...] = w_down[...].astype(BF)
+    bf_out[...] = w_out[...].astype(BF)
+    bf_qkv[...] = w_qkv[...].reshape(D, D).astype(BF)
+
+    for r in range(4):
+        normed[128 * r : 128 * r + 128, :] = act_refs[r][0:128, :]
+        grad_y[128 * r : 128 * r + 128, :] = act_refs[r][128:256, :]
+    bias_up = tails[0:1, :]
+    flat_bias = tails[1:2, :]
+    bias_qkv = jnp.zeros((1, D), F32)
+    for j in range(3):
+        keep = (lane >= 256 * j) & (lane < 256 * j + PART)
+        bias_qkv = jnp.where(keep, turned(flat_bias, 64 * j), bias_qkv)
+    bias_y = jnp.where(plane == 0, tails[2:3, :] + tails[8:9, :], 0.0)
+    gain_one, shift_one = tails[9:10, :], tails[10:11, :]
+    gain_two, shift_two = tails[11:12, :], tails[12:13, :]
+
+    def act_of(gain, shift):
+        return (normed[...].astype(F32) * gain + shift).astype(BF)
+
+    act_one = act_of(gain_one, shift_one)
+    qkv[...] = dot_nn(act_one, bf_qkv[...]) + bias_qkv
+    g_attn[...] = dot_nt(grad_y[...], bf_out[...]).astype(BF)
+
+    rows = lax.broadcasted_iota(jnp.int32, (128, 128), 0)
+    cols = lax.broadcasted_iota(jnp.int32, (128, 128), 1)
+    same_block = (rows < 64) == (cols < 64)
+    eye = rows == cols
+    in_head = lanes_of(128) % 64
+    freq = jnp.exp((in_head % 8).astype(F32) * (-2.0 * math.log(10000.0) / ROT))
+    low_half = lanes_of(128) < 64
+    for r in range(4):
+        span = slice(128 * r, 128 * r + 128)
+        seg_row = jnp.broadcast_to(act_refs[r][256:272, 0:128].astype(F32)[0:1], (128, 128))
+        seg_col = jnp.sum(jnp.where(eye, seg_row, 0.0), axis=1, keepdims=True)
+        same = (seg_col == seg_row) & same_block
+        allowed = same & (cols <= rows) & ((seg_col >= 0.0) | eye)
+        position = jnp.sum(jnp.where(same & (cols < rows), 1.0, 0.0), axis=1, keepdims=True)
+        angle = position * freq
+        cos_t = jnp.where(in_head < ROT, jnp.cos(angle), 1.0)
+        sine = jnp.sin(angle)
+        sin_a = jnp.where(in_head < 8, sine, 0.0)
+        sin_b = jnp.where((in_head >= 8) & (in_head < ROT), sine, 0.0)
+
+        def rotated(x):
+            return x * cos_t - turned(x, -8) * sin_a + turned(x, 8) * sin_b
+
+        def unrotated(x):
+            return x * cos_t + turned(x, -8) * sin_a - turned(x, 8) * sin_b
+
+        for tile in range(2):
+            at = [256 * j + 128 * tile for j in range(3)]
+            query = rotated(qkv[span, at[0] : at[0] + 128]).astype(BF)
+            key = rotated(qkv[span, at[1] : at[1] + 128]).astype(BF)
+            value = qkv[span, at[2] : at[2] + 128].astype(BF)
+            g_out = g_attn[span, 128 * tile : 128 * tile + 128]
+            parts = []
+            for half in range(2 - tile):
+                mask = low_half if half == 0 else jnp.logical_not(low_half)
+                key_h = jnp.where(mask, key, jnp.zeros_like(key))
+                value_h = jnp.where(mask, value, jnp.zeros_like(value))
+                scores = dot_nt(query, key_h) * HEAD_DIM ** (-0.5)
+                masked = jnp.where(allowed, scores, -1e30)
+                top = jnp.max(masked, axis=1, keepdims=True)
+                expo = jnp.where(allowed, jnp.exp(masked - top), 0.0)
+                prob = expo * (1.0 / jnp.sum(expo, axis=1, keepdims=True))
+                prob_bf = prob.astype(BF)
+                g_prob = dot_nt(g_out, value_h)
+                delta = jnp.sum(prob * g_prob, axis=1, keepdims=True)
+                g_score = (prob * (g_prob - delta) * HEAD_DIM ** (-0.5)).astype(BF)
+                parts.append(
+                    (
+                        dot_nn(prob_bf, value),
+                        dot_tn(prob_bf, g_out),
+                        dot_nn(g_score, key),
+                        dot_tn(g_score, query),
+                    )
+                )
+            if tile == 0:
+                o, gv, gq, gk = [jnp.where(low_half, a, b) for a, b in zip(*parts)]
+            else:
+                o, gv, gq, gk = [jnp.where(low_half, a, 0.0) for a in parts[0]]
+            attn[span, 128 * tile : 128 * tile + 128] = o.astype(BF)
+            g_qkv[span, at[0] : at[0] + 128] = unrotated(gq)
+            g_qkv[span, at[1] : at[1] + 128] = unrotated(gk)
+            g_qkv[span, at[2] : at[2] + 128] = gv
+    y = dot_nn(attn[...], bf_out[...]) + bias_y
+    grad_out = dot_tn(attn[...], grad_y[...])
+    g_bias_qkv = jnp.sum(g_qkv[...], axis=0, keepdims=True)
+    g_qkv_bf = g_qkv[...].astype(BF)
+    w_qkv[...] = dot_tn(act_one, g_qkv_bf).reshape(24, 4, 8, D)
+    g_act_one = dot_nt(g_qkv_bf, bf_qkv[...])
+    w_out[...] = grad_out
+
+    act_two = act_of(gain_two, shift_two)
+    up[...] = dot_nn(act_two, bf_up[...]) + bias_up
+    cdf = 0.5 * (1.0 + lax.erf(up[...] * 0.7071067811865476))
+    hidden = (up[...] * cdf).astype(BF)
+    y = y + dot_nn(hidden, bf_down[...])
+    for r in range(4):
+        back_refs[r][0:128, :] = y[128 * r : 128 * r + 128].astype(BF)
+    w_down[...] = dot_tn(hidden, grad_y[...])
+    pdf = jnp.exp(-0.5 * up[...] * up[...]) * 0.3989422804014327
+    g_up = dot_nt(grad_y[...], bf_down[...]) * (cdf + up[...] * pdf)
+    g_bias_up = jnp.sum(g_up, axis=0, keepdims=True)
+    g_up_bf = g_up.astype(BF)
+    w_up[...] = dot_tn(act_two, g_up_bf)
+    g_act_two = dot_nt(g_up_bf, bf_up[...])
+    wide = normed[...].astype(F32)
+    for r in range(4):
+        span = slice(128 * r, 128 * r + 128)
+        back_refs[r][128:256, :] = (g_act_one[span] * gain_one + g_act_two[span] * gain_two).astype(BF)
+
+    def row_sum(x):
+        return jnp.sum(x, axis=0, keepdims=True)
+
+    g_bias_y = row_sum(grad_y[0:128, :].astype(F32))
+    flat_bias = jnp.zeros((1, D), F32)
+    for j in range(3):
+        keep = (lane >= PART * j) & (lane < PART * (j + 1))
+        flat_bias = jnp.where(keep, turned(g_bias_qkv, -64 * j), flat_bias)
+    tails[...] = jnp.zeros_like(tails)
+    tails[0:1, :] = g_bias_up
+    tails[1:2, :] = flat_bias
+    tails[2:3, :] = g_bias_y
+    tails[8:9, :] = g_bias_y
+    tails[9:10, :] = row_sum(g_act_one * wide)
+    tails[10:11, :] = row_sum(g_act_one)
+    tails[11:12, :] = row_sum(g_act_two * wide)
+    tails[12:13, :] = row_sum(g_act_two)
+
+    for j in range(3):
+        total = None
+        for i in range(4):
+            piece = w_qkv[:, i, :, 256 * j : 256 * j + 256].reshape(PART, 256)
+            piece = jnp.where(lanes_of(256) < PART, piece, 0.0)
+            piece = jnp.concatenate([piece, jnp.zeros((PART, 512), F32)], axis=1)
+            piece = turned(piece, PART * i)
+            total = piece if total is None else total + piece
+        packed[j] = total
+    for index, ref in enumerate(grad_refs):
+        q = place_of(index)
+        for i in range(3):
+            for j in range(3):
+                slab[24 * i + 8 * j : 24 * i + 8 * j + 8, :] = packed[
+                    j, pl.ds(pl.multiple_of(24 * q + 8 * i, 8), 8), :
+                ]
+
+        @pl.when(q >= 3)
+        def _():
+            slab[80:152, :] = w_up[pl.ds(pl.multiple_of(72 * q - 192, 8), 72), :]
+
+        @pl.when(q == 2)
+        def _():
+            slab[80:104, :] = w_up[0:24, :]
+            slab[104:168, :] = w_out[128:192, :]
+
+        @pl.when((q < 2) & (plane < 3))
+        def _():
+            slab[80:144, :] = w_out[pl.ds(pl.multiple_of(64 * q, 8), 64), :]
+
+        @pl.when((q < 2) & (plane == 3))
+        def _():
+            slab[80:176, :] = w_out[pl.ds(pl.multiple_of(96 * q, 8), 96), :]
+
+        @pl.when(q < 5)
+        def _():
+            slab[176:248, :] = w_up[pl.ds(pl.multiple_of(384 + 72 * q, 8), 72), :]
+
+        @pl.when(q == 5)
+        def _():
+            slab[176:200, :] = w_up[744:768, :]
+            slab[200:248, :] = w_down[0:48, :]
+
+        @pl.when(q > 5)
+        def _():
+            slab[176:248, :] = w_down[pl.ds(pl.multiple_of(72 * q - 384, 8), 72), :]
+
+        slab[256:328, :] = w_down[pl.ds(pl.multiple_of(192 + 72 * q, 8), 72), :]
+        slab[328:344, :] = tails[...]
+        ref[...] = slab[...].astype(BF)
+
+
+def local_call(kernel, outs, scratch, *operands):
+    vmem = pl.BlockSpec(memory_space=pltpu.VMEM)
+    return pl.pallas_call(
+        kernel,
+        out_shape=outs,
+        in_specs=[pl.BlockSpec(memory_space=pltpu.SMEM)] + [vmem] * (len(operands) - 1),
+        out_specs=jax.tree.map(lambda _: vmem, outs),
+        scratch_shapes=scratch,
+    )(*operands)
+
+
+def sliced_body(planes, places, block_input, out_grad, seg_ids, params, first_moment, second_moment):
+    count = planes * places * 2
+    spread = TAIL // count
+    dp, core = lax.axis_index("dp"), lax.axis_index("fsdp")
+    plane, spot = dp // places, dp % places
+    where_owner = jnp.stack([plane, 2 * spot + core]).astype(jnp.int32)
+    where_spot = jnp.stack([plane, spot, core]).astype(jnp.int32)
+    across = [
+        [(i, (i // places ^ r) * places + i % places) for i in range(planes * places)]
+        for r in range(planes)
+    ]
+    within = [
+        [(i, i // places * places + (i % places ^ r)) for i in range(planes * places)]
+        for r in range(places)
+    ]
+
+    def to_plane(value, r):
+        return lax.ppermute(value, "dp", across[r]) if r else value
+
+    def to_spot(value, r):
+        return lax.ppermute(value, "dp", within[r]) if r else value
+
+    def to_core(value):
+        return lax.ppermute(value, "fsdp", [(0, 1), (1, 0)])
+
+    micro, row_count, _ = block_input.shape
+    tokens = micro * row_count
+    flat_x = block_input.reshape(tokens, D)
+    mean = jnp.mean(flat_x, axis=-1, keepdims=True)
+    centred = flat_x - mean
+    inv_std = lax.rsqrt(jnp.mean(centred * centred, axis=-1, keepdims=True) + NORM_EPS)
+    normed = centred * inv_std
+    valid = (seg_ids >= 0).astype(F32).reshape(tokens, 1)
+    grad_y = out_grad.reshape(tokens, D) * valid
+    seg_rows = jnp.pad(seg_ids.reshape(1, tokens).astype(BF), ((0, 15), (0, D - tokens)))
+    sent_acts = jnp.concatenate([normed.astype(BF), grad_y.astype(BF), seg_rows])
+    acts = [to_plane(sent_acts, r) for r in range(planes)]
+
+    heads, hidden = permutations()
+    rows, tail = rows_from_flat(params, spread, count)
+    tail = jnp.pad(tail, ((0, 3), (0, 0)))
+    spot_shape = jax.ShapeDtypeStruct((SPOT, D), BF)
+    slab_shape = jax.ShapeDtypeStruct((SLAB, D), BF)
+    spots = local_call(
+        pack_kernel, [spot_shape] * planes, [pltpu.VMEM((planes, SPOT, D), F32)],
+        where_owner, rows, tail, heads, hidden,
+    )
+    spots = [to_plane(spots[r], r) for r in range(planes)]
+    slab = local_call(slab_kernel, slab_shape, [], where_owner, *spots)
+    slabs = [to_spot(slab, r) for r in range(places)]
+    slabs = slabs + [to_core(s) for s in slabs]
+
+    total = planes * tokens
+    outs = local_call(
+        layer_kernel,
+        [slab_shape] * 8 + [jax.ShapeDtypeStruct((2 * tokens, D), BF)] * planes,
+        [
+            pltpu.VMEM((D, D), F32),
+            pltpu.VMEM((D, D), F32),
+            pltpu.VMEM((256, D), F32),
+            pltpu.VMEM((3, PART, D), F32),
+            pltpu.VMEM((24, 4, 8, D), F32),
+            pltpu.VMEM((16, D), F32),
+            pltpu.VMEM((D, D), BF),
+            pltpu.VMEM((D, D), BF),
+            pltpu.VMEM((256, D), BF),
+            pltpu.VMEM((D, D), BF),
+            pltpu.VMEM((total, D), BF),
+            pltpu.VMEM((total, D), BF),
+            pltpu.VMEM((total, D), F32),
+            pltpu.VMEM((total, 256), BF),
+            pltpu.VMEM((total, D), F32),
+            pltpu.VMEM((total, 256), BF),
+            pltpu.VMEM((total, D), F32),
+            pltpu.VMEM((SLAB, D), F32),
+        ],
+        where_spot, *acts, *slabs,
+    )
+    grads, backs = outs[:8], outs[8:]
+    paired = [
+        (grads[r].astype(F32) + to_core(grads[4 + r]).astype(F32)).astype(BF) for r in range(places)
+    ]
+    arrived = [to_spot(paired[r], r) for r in range(places)]
+    backs = [to_plane(backs[r], r) for r in range(planes)]
+    spots = local_call(
+        split_kernel, [spot_shape] * planes, [pltpu.VMEM((SLAB, D), F32)], where_owner, *arrived
+    )
+    spots = [to_plane(spots[r], r) for r in range(planes)]
+    grad_rows, grad_tail = local_call(
+        unpack_kernel,
+        [
+            jax.ShapeDtypeStruct(rows.shape, F32),
+            jax.ShapeDtypeStruct((16, D), F32),
+        ],
+        [pltpu.VMEM((planes, SPOT, D), F32)],
+        where_owner, *spots, heads, hidden,
+    )
+    back = sum(b.astype(F32) for b in backs)
+    result = flat_x + back[:tokens]
+    scaled = back[tokens:]
+    input_grad = grad_y + inv_std * (
+        scaled
+        - jnp.mean(scaled, axis=-1, keepdims=True)
+        - normed * jnp.mean(scaled * normed, axis=-1, keepdims=True)
+    )
+    owned = flat_from_rows(grad_rows, grad_tail[:13], spread, count)
+    new_params, new_first, new_second = adam_update(params, owned, first_moment, second_moment)
+    return (
+        result.reshape(block_input.shape),
+        input_grad.reshape(block_input.shape),
+        owned,
+        new_params,
+        new_first,
+        new_second,
+    )
+
+
 def solution(mesh):
-    in_specs = (
-        P(None, ("dp", "fsdp"), None),
-        P(None, ("dp", "fsdp"), None),
-        P(None, ("dp", "fsdp")),
-        P(("dp", "fsdp")),
-        P(("dp", "fsdp")),
-        P(("dp", "fsdp")),
-    )
-    out_specs = (
-        P(None, ("dp", "fsdp"), None),
-        P(None, ("dp", "fsdp"), None),
-        P(("dp", "fsdp")),
-        P(("dp", "fsdp")),
-        P(("dp", "fsdp")),
-        P(("dp", "fsdp")),
-    )
-    count = mesh.shape["dp"] * mesh.shape["fsdp"]
-    return jax.shard_map(functools.partial(body, count), mesh=mesh, in_specs=in_specs, out_specs=out_specs, check_vma=False)
+    vector, tokens = P(AXES), P(None, AXES, None)
+    dp, cores = mesh.shape["dp"], mesh.shape["fsdp"]
+    if dp == PLANES * PLANES and cores == 2:
+        step = functools.partial(sliced_body, PLANES, dp // PLANES)
+    else:
+        step = functools.partial(body, dp * cores)
+    return jax.shard_map(
+        step,
+        mesh=mesh,
+        in_specs=(tokens, tokens, P(None, AXES), vector, vector, vector),
+        out_specs=(tokens, tokens, vector, vector, vector, vector),
+        check_vma=False,
+    )

time: 512 us -> 211 us (0.41); the launches traced: 502 us -> 208 us
  waiting for transfers between devices: 265 us -> 109 us
  local copies, waits for them, and re-layouts: 103 us -> 9.74 us
  matrix products: 58.2 us -> 0 us
  other arithmetic: 58.5 us -> 17.3 us
  Pallas kernels: 0 us -> 38.2 us
  starting transfers between devices: 2.12 us -> 32.5 us
  between operations: 15.1 us -> 0.95 us
    reduce_scatter x1 -> x0, waiting for transfers between devices: 159 us -> none  [body(): lax.psum_scatter(out, AXES, scatter_dimension=0, tiled=False)]
    ppermute x0 -> x26, waiting for transfers between devices: none -> 109 us  [the longest x12 78.8 us: to_plane(): return lax.ppermute(value, 'dp', across[r]) if r else value]
    all_gather x1 -> x0, waiting for transfers between devices: 98.4 us -> none  [body(): whole = lax.all_gather(sent, AXES, axis=0, tiled=False)]
    dot_general x18 -> x0, matrix products: 58.2 us -> none  [the longest x6 14.1 us: product(): return jnp.einsum(form, left, right, preferred_element_type=jnp.float32)]
    slice x10 -> x0, local copies, waits for them, and re-layouts: 46.2 us -> none  [the longest x2 26.6 us: unpack_flat(): pieces_out.append(flat_vec[offset:offset + length].reshape(item_shape))]
    pallas_call x0 -> x5, Pallas kernels: none -> 38.2 us  [local_call(): pl.pallas_call(kernel, out_shape=outs, in_specs=[pl.BlockSpec(memory_spac...]
    concatenate x3 -> x1, other arithmetic: 34.6 us -> 0.03 us  [sliced_body(): jnp.concatenate([normed.astype(BF), grad_y.astype(BF), seg_rows])]
    ppermute x0 -> x26, starting transfers between devices: none -> 31.9 us  [the longest x12 23.3 us: to_plane(): return lax.ppermute(value, 'dp', across[r]) if r else value]
  transfers between devices with their start and end apart: 4 -> 28, of which waited for: 4 -> 15; matrix products, arithmetic and copies ran while one was open for 3% -> 7% of each run, Pallas kernels for 0% -> 0%
where the time goes in v2:
time: 211 us; the launch traced here: 208 us
  waiting for transfers between devices  109 us (52%)
  Pallas kernels  38.2 us (18%)
  starting transfers between devices  32.5 us (15%)
  other arithmetic  17.3 us (8%)
  local copies, waits for them, and re-layouts  9.74 us (5%)
    ppermute x12, waiting for transfers between devices, to_plane(): return lax.ppermute(value, 'dp', across[r]) if r else value  78.8 us
    pallas_call x5, Pallas kernels, local_call(): pl.pallas_call(kernel, out_shape=outs, in_specs=[pl.BlockSpec(memory_spac...  38.2 us
    ppermute x6, waiting for transfers between devices, to_spot(): return lax.ppermute(value, 'dp', within[r]) if r else value  29.8 us
    ppermute x12, starting transfers between devices, to_plane(): return lax.ppermute(value, 'dp', across[r]) if r else value  23.3 us
    ppermute x6, starting transfers between devices, to_spot(): return lax.ppermute(value, 'dp', within[r]) if r else value  7.52 us
    unnamed x62, local copies, waits for them, and re-layouts  5.96 us
    sub x1, other arithmetic, adam_update(): params - LEARN_RATE * (first_hat / (jnp.sqrt(second_hat) + ADAM_EPS) + WE...  4.4 us
  transfers between devices with their start and end apart: 28, of which 15 were waited for; matrix products, arithmetic and copies ran while one was open for 7% of the time, Pallas kernels for 0%

profile of v2, /device:TPU:0, one launch (start us, length us, event | category | flops | bytes accessed | tf_op | source)
XLA Modules:
  0.0 207.8 jit_solution(10104293970863673769)
XLA Ops:
  5.1 2.3 %fusion = (bf16[768,768]{1,0:T(8,128)(2,1)}, bf16[768,768]{1,0:T(8,128)(2,1)}) fusion(s32[768]{0:T(1024)S(1)} %fusion.16, s32[768]{0:T(1024)S(1)} %fusion.19), kind=kLoop, calls=%fused_computation.2 | loop fusion | flops 2359296 | bytes 2365440 | tf_op jit(solution)/shard_map/convert_element_type | solution.py:395
  11.1 5.9 %shard_map.109 = (bf16[96,768]{1,0:T(8,128)(2,1)}, bf16[96,768]{1,0:T(8,128)(2,1)}, bf16[96,768]{1,0:T(8,128)(2,1)}, bf16[96,768]{1,0:T(8,128)(2,1)}) custom-call(s32[2]{0:T(128)} %pad_add_fusion.1.where_ref, f32[288,768]{1,0:T(8,128)} %reshape.166.rows_ref, f32[16,768]{1,0:T(8,128)} %pad.9.tail_ref, bf16[768,768]{1,0:T(8,128)(2,1)} %get-tuple-element.60.heads_ref.refs_4_, ...), custom_call_target="tpu_custom_call" | custom-call | tf_op jit(solution)/shard_map/pallas_call | solution.py:831
  16.9 3.9 %collective-permute-start.5 = (bf16[96,768]{1,0:T(8,128)(2,1)}, bf16[96,768]{1,0:T(8,128)(2,1)S(1)}, u32[]{:S(2)}, u32[]{:S(2)}) collective-permute-start(bf16[96,768]{1,0:T(8,128)(2,1)} %get-tuple-element.30), channel_id=1, source_target_pairs={{0,16},{2,18},{4,20},{6,22},{8,24},{10,26},{12,28},{14,30},{16,0},... | collective-permute-start | bytes 442376 | tf_op jit(solution)/shard_map/ppermute | solution.py:857
  22.4 3.6 %collective-permute-done.4.b_ref = bf16[96,768]{1,0:T(8,128)(2,1)S(1)} collective-permute-done((bf16[96,768]{1,0:T(8,128)(2,1)}, bf16[96,768]{1,0:T(8,128)(2,1)S(1)}, u32[]{:S(2)}, u32[]{:S(2)}) %collective-permute-start.4) | collective-permute-done | bytes 147488 | tf_op jit(solution)/shard_map/ppermute | solution.py:857
  26.0 7.0 %collective-permute-done.6.d_ref = bf16[96,768]{1,0:T(8,128)(2,1)S(1)} collective-permute-done((bf16[96,768]{1,0:T(8,128)(2,1)}, bf16[96,768]{1,0:T(8,128)(2,1)S(1)}, u32[]{:S(2)}, u32[]{:S(2)}) %collective-permute-start.6) | collective-permute-done | bytes 147488 | tf_op jit(solution)/shard_map/ppermute | solution.py:857
  35.6 2.9 %collective-permute-start.9 = (bf16[352,768]{1,0:T(8,128)(2,1)}, bf16[352,768]{1,0:T(8,128)(2,1)S(1)}, u32[]{:S(2)}, u32[]{:S(2)}) collective-permute-start(bf16[352,768]{1,0:T(8,128)(2,1)} %shard_map.110.refs_4_), channel_id=1, source_target_pairs={{0,6},{2,4},{4,2},{6,0},{8,14},{10,12},{12,10},{14,8},{16,22},{18,... | collective-permute-start | bytes 1622024 | tf_op jit(solution)/shard_map/ppermute | solution.py:860
  39.5 2.7 %collective-permute-start.2 = (bf16[272,768]{1,0:T(8,128)(2,1)S(1)}, bf16[272,768]{1,0:T(8,128)(2,1)S(1)}, u32[]{:S(2)}, u32[]{:S(2)}) collective-permute-start(bf16[272,768]{1,0:T(8,128)(2,1)S(1)} %fusion.6.refs_0_), channel_id=1, source_target_pairs={{0,24},{2,26},{4,28},{6,30},{8,16},{10,18},{12,20},{14,22},{16,8},... | collective-permute-start | bytes 1253384 | tf_op jit(solution)/shard_map/ppermute | solution.py:857
  42.1 2.5 %collective-permute-start.1 = (bf16[272,768]{1,0:T(8,128)(2,1)S(1)}, bf16[272,768]{1,0:T(8,128)(2,1)S(1)}, u32[]{:S(2)}, u32[]{:S(2)}) collective-permute-start(bf16[272,768]{1,0:T(8,128)(2,1)S(1)} %fusion.6.refs_0_), channel_id=1, source_target_pairs={{0,16},{2,18},{4,20},{6,22},{8,24},{10,26},{12,28},{14,30},{16,0},... | collective-permute-start | bytes 1253384 | tf_op jit(solution)/shard_map/ppermute | solution.py:857
  44.7 9.3 %collective-permute-done.2.refs_3_ = bf16[272,768]{1,0:T(8,128)(2,1)S(1)} collective-permute-done((bf16[272,768]{1,0:T(8,128)(2,1)S(1)}, bf16[272,768]{1,0:T(8,128)(2,1)S(1)}, u32[]{:S(2)}, u32[]{:S(2)}) %collective-permute-start.2) | collective-permute-done | bytes 417824 | tf_op jit(solution)/shard_map/ppermute | solution.py:857
  54.5 8.5 %collective-permute-done.8.refs_6_ = bf16[352,768]{1,0:T(8,128)(2,1)S(1)} collective-permute-done((bf16[352,768]{1,0:T(8,128)(2,1)}, bf16[352,768]{1,0:T(8,128)(2,1)S(1)}, u32[]{:S(2)}, u32[]{:S(2)}) %collective-permute-start.8) | collective-permute-done | bytes 540704 | tf_op jit(solution)/shard_map/ppermute | solution.py:860
  63.6 15.8 %collective-permute-done.1.refs_2_ = bf16[272,768]{1,0:T(8,128)(2,1)S(1)} collective-permute-done((bf16[272,768]{1,0:T(8,128)(2,1)S(1)}, bf16[272,768]{1,0:T(8,128)(2,1)S(1)}, u32[]{:S(2)}, u32[]{:S(2)}) %collective-permute-start.1) | collective-permute-done | bytes 417824 | tf_op jit(solution)/shard_map/ppermute | solution.py:857
  80.1 10.9 %collective-permute-done.refs_1_ = bf16[272,768]{1,0:T(8,128)(2,1)S(1)} collective-permute-done((bf16[272,768]{1,0:T(8,128)(2,1)S(1)}, bf16[272,768]{1,0:T(8,128)(2,1)S(1)}, u32[]{:S(2)}, u32[]{:S(2)}) %collective-permute-start) | collective-permute-done | bytes 417824 | tf_op jit(solution)/shard_map/ppermute | solution.py:857
  93.0 19.9 %shard_map.111 = (bf16[352,768]{1,0:T(8,128)(2,1)}, bf16[352,768]{1,0:T(8,128)(2,1)}, bf16[352,768]{1,0:T(8,128)(2,1)}, bf16[352,768]{1,0:T(8,128)(2,1)}, bf16[3...) custom-call(s32[3]{0:T(128)} %pad_add_fusion.where_ref, ...), custom_call_target="tpu_custom_call" | custom-call | tf_op jit(solution)/shard_map/pallas_call | solution.py:831
  113.2 2.5 %collective-permute-start.15 = (bf16[256,768]{1,0:T(8,128)(2,1)}, bf16[256,768]{1,0:T(8,128)(2,1)S(1)}, u32[]{:S(2)}, u32[]{:S(2)}) collective-permute-start(bf16[256,768]{1,0:T(8,128)(2,1)} %get-tuple-element.34), channel_id=1, source_target_pairs={{0,16},{2,18},{4,20},{6,22},{8,24},{10,26},{12,28},{14,30},{16,0},... | collective-permute-start | bytes 1179656 | tf_op jit(solution)/shard_map/ppermute | solution.py:857
  117.8 12.9 %collective-permute-done.14 = bf16[256,768]{1,0:T(8,128)(2,1)S(1)} collective-permute-done((bf16[256,768]{1,0:T(8,128)(2,1)}, bf16[256,768]{1,0:T(8,128)(2,1)S(1)}, u32[]{:S(2)}, u32[]{:S(2)}) %collective-permute-start.14) | collective-permute-done | bytes 393248 | tf_op jit(solution)/shard_map/ppermute | solution.py:857
  130.7 12.5 %collective-permute-done.15 = bf16[256,768]{1,0:T(8,128)(2,1)S(1)} collective-permute-done((bf16[256,768]{1,0:T(8,128)(2,1)}, bf16[256,768]{1,0:T(8,128)(2,1)S(1)}, u32[]{:S(2)}, u32[]{:S(2)}) %collective-permute-start.15) | collective-permute-done | bytes 393248 | tf_op jit(solution)/shard_map/ppermute | solution.py:857
  152.5 9.0 %collective-permute-done.19.b_ref = bf16[352,768]{1,0:T(8,128)(2,1)S(1)} collective-permute-done((bf16[352,768]{1,0:T(8,128)(2,1)S(1)}, bf16[352,768]{1,0:T(8,128)(2,1)S(1)}, u32[]{:S(2)}, u32[]{:S(2)}) %collective-permute-start.19) | collective-permute-done | bytes 540704 | tf_op jit(solution)/shard_map/ppermute | solution.py:860
  161.5 10.6 %collective-permute-done.21.c_ref = bf16[352,768]{1,0:T(8,128)(2,1)S(1)} collective-permute-done((bf16[352,768]{1,0:T(8,128)(2,1)S(1)}, bf16[352,768]{1,0:T(8,128)(2,1)S(1)}, u32[]{:S(2)}, u32[]{:S(2)}) %collective-permute-start.21) | collective-permute-done | bytes 540704 | tf_op jit(solution)/shard_map/ppermute | solution.py:860
  173.2 2.8 %shard_map.112 = (bf16[96,768]{1,0:T(8,128)(2,1)}, bf16[96,768]{1,0:T(8,128)(2,1)}, bf16[96,768]{1,0:T(8,128)(2,1)}, bf16[96,768]{1,0:T(8,128)(2,1)}) custom-call(s32[2]{0:T(128)} %pad_add_fusion.1.where_ref, bf16[352,768]{1,0:T(8,128)(2,1)} %add_convert_fusion.3.a_ref, bf16[352,768]{1,0:T(8,128)(2,1)} %copy-done.15, bf16[352,768]{1,0:T(8,128)(2,1)} %copy-done.16, ...), custom_call_target="tpu_custom_call" | custom-call | tf_op jit(solution)/shard_map/pallas_call | solution.py:831
  176.1 5.1 %collective-permute-start.24 = (bf16[96,768]{1,0:T(8,128)(2,1)}, bf16[96,768]{1,0:T(8,128)(2,1)S(1)}, u32[]{:S(2)}, u32[]{:S(2)}) collective-permute-start(bf16[96,768]{1,0:T(8,128)(2,1)} %get-tuple-element.45), channel_id=1, source_target_pairs={{0,8},{2,10},{4,12},{6,14},{8,0},{10,2},{12,4},{14,6},{16,24},{18,... | collective-permute-start | bytes 442376 | tf_op jit(solution)/shard_map/ppermute | solution.py:857
  185.1 3.3 %collective-permute-done.24.refs_1_ = bf16[96,768]{1,0:T(8,128)(2,1)S(1)} collective-permute-done((bf16[96,768]{1,0:T(8,128)(2,1)}, bf16[96,768]{1,0:T(8,128)(2,1)S(1)}, u32[]{:S(2)}, u32[]{:S(2)}) %collective-permute-start.24) | collective-permute-done | bytes 147488 | tf_op jit(solution)/shard_map/ppermute | solution.py:857
  188.4 3.7 %collective-permute-done.25.refs_2_ = bf16[96,768]{1,0:T(8,128)(2,1)S(1)} collective-permute-done((bf16[96,768]{1,0:T(8,128)(2,1)}, bf16[96,768]{1,0:T(8,128)(2,1)S(1)}, u32[]{:S(2)}, u32[]{:S(2)}) %collective-permute-start.25) | collective-permute-done | bytes 147488 | tf_op jit(solution)/shard_map/ppermute | solution.py:857
  192.8 7.6 %shard_map.113 = (f32[288,768]{1,0:T(8,128)}, f32[16,768]{1,0:T(8,128)}) custom-call(s32[2]{0:T(128)} %pad_add_fusion.1.where_ref, bf16[96,768]{1,0:T(8,128)(2,1)} %get-tuple-element.44.refs_0_, bf16[96,768]{1,0:T(8,128)(2,1)} %copy-done.22, bf16[96,768]{1,0:T(8,128)(2,1)} %copy-done.23, bf16[96,768]{1,0:T(8,128)(2,1)} %copy-done.24, ...), custom_call_target="tpu_custom_call" | custom-call | tf_op jit(solution)/shard_map/pallas_call | solution.py:831
  203.4 4.4 %multiply_subtract_fusion = (f32[221496]{0:T(1024)}, f32[221496]{0:T(1024)}, f32[221496]{0:T(1024)}, f32[221496]{0:T(1024)}) fusion(f32[221496]{0:T(1024)S(1)} %copy-done.1, f32[221496]{0:T(1024)} %param.10, f32[221496]{0:T(1024)} %param.11, s32[]{:T(128)S(6)} %select_n.164, f32[9984]{0:T(1024)S(1)} %broadcast_select_fusion, f32[221184]{0:T(1024)S(1)} %reshape.170), kind=kLoop, calls=%fused_computation.15 | loop fusion | flops 3543936 | bytes 7126564 | tf_op jit(solution)/shard_map/sub | solution.py:283
  (136 shorter events, 37.6 us)
Async XLA Ops:
  16.9 9.1 %collective-permute-start.5 = (bf16[96,768]{1,0:T(8,128)(2,1)}, bf16[96,768]{1,0:T(8,128)(2,1)S(1)}, u32[]{:S(2)}, u32[]{:S(2)}) collective-permute-start(bf16[96,768]{1,0:T(8,128)(2,1)} %get-tuple-element.30), channel_id=1, source_target_pairs={{0,16},{2,18},{4,20},{6,22},{8,24},{10,26},{12,28},{14,30},{16,0},... | collective-permute-start | bytes 442376 | tf_op jit(solution)/shard_map/ppermute | solution.py:857
  20.8 12.2 %collective-permute-start.6 = (bf16[96,768]{1,0:T(8,128)(2,1)}, bf16[96,768]{1,0:T(8,128)(2,1)S(1)}, u32[]{:S(2)}, u32[]{:S(2)}) collective-permute-start(bf16[96,768]{1,0:T(8,128)(2,1)} %get-tuple-element.31), channel_id=1, source_target_pairs={{0,24},{2,26},{4,28},{6,30},{8,16},{10,18},{12,20},{14,22},{16,8},... | collective-permute-start | bytes 442376 | tf_op jit(solution)/shard_map/ppermute | solution.py:857
  35.6 18.3 %collective-permute-start.9 = (bf16[352,768]{1,0:T(8,128)(2,1)}, bf16[352,768]{1,0:T(8,128)(2,1)S(1)}, u32[]{:S(2)}, u32[]{:S(2)}) collective-permute-start(bf16[352,768]{1,0:T(8,128)(2,1)} %shard_map.110.refs_4_), channel_id=1, source_target_pairs={{0,6},{2,4},{4,2},{6,0},{8,14},{10,12},{12,10},{14,8},{16,22},{18,... | collective-permute-start | bytes 1622024 | tf_op jit(solution)/shard_map/ppermute | solution.py:860
  38.5 24.4 %collective-permute-start.8 = (bf16[352,768]{1,0:T(8,128)(2,1)}, bf16[352,768]{1,0:T(8,128)(2,1)S(1)}, u32[]{:S(2)}, u32[]{:S(2)}) collective-permute-start(bf16[352,768]{1,0:T(8,128)(2,1)} %shard_map.110.refs_4_), channel_id=1, source_target_pairs={{0,4},{2,6},{4,0},{6,2},{8,12},{10,14},{12,8},{14,10},{16,20},{18,... | collective-permute-start | bytes 1622024 | tf_op jit(solution)/shard_map/ppermute | solution.py:860
  38.6 25.0 %collective-permute-start.7 = (bf16[352,768]{1,0:T(8,128)(2,1)}, bf16[352,768]{1,0:T(8,128)(2,1)S(1)}, u32[]{:S(2)}, u32[]{:S(2)}) collective-permute-start(bf16[352,768]{1,0:T(8,128)(2,1)} %shard_map.110.refs_4_), channel_id=1, source_target_pairs={{0,2},{2,0},{4,6},{6,4},{8,10},{10,8},{12,14},{14,12},{16,18},{18,... | collective-permute-start | bytes 1622024 | tf_op jit(solution)/shard_map/ppermute | solution.py:860
  39.5 14.5 %collective-permute-start.2 = (bf16[272,768]{1,0:T(8,128)(2,1)S(1)}, bf16[272,768]{1,0:T(8,128)(2,1)S(1)}, u32[]{:S(2)}, u32[]{:S(2)}) collective-permute-start(bf16[272,768]{1,0:T(8,128)(2,1)S(1)} %fusion.6.refs_0_), channel_id=1, source_target_pairs={{0,24},{2,26},{4,28},{6,30},{8,16},{10,18},{12,20},{14,22},{16,8},... | collective-permute-start | bytes 1253384 | tf_op jit(solution)/shard_map/ppermute | solution.py:857
  42.1 37.2 %collective-permute-start.1 = (bf16[272,768]{1,0:T(8,128)(2,1)S(1)}, bf16[272,768]{1,0:T(8,128)(2,1)S(1)}, u32[]{:S(2)}, u32[]{:S(2)}) collective-permute-start(bf16[272,768]{1,0:T(8,128)(2,1)S(1)} %fusion.6.refs_0_), channel_id=1, source_target_pairs={{0,16},{2,18},{4,20},{6,22},{8,24},{10,26},{12,28},{14,30},{16,0},... | collective-permute-start | bytes 1253384 | tf_op jit(solution)/shard_map/ppermute | solution.py:857
  54.0 37.0 %collective-permute-start.10 = (bf16[352,768]{1,0:T(8,128)(2,1)}, bf16[352,768]{1,0:T(8,128)(2,1)S(1)}, u32[]{:S(2)}, u32[]{:S(2)}) collective-permute-start(bf16[352,768]{1,0:T(8,128)(2,1)} %shard_map.110.refs_4_), channel_id=1, source_target_pairs={{0,1},{1,0},{2,3},{3,2},{4,5},{5,4},{6,7},{7,6},{8,9},{9,8},{10,11... | collective-permute-start | bytes 1622024 | tf_op jit(solution)/shard_map/ppermute | solution.py:863
  54.0 37.0 %collective-permute-start.13 = (bf16[352,768]{1,0:T(8,128)(2,1)S(1)}, bf16[352,768]{1,0:T(8,128)(2,1)S(1)}, u32[]{:S(2)}, u32[]{:S(2)}) collective-permute-start(bf16[352,768]{1,0:T(8,128)(2,1)S(1)} %collective-permute-done.9.refs_7_), channel_id=1, source_target_pairs={{0,1},{1,0},{2,3},{3,2},{4,5},{5,4},{6,7},{7,6},{8,9},{9,8},{10,11... | collective-permute-start | bytes 1622024 | tf_op jit(solution)/shard_map/ppermute | solution.py:863
  62.9 28.0 %collective-permute-start.12 = (bf16[352,768]{1,0:T(8,128)(2,1)S(1)}, bf16[352,768]{1,0:T(8,128)(2,1)S(1)}, u32[]{:S(2)}, u32[]{:S(2)}) collective-permute-start(bf16[352,768]{1,0:T(8,128)(2,1)S(1)} %collective-permute-done.8.refs_6_), channel_id=1, source_target_pairs={{0,1},{1,0},{2,3},{3,2},{4,5},{5,4},{6,7},{7,6},{8,9},{9,8},{10,11... | collective-permute-start | bytes 1622024 | tf_op jit(solution)/shard_map/ppermute | solution.py:863
  63.6 29.3 %collective-permute-start.11 = (bf16[352,768]{1,0:T(8,128)(2,1)S(1)}, bf16[352,768]{1,0:T(8,128)(2,1)}, u32[]{:S(2)}, u32[]{:S(2)}) collective-permute-start(bf16[352,768]{1,0:T(8,128)(2,1)S(1)} %collective-permute-done.7.refs_5_), channel_id=1, source_target_pairs={{0,1},{1,0},{2,3},{3,2},{4,5},{5,4},{6,7},{7,6},{8,9},{9,8},{10,11... | collective-permute-start | bytes 1622024 | tf_op jit(solution)/shard_map/ppermute | solution.py:863
  79.4 11.6 %collective-permute-start = (bf16[272,768]{1,0:T(8,128)(2,1)S(1)}, bf16[272,768]{1,0:T(8,128)(2,1)S(1)}, u32[]{:S(2)}, u32[]{:S(2)}) collective-permute-start(bf16[272,768]{1,0:T(8,128)(2,1)S(1)} %fusion.6.refs_0_), channel_id=1, source_target_pairs={{0,8},{2,10},{4,12},{6,14},{8,0},{10,2},{12,4},{14,6},{16,24},{18,... | collective-permute-start | bytes 1253384 | tf_op jit(solution)/shard_map/ppermute | solution.py:857
  112.9 17.8 %collective-permute-start.14 = (bf16[256,768]{1,0:T(8,128)(2,1)}, bf16[256,768]{1,0:T(8,128)(2,1)S(1)}, u32[]{:S(2)}, u32[]{:S(2)}) collective-permute-start(bf16[256,768]{1,0:T(8,128)(2,1)} %get-tuple-element.33), channel_id=1, source_target_pairs={{0,8},{2,10},{4,12},{6,14},{8,0},{10,2},{12,4},{14,6},{16,24},{18,... | collective-permute-start | bytes 1179656 | tf_op jit(solution)/shard_map/ppermute | solution.py:857
  113.2 30.0 %collective-permute-start.15 = (bf16[256,768]{1,0:T(8,128)(2,1)}, bf16[256,768]{1,0:T(8,128)(2,1)S(1)}, u32[]{:S(2)}, u32[]{:S(2)}) collective-permute-start(bf16[256,768]{1,0:T(8,128)(2,1)} %get-tuple-element.34), channel_id=1, source_target_pairs={{0,16},{2,18},{4,20},{6,22},{8,24},{10,26},{12,28},{14,30},{16,0},... | collective-permute-start | bytes 1179656 | tf_op jit(solution)/shard_map/ppermute | solution.py:857
  115.7 27.4 %collective-permute-start.16 = (bf16[256,768]{1,0:T(8,128)(2,1)}, bf16[256,768]{1,0:T(8,128)(2,1)S(1)}, u32[]{:S(2)}, u32[]{:S(2)}) collective-permute-start(bf16[256,768]{1,0:T(8,128)(2,1)} %get-tuple-element.35), channel_id=1, source_target_pairs={{0,24},{2,26},{4,28},{6,30},{8,16},{10,18},{12,20},{14,22},{16,8},... | collective-permute-start | bytes 1179656 | tf_op jit(solution)/shard_map/ppermute | solution.py:857
  117.3 28.8 %collective-permute-start.18 = (bf16[352,768]{1,0:T(8,128)(2,1)}, bf16[352,768]{1,0:T(8,128)(2,1)S(1)}, u32[]{:S(2)}, u32[]{:S(2)}) collective-permute-start(bf16[352,768]{1,0:T(8,128)(2,1)} %get-tuple-element.39), channel_id=1, source_target_pairs={{0,1},{1,0},{2,3},{3,2},{4,5},{5,4},{6,7},{7,6},{8,9},{9,8},{10,11... | collective-permute-start | bytes 1622024 | tf_op jit(solution)/shard_map/ppermute | solution.py:863
  117.3 34.3 %collective-permute-start.17 = (bf16[352,768]{1,0:T(8,128)(2,1)}, bf16[352,768]{1,0:T(8,128)(2,1)S(1)}, u32[]{:S(2)}, u32[]{:S(2)}) collective-permute-start(bf16[352,768]{1,0:T(8,128)(2,1)} %get-tuple-element.37), channel_id=1, source_target_pairs={{0,1},{1,0},{2,3},{3,2},{4,5},{5,4},{6,7},{7,6},{8,9},{9,8},{10,11... | collective-permute-start | bytes 1622024 | tf_op jit(solution)/shard_map/ppermute | solution.py:863
  130.7 16.9 %collective-permute-start.20 = (bf16[352,768]{1,0:T(8,128)(2,1)}, bf16[352,768]{1,0:T(8,128)(2,1)S(1)}, u32[]{:S(2)}, u32[]{:S(2)}) collective-permute-start(bf16[352,768]{1,0:T(8,128)(2,1)} %get-tuple-element.41), channel_id=1, source_target_pairs={{0,1},{1,0},{2,3},{3,2},{4,5},{5,4},{6,7},{7,6},{8,9},{9,8},{10,11... | collective-permute-start | bytes 1622024 | tf_op jit(solution)/shard_map/ppermute | solution.py:863
  146.3 15.2 %collective-permute-start.19 = (bf16[352,768]{1,0:T(8,128)(2,1)S(1)}, bf16[352,768]{1,0:T(8,128)(2,1)S(1)}, u32[]{:S(2)}, u32[]{:S(2)}) collective-permute-start(bf16[352,768]{1,0:T(8,128)(2,1)S(1)} %add_convert_fusion.2), channel_id=1, source_target_pairs={{0,2},{2,0},{4,6},{6,4},{8,10},{10,8},{12,14},{14,12},{16,18},{18,... | collective-permute-start | bytes 1622024 | tf_op jit(solution)/shard_map/ppermute | solution.py:860
  147.8 24.4 %collective-permute-start.21 = (bf16[352,768]{1,0:T(8,128)(2,1)S(1)}, bf16[352,768]{1,0:T(8,128)(2,1)S(1)}, u32[]{:S(2)}, u32[]{:S(2)}) collective-permute-start(bf16[352,768]{1,0:T(8,128)(2,1)S(1)} %add_convert_fusion.1), channel_id=1, source_target_pairs={{0,4},{2,6},{4,0},{6,2},{8,12},{10,14},{12,8},{14,10},{16,20},{18,... | collective-permute-start | bytes 1622024 | tf_op jit(solution)/shard_map/ppermute | solution.py:860
  149.5 23.7 %collective-permute-start.23 = (bf16[352,768]{1,0:T(8,128)(2,1)S(1)}, bf16[352,768]{1,0:T(8,128)(2,1)}, u32[]{:S(2)}, u32[]{:S(2)}) collective-permute-start(bf16[352,768]{1,0:T(8,128)(2,1)S(1)} %add_convert_fusion), channel_id=1, source_target_pairs={{0,6},{2,4},{4,2},{6,0},{8,14},{10,12},{12,10},{14,8},{16,22},{18,... | collective-permute-start | bytes 1622024 | tf_op jit(solution)/shard_map/ppermute | solution.py:860
  176.1 12.3 %collective-permute-start.24 = (bf16[96,768]{1,0:T(8,128)(2,1)}, bf16[96,768]{1,0:T(8,128)(2,1)S(1)}, u32[]{:S(2)}, u32[]{:S(2)}) collective-permute-start(bf16[96,768]{1,0:T(8,128)(2,1)} %get-tuple-element.45), channel_id=1, source_target_pairs={{0,8},{2,10},{4,12},{6,14},{8,0},{10,2},{12,4},{14,6},{16,24},{18,... | collective-permute-start | bytes 442376 | tf_op jit(solution)/shard_map/ppermute | solution.py:857
  181.1 11.0 %collective-permute-start.25 = (bf16[96,768]{1,0:T(8,128)(2,1)}, bf16[96,768]{1,0:T(8,128)(2,1)S(1)}, u32[]{:S(2)}, u32[]{:S(2)}) collective-permute-start(bf16[96,768]{1,0:T(8,128)(2,1)} %get-tuple-element.46), channel_id=1, source_target_pairs={{0,16},{2,18},{4,20},{6,22},{8,24},{10,26},{12,28},{14,30},{16,0},... | collective-permute-start | bytes 442376 | tf_op jit(solution)/shard_map/ppermute | solution.py:857
  183.0 9.1 %collective-permute-start.26 = (bf16[96,768]{1,0:T(8,128)(2,1)}, bf16[96,768]{1,0:T(8,128)(2,1)S(1)}, u32[]{:S(2)}, u32[]{:S(2)}) collective-permute-start(bf16[96,768]{1,0:T(8,128)(2,1)} %get-tuple-element.47), channel_id=1, source_target_pairs={{0,24},{2,26},{4,28},{6,30},{8,16},{10,18},{12,20},{14,22},{16,8},... | collective-permute-start | bytes 442376 | tf_op jit(solution)/shard_map/ppermute | solution.py:857
  (35 other events, 310.5 us)

commit v3 on v2

--- a/solution.py
+++ b/solution.py
@@ -7,6 +7,7 @@
 from jax.experimental import pallas as pl
 from jax.experimental.pallas import tpu as pltpu
 from jax.sharding import PartitionSpec as P
+
 
 D = 768
 FF = 3072
@@ -190,20 +191,7 @@
 
 
 def backward(kept_state, grad_rows, weights):
-    (
-        w_qkv,
-        w_out,
-        w_up,
-        w_down,
-        b_qkv,
-        b_out,
-        b_up,
-        b_down,
-        gain_one,
-        shift_one,
-        gain_two,
-        shift_two,
-    ) = weights
+    (w_qkv, w_out, w_up, w_down, _, _, _, _, gain_one, _, gain_two, _) = weights
     (
         normed_one,
         inv_one,
@@ -240,7 +228,7 @@
     grad_act_two = jnp.dot(grad_up_bf, w_up.T, preferred_element_type=jnp.float32)
     grad_attn = jnp.dot(grad_y_bf, w_out.T, preferred_element_type=jnp.float32).astype(jnp.bfloat16)
     grad_attn = grad_attn.reshape(group_count, row_count, HEADS, HEAD_DIM)
-    prob_rows, unused_total = softmax_rows(query_bf, key_bf, allowed, log_total)
+    prob_rows, _ = softmax_rows(query_bf, key_bf, allowed, log_total)
     prob_bf = prob_rows.astype(jnp.bfloat16)
     grad_value = product("ghqk,gqhd->gkhd", prob_bf, grad_attn)
     grad_prob = product("gqhd,gkhd->ghqk", grad_attn, value_bf)
@@ -287,7 +275,6 @@
 
 
 AXES = ("dp", "fsdp")
-MATRIX_ROWS = 9 * D + 3 * D
 TAIL = 13 * D
 
 
@@ -837,6 +824,10 @@
     )(*operands)
 
 
+def sliced_step(planes, places, *args):
+    return sliced_body(planes, places, *args)
+
+
 def sliced_body(planes, places, block_input, out_grad, seg_ids, params, first_moment, second_moment):
     count = planes * places * 2
     spread = TAIL // count
@@ -873,7 +864,8 @@
     grad_y = out_grad.reshape(tokens, D) * valid
     seg_rows = jnp.pad(seg_ids.reshape(1, tokens).astype(BF), ((0, 15), (0, D - tokens)))
     sent_acts = jnp.concatenate([normed.astype(BF), grad_y.astype(BF), seg_rows])
-    acts = [to_plane(sent_acts, r) for r in range(planes)]
+    acts = [to_plane(sent_acts, r) for r in range(3)]
+    acts.append(to_plane(acts[2], 1))
 
     heads, hidden = permutations()
     rows, tail = rows_from_flat(params, spread, count)
@@ -920,7 +912,12 @@
         (grads[r].astype(F32) + to_core(grads[4 + r]).astype(F32)).astype(BF) for r in range(places)
     ]
     arrived = [to_spot(paired[r], r) for r in range(places)]
-    backs = [to_plane(backs[r], r) for r in range(planes)]
+    passed = to_plane(backs[3], 1)
+    backs = [
+        backs[0],
+        to_plane(backs[1], 1),
+        to_plane((backs[2].astype(F32) + passed.astype(F32)).astype(BF), 2),
+    ]
     spots = local_call(
         split_kernel, [spot_shape] * planes, [pltpu.VMEM((SLAB, D), F32)], where_owner, *arrived
     )
@@ -958,7 +955,7 @@
     vector, tokens = P(AXES), P(None, AXES, None)
     dp, cores = mesh.shape["dp"], mesh.shape["fsdp"]
     if dp == PLANES * PLANES and cores == 2:
-        step = functools.partial(sliced_body, PLANES, dp // PLANES)
+        step = functools.partial(sliced_step, PLANES, dp // PLANES)
     else:
         step = functools.partial(body, dp * cores)
     return jax.shard_map(

time: 211 us -> 177 us (0.84)
  waiting for transfers between devices: 109 us -> 79.1 us
    ppermute x6, waiting for transfers between devices: 29.8 us -> 8.52 us  [to_spot(): return lax.ppermute(value, 'dp', within[r]) if r else value]
    ppermute x12, waiting for transfers between devices: 78.8 us -> 70 us  [to_plane(): return lax.ppermute(value, 'dp', across[r]) if r else value]
    unnamed x62 -> x58, local copies, waits for them, and re-layouts: 5.96 us -> 5.16 us
  transfers between devices with their start and end apart: 28 -> 28, of which waited for: 15 -> 12; matrix products, arithmetic and copies ran while one was open for 7% -> 7% of each run, Pallas kernels for 0% -> 0%
where the time goes in v3:
time: 177 us; the launch traced here: 175 us
  waiting for transfers between devices  79.1 us (45%)
  Pallas kernels  38.3 us (22%)
  starting transfers between devices  32 us (18%)
  other arithmetic  15.4 us (9%)
  local copies, waits for them, and re-layouts  8.95 us (5%)
    ppermute x12, waiting for transfers between devices, to_plane(): return lax.ppermute(value, 'dp', across[r]) if r else value  70 us
    pallas_call x5, Pallas kernels, local_call(): pl.pallas_call(kernel, out_shape=outs, in_specs=[pl.BlockSpec(memory_spac...  38.3 us
    ppermute x12, starting transfers between devices, to_plane(): return lax.ppermute(value, 'dp', across[r]) if r else value  22.8 us
    ppermute x6, waiting for transfers between devices, to_spot(): return lax.ppermute(value, 'dp', within[r]) if r else value  8.52 us
    ppermute x6, starting transfers between devices, to_spot(): return lax.ppermute(value, 'dp', within[r]) if r else value  7.48 us
    unnamed x58, local copies, waits for them, and re-layouts  5.16 us
    sub x1, other arithmetic, adam_update(): params - LEARN_RATE * (first_hat / (jnp.sqrt(second_hat) + ADAM_EPS) + WE...  4.4 us
  transfers between devices with their start and end apart: 28, of which 12 were waited for; matrix products, arithmetic and copies ran while one was open for 7% of the time, Pallas kernels for 0%

profile of v3, /device:TPU:0, one launch (start us, length us, event | category | flops | bytes accessed | tf_op | source)
XLA Modules:
  0.0 174.7 jit_solution(15733587894525505245)
XLA Ops:
  5.1 2.3 %fusion = (bf16[768,768]{1,0:T(8,128)(2,1)}, bf16[768,768]{1,0:T(8,128)(2,1)}) fusion(s32[768]{0:T(1024)S(1)} %fusion.16, s32[768]{0:T(1024)S(1)} %fusion.19), kind=kLoop, calls=%fused_computation.2 | loop fusion | flops 2359296 | bytes 2365440 | tf_op jit(solution)/shard_map/convert_element_type | solution.py:382
  11.1 5.9 %shard_map.109 = (bf16[96,768]{1,0:T(8,128)(2,1)}, bf16[96,768]{1,0:T(8,128)(2,1)}, bf16[96,768]{1,0:T(8,128)(2,1)}, bf16[96,768]{1,0:T(8,128)(2,1)}) custom-call(s32[2]{0:T(128)} %pad_add_fusion.1.where_ref, f32[288,768]{1,0:T(8,128)} %reshape.166.rows_ref, f32[16,768]{1,0:T(8,128)} %pad.9.tail_ref, bf16[768,768]{1,0:T(8,128)(2,1)} %get-tuple-element.60.heads_ref.refs_4_, ...), custom_call_target="tpu_custom_call" | custom-call | tf_op jit(solution)/shard_map/pallas_call | solution.py:818
  16.9 3.9 %collective-permute-start.5 = (bf16[96,768]{1,0:T(8,128)(2,1)}, bf16[96,768]{1,0:T(8,128)(2,1)S(1)}, u32[]{:S(2)}, u32[]{:S(2)}) collective-permute-start(bf16[96,768]{1,0:T(8,128)(2,1)} %get-tuple-element.30), channel_id=1, source_target_pairs={{0,16},{2,18},{4,20},{6,22},{8,24},{10,26},{12,28},{14,30},{16,0},... | collective-permute-start | bytes 442376 | tf_op jit(solution)/shard_map/ppermute | solution.py:848
  22.4 3.5 %collective-permute-done.4.b_ref = bf16[96,768]{1,0:T(8,128)(2,1)S(1)} collective-permute-done((bf16[96,768]{1,0:T(8,128)(2,1)}, bf16[96,768]{1,0:T(8,128)(2,1)S(1)}, u32[]{:S(2)}, u32[]{:S(2)}) %collective-permute-start.4) | collective-permute-done | bytes 147488 | tf_op jit(solution)/shard_map/ppermute | solution.py:848
  26.0 7.1 %collective-permute-done.6.d_ref = bf16[96,768]{1,0:T(8,128)(2,1)S(1)} collective-permute-done((bf16[96,768]{1,0:T(8,128)(2,1)}, bf16[96,768]{1,0:T(8,128)(2,1)S(1)}, u32[]{:S(2)}, u32[]{:S(2)}) %collective-permute-start.6) | collective-permute-done | bytes 147488 | tf_op jit(solution)/shard_map/ppermute | solution.py:848
  33.7 2.0 %shard_map.110.refs_4_ = bf16[352,768]{1,0:T(8,128)(2,1)} custom-call(s32[2]{0:T(128)} %pad_add_fusion.1.where_ref, bf16[96,768]{1,0:T(8,128)(2,1)} %get-tuple-element.28.a_ref, bf16[96,768]{1,0:T(8,128)(2,1)} %copy-done.24, bf16[96,768]{1,0:T(8,128)(2,1)} %copy-done.25, bf16[96,768]{1,0:T(8,128)(2,1)} %copy-done.26), custom_call_target="tpu_custom_call" | custom-call | tf_op jit(solution)/shard_map/pallas_call | solution.py:818
  35.7 2.9 %collective-permute-start.9 = (bf16[352,768]{1,0:T(8,128)(2,1)}, bf16[352,768]{1,0:T(8,128)(2,1)S(1)}, u32[]{:S(2)}, u32[]{:S(2)}) collective-permute-start(bf16[352,768]{1,0:T(8,128)(2,1)} %shard_map.110.refs_4_), channel_id=1, source_target_pairs={{0,6},{2,4},{4,2},{6,0},{8,14},{10,12},{12,10},{14,8},{16,22},{18,... | collective-permute-start | bytes 1622024 | tf_op jit(solution)/shard_map/ppermute | solution.py:851
  39.5 4.9 %collective-permute-start.1 = (bf16[272,768]{1,0:T(8,128)(2,1)S(1)}, bf16[272,768]{1,0:T(8,128)(2,1)S(1)}, u32[]{:S(2)}, u32[]{:S(2)}) collective-permute-start(bf16[272,768]{1,0:T(8,128)(2,1)S(1)} %fusion.6.refs_0_), channel_id=1, source_target_pairs={{0,16},{2,18},{4,20},{6,22},{8,24},{10,26},{12,28},{14,30},{16,0},... | collective-permute-start | bytes 1253384 | tf_op jit(solution)/shard_map/ppermute | solution.py:848
  44.4 18.1 %collective-permute-done.1.refs_2_ = bf16[272,768]{1,0:T(8,128)(2,1)S(1)} collective-permute-done((bf16[272,768]{1,0:T(8,128)(2,1)S(1)}, bf16[272,768]{1,0:T(8,128)(2,1)S(1)}, u32[]{:S(2)}, u32[]{:S(2)}) %collective-permute-start.1) | collective-permute-done | bytes 417824 | tf_op jit(solution)/shard_map/ppermute | solution.py:848
  63.7 3.7 %collective-permute-start.2 = (bf16[272,768]{1,0:T(8,128)(2,1)S(1)}, bf16[272,768]{1,0:T(8,128)(2,1)S(1)}, u32[]{:S(2)}, u32[]{:S(2)}) collective-permute-start(bf16[272,768]{1,0:T(8,128)(2,1)S(1)} %collective-permute-done.1.refs_2_), channel_id=1, source_target_pairs={{0,8},{2,10},{4,12},{6,14},{8,0},{10,2},{12,4},{14,6},{16,24},{18,... | collective-permute-start | bytes 1253384 | tf_op jit(solution)/shard_map/ppermute | solution.py:848
  68.0 9.6 %collective-permute-done.2.refs_3_ = bf16[272,768]{1,0:T(8,128)(2,1)S(1)} collective-permute-done((bf16[272,768]{1,0:T(8,128)(2,1)S(1)}, bf16[272,768]{1,0:T(8,128)(2,1)S(1)}, u32[]{:S(2)}, u32[]{:S(2)}) %collective-permute-start.2) | collective-permute-done | bytes 417824 | tf_op jit(solution)/shard_map/ppermute | solution.py:848
  79.4 20.0 %shard_map.111 = (bf16[352,768]{1,0:T(8,128)(2,1)}, bf16[352,768]{1,0:T(8,128)(2,1)}, bf16[352,768]{1,0:T(8,128)(2,1)}, bf16[352,768]{1,0:T(8,128)(2,1)}, bf16[3...) custom-call(s32[3]{0:T(128)} %pad_add_fusion.where_ref, ...), custom_call_target="tpu_custom_call" | custom-call | tf_op jit(solution)/shard_map/pallas_call | solution.py:818
  99.4 1.8 %collective-permute-start.15 = (bf16[256,768]{1,0:T(8,128)(2,1)}, bf16[256,768]{1,0:T(8,128)(2,1)}, u32[]{:S(2)}, u32[]{:S(2)}) collective-permute-start(bf16[256,768]{1,0:T(8,128)(2,1)} %get-tuple-element.35), channel_id=1, source_target_pairs={{0,8},{2,10},{4,12},{6,14},{8,0},{10,2},{12,4},{14,6},{16,24},{18,... | collective-permute-start | bytes 1179656 | tf_op jit(solution)/shard_map/ppermute | solution.py:848
  102.0 9.8 %collective-permute-done.15 = bf16[256,768]{1,0:T(8,128)(2,1)} collective-permute-done((bf16[256,768]{1,0:T(8,128)(2,1)}, bf16[256,768]{1,0:T(8,128)(2,1)}, u32[]{:S(2)}, u32[]{:S(2)}) %collective-permute-start.15) | collective-permute-done | bytes 393248 | tf_op jit(solution)/shard_map/ppermute | solution.py:848
  113.0 2.4 %collective-permute-start.16 = (bf16[256,768]{1,0:T(8,128)(2,1)S(1)}, bf16[256,768]{1,0:T(8,128)(2,1)S(1)}, u32[]{:S(2)}, u32[]{:S(2)}) collective-permute-start(bf16[256,768]{1,0:T(8,128)(2,1)S(1)} %add_convert_fusion.4), channel_id=1, source_target_pairs={{0,16},{2,18},{4,20},{6,22},{8,24},{10,26},{12,28},{14,30},{16,0},... | collective-permute-start | bytes 1179656 | tf_op jit(solution)/shard_map/ppermute | solution.py:848
  122.2 11.8 %collective-permute-done.16 = bf16[256,768]{1,0:T(8,128)(2,1)S(1)} collective-permute-done((bf16[256,768]{1,0:T(8,128)(2,1)S(1)}, bf16[256,768]{1,0:T(8,128)(2,1)S(1)}, u32[]{:S(2)}, u32[]{:S(2)}) %collective-permute-start.16) | collective-permute-done | bytes 393248 | tf_op jit(solution)/shard_map/ppermute | solution.py:848
  134.4 8.0 %collective-permute-done.21.c_ref = bf16[352,768]{1,0:T(8,128)(2,1)S(1)} collective-permute-done((bf16[352,768]{1,0:T(8,128)(2,1)S(1)}, bf16[352,768]{1,0:T(8,128)(2,1)S(1)}, u32[]{:S(2)}, u32[]{:S(2)}) %collective-permute-start.21) | collective-permute-done | bytes 540704 | tf_op jit(solution)/shard_map/ppermute | solution.py:851
  143.2 2.8 %shard_map.112 = (bf16[96,768]{1,0:T(8,128)(2,1)}, bf16[96,768]{1,0:T(8,128)(2,1)}, bf16[96,768]{1,0:T(8,128)(2,1)}, bf16[96,768]{1,0:T(8,128)(2,1)}) custom-call(s32[2]{0:T(128)} %pad_add_fusion.1.where_ref, bf16[352,768]{1,0:T(8,128)(2,1)} %add_convert_fusion.3.a_ref, bf16[352,768]{1,0:T(8,128)(2,1)} %copy-done.15, bf16[352,768]{1,0:T(8,128)(2,1)} %copy-done.16, ...), custom_call_target="tpu_custom_call" | custom-call | tf_op jit(solution)/shard_map/pallas_call | solution.py:818
  146.3 2.4 %collective-permute-start.25 = (bf16[96,768]{1,0:T(8,128)(2,1)}, bf16[96,768]{1,0:T(8,128)(2,1)S(1)}, u32[]{:S(2)}, u32[]{:S(2)}) collective-permute-start(bf16[96,768]{1,0:T(8,128)(2,1)} %get-tuple-element.46), channel_id=1, source_target_pairs={{0,16},{2,18},{4,20},{6,22},{8,24},{10,26},{12,28},{14,30},{16,0},... | collective-permute-start | bytes 442376 | tf_op jit(solution)/shard_map/ppermute | solution.py:848
  148.7 1.7 collective-permute-start.26
  150.4 2.8 %collective-permute-done.24.refs_1_ = bf16[96,768]{1,0:T(8,128)(2,1)S(1)} collective-permute-done((bf16[96,768]{1,0:T(8,128)(2,1)}, bf16[96,768]{1,0:T(8,128)(2,1)S(1)}, u32[]{:S(2)}, u32[]{:S(2)}) %collective-permute-start.24) | collective-permute-done | bytes 147488 | tf_op jit(solution)/shard_map/ppermute | solution.py:848
  153.2 5.7 %collective-permute-done.25.refs_2_ = bf16[96,768]{1,0:T(8,128)(2,1)S(1)} collective-permute-done((bf16[96,768]{1,0:T(8,128)(2,1)}, bf16[96,768]{1,0:T(8,128)(2,1)S(1)}, u32[]{:S(2)}, u32[]{:S(2)}) %collective-permute-start.25) | collective-permute-done | bytes 147488 | tf_op jit(solution)/shard_map/ppermute | solution.py:848
  159.6 7.6 %shard_map.113 = (f32[288,768]{1,0:T(8,128)}, f32[16,768]{1,0:T(8,128)}) custom-call(s32[2]{0:T(128)} %pad_add_fusion.1.where_ref, bf16[96,768]{1,0:T(8,128)(2,1)} %get-tuple-element.44.refs_0_, bf16[96,768]{1,0:T(8,128)(2,1)} %copy-done.21, bf16[96,768]{1,0:T(8,128)(2,1)} %copy-done.22, bf16[96,768]{1,0:T(8,128)(2,1)} %copy-done.23, ...), custom_call_target="tpu_custom_call" | custom-call | tf_op jit(solution)/shard_map/pallas_call | solution.py:818
  170.3 4.4 %multiply_subtract_fusion = (f32[221496]{0:T(1024)}, f32[221496]{0:T(1024)}, f32[221496]{0:T(1024)}, f32[221496]{0:T(1024)}) fusion(f32[221496]{0:T(1024)S(1)} %copy-done.1, f32[221496]{0:T(1024)} %param.10, f32[221496]{0:T(1024)} %param.11, s32[]{:T(128)S(6)} %select_n.164, f32[9984]{0:T(1024)S(1)} %broadcast_select_fusion, f32[221184]{0:T(1024)S(1)} %reshape.170), kind=kLoop, calls=%fused_computation.15 | loop fusion | flops 3543936 | bytes 7126564 | tf_op jit(solution)/shard_map/sub | solution.py:271
  (133 shorter events, 28.7 us)
Async XLA Ops:
  1.5 8.1 %collective-permute-start.3 = (f32[9984]{0:T(1024)S(1)}, f32[9984]{0:T(1024)S(1)}, u32[]{:S(2)}, u32[]{:S(2)}) collective-permute-start(f32[9984]{0:T(1024)S(1)} %slice.18), channel_id=1, source_target_pairs={{0,1},{1,2},{2,3},{3,4},{4,5},{5,6},{6,7},{7,8},{8,9},{9,10},{10,1... | collective-permute-start | bytes 119816 | tf_op jit(solution)/shard_map/ppermute | solution.py:284
  16.9 9.0 %collective-permute-start.4 = (bf16[96,768]{1,0:T(8,128)(2,1)}, bf16[96,768]{1,0:T(8,128)(2,1)S(1)}, u32[]{:S(2)}, u32[]{:S(2)}) collective-permute-start(bf16[96,768]{1,0:T(8,128)(2,1)} %get-tuple-element.29), channel_id=1, source_target_pairs={{0,8},{2,10},{4,12},{6,14},{8,0},{10,2},{12,4},{14,6},{16,24},{18,... | collective-permute-start | bytes 442376 | tf_op jit(solution)/shard_map/ppermute | solution.py:848
  16.9 9.0 %collective-permute-start.5 = (bf16[96,768]{1,0:T(8,128)(2,1)}, bf16[96,768]{1,0:T(8,128)(2,1)S(1)}, u32[]{:S(2)}, u32[]{:S(2)}) collective-permute-start(bf16[96,768]{1,0:T(8,128)(2,1)} %get-tuple-element.30), channel_id=1, source_target_pairs={{0,16},{2,18},{4,20},{6,22},{8,24},{10,26},{12,28},{14,30},{16,0},... | collective-permute-start | bytes 442376 | tf_op jit(solution)/shard_map/ppermute | solution.py:848
  20.8 12.2 %collective-permute-start.6 = (bf16[96,768]{1,0:T(8,128)(2,1)}, bf16[96,768]{1,0:T(8,128)(2,1)S(1)}, u32[]{:S(2)}, u32[]{:S(2)}) collective-permute-start(bf16[96,768]{1,0:T(8,128)(2,1)} %get-tuple-element.31), channel_id=1, source_target_pairs={{0,24},{2,26},{4,28},{6,30},{8,16},{10,18},{12,20},{14,22},{16,8},... | collective-permute-start | bytes 442376 | tf_op jit(solution)/shard_map/ppermute | solution.py:848
  35.7 26.9 %collective-permute-start.9 = (bf16[352,768]{1,0:T(8,128)(2,1)}, bf16[352,768]{1,0:T(8,128)(2,1)S(1)}, u32[]{:S(2)}, u32[]{:S(2)}) collective-permute-start(bf16[352,768]{1,0:T(8,128)(2,1)} %shard_map.110.refs_4_), channel_id=1, source_target_pairs={{0,6},{2,4},{4,2},{6,0},{8,14},{10,12},{12,10},{14,8},{16,22},{18,... | collective-permute-start | bytes 1622024 | tf_op jit(solution)/shard_map/ppermute | solution.py:851
  38.6 24.5 %collective-permute-start.8 = (bf16[352,768]{1,0:T(8,128)(2,1)}, bf16[352,768]{1,0:T(8,128)(2,1)S(1)}, u32[]{:S(2)}, u32[]{:S(2)}) collective-permute-start(bf16[352,768]{1,0:T(8,128)(2,1)} %shard_map.110.refs_4_), channel_id=1, source_target_pairs={{0,4},{2,6},{4,0},{6,2},{8,12},{10,14},{12,8},{14,10},{16,20},{18,... | collective-permute-start | bytes 1622024 | tf_op jit(solution)/shard_map/ppermute | solution.py:851
  38.6 25.0 %collective-permute-start.7 = (bf16[352,768]{1,0:T(8,128)(2,1)}, bf16[352,768]{1,0:T(8,128)(2,1)S(1)}, u32[]{:S(2)}, u32[]{:S(2)}) collective-permute-start(bf16[352,768]{1,0:T(8,128)(2,1)} %shard_map.110.refs_4_), channel_id=1, source_target_pairs={{0,2},{2,0},{4,6},{6,4},{8,10},{10,8},{12,14},{14,12},{16,18},{18,... | collective-permute-start | bytes 1622024 | tf_op jit(solution)/shard_map/ppermute | solution.py:851
  39.5 23.0 %collective-permute-start.1 = (bf16[272,768]{1,0:T(8,128)(2,1)S(1)}, bf16[272,768]{1,0:T(8,128)(2,1)S(1)}, u32[]{:S(2)}, u32[]{:S(2)}) collective-permute-start(bf16[272,768]{1,0:T(8,128)(2,1)S(1)} %fusion.6.refs_0_), channel_id=1, source_target_pairs={{0,16},{2,18},{4,20},{6,22},{8,24},{10,26},{12,28},{14,30},{16,0},... | collective-permute-start | bytes 1253384 | tf_op jit(solution)/shard_map/ppermute | solution.py:848
  44.4 19.3 %collective-permute-start = (bf16[272,768]{1,0:T(8,128)(2,1)S(1)}, bf16[272,768]{1,0:T(8,128)(2,1)S(1)}, u32[]{:S(2)}, u32[]{:S(2)}) collective-permute-start(bf16[272,768]{1,0:T(8,128)(2,1)S(1)} %fusion.6.refs_0_), channel_id=1, source_target_pairs={{0,8},{2,10},{4,12},{6,14},{8,0},{10,2},{12,4},{14,6},{16,24},{18,... | collective-permute-start | bytes 1253384 | tf_op jit(solution)/shard_map/ppermute | solution.py:848
  62.5 15.0 %collective-permute-start.13 = (bf16[352,768]{1,0:T(8,128)(2,1)S(1)}, bf16[352,768]{1,0:T(8,128)(2,1)S(1)}, u32[]{:S(2)}, u32[]{:S(2)}) collective-permute-start(bf16[352,768]{1,0:T(8,128)(2,1)S(1)} %collective-permute-done.9.refs_7_), channel_id=1, source_target_pairs={{0,1},{1,0},{2,3},{3,2},{4,5},{5,4},{6,7},{7,6},{8,9},{9,8},{10,11... | collective-permute-start | bytes 1622024 | tf_op jit(solution)/shard_map/ppermute | solution.py:854
  63.0 14.6 %collective-permute-start.12 = (bf16[352,768]{1,0:T(8,128)(2,1)S(1)}, bf16[352,768]{1,0:T(8,128)(2,1)S(1)}, u32[]{:S(2)}, u32[]{:S(2)}) collective-permute-start(bf16[352,768]{1,0:T(8,128)(2,1)S(1)} %collective-permute-done.8.refs_6_), channel_id=1, source_target_pairs={{0,1},{1,0},{2,3},{3,2},{4,5},{5,4},{6,7},{7,6},{8,9},{9,8},{10,11... | collective-permute-start | bytes 1622024 | tf_op jit(solution)/shard_map/ppermute | solution.py:854
  63.7 15.7 %collective-permute-start.11 = (bf16[352,768]{1,0:T(8,128)(2,1)S(1)}, bf16[352,768]{1,0:T(8,128)(2,1)}, u32[]{:S(2)}, u32[]{:S(2)}) collective-permute-start(bf16[352,768]{1,0:T(8,128)(2,1)S(1)} %collective-permute-done.7.refs_5_), channel_id=1, source_target_pairs={{0,1},{1,0},{2,3},{3,2},{4,5},{5,4},{6,7},{7,6},{8,9},{9,8},{10,11... | collective-permute-start | bytes 1622024 | tf_op jit(solution)/shard_map/ppermute | solution.py:854
  63.7 13.9 %collective-permute-start.2 = (bf16[272,768]{1,0:T(8,128)(2,1)S(1)}, bf16[272,768]{1,0:T(8,128)(2,1)S(1)}, u32[]{:S(2)}, u32[]{:S(2)}) collective-permute-start(bf16[272,768]{1,0:T(8,128)(2,1)S(1)} %collective-permute-done.1.refs_2_), channel_id=1, source_target_pairs={{0,8},{2,10},{4,12},{6,14},{8,0},{10,2},{12,4},{14,6},{16,24},{18,... | collective-permute-start | bytes 1253384 | tf_op jit(solution)/shard_map/ppermute | solution.py:848
  99.4 12.4 %collective-permute-start.15 = (bf16[256,768]{1,0:T(8,128)(2,1)}, bf16[256,768]{1,0:T(8,128)(2,1)}, u32[]{:S(2)}, u32[]{:S(2)}) collective-permute-start(bf16[256,768]{1,0:T(8,128)(2,1)} %get-tuple-element.35), channel_id=1, source_target_pairs={{0,8},{2,10},{4,12},{6,14},{8,0},{10,2},{12,4},{14,6},{16,24},{18,... | collective-permute-start | bytes 1179656 | tf_op jit(solution)/shard_map/ppermute | solution.py:848
  101.2 11.8 %collective-permute-start.18 = (bf16[352,768]{1,0:T(8,128)(2,1)}, bf16[352,768]{1,0:T(8,128)(2,1)S(1)}, u32[]{:S(2)}, u32[]{:S(2)}) collective-permute-start(bf16[352,768]{1,0:T(8,128)(2,1)} %get-tuple-element.39), channel_id=1, source_target_pairs={{0,1},{1,0},{2,3},{3,2},{4,5},{5,4},{6,7},{7,6},{8,9},{9,8},{10,11... | collective-permute-start | bytes 1622024 | tf_op jit(solution)/shard_map/ppermute | solution.py:854
  101.2 14.4 %collective-permute-start.20 = (bf16[352,768]{1,0:T(8,128)(2,1)}, bf16[352,768]{1,0:T(8,128)(2,1)S(1)}, u32[]{:S(2)}, u32[]{:S(2)}) collective-permute-start(bf16[352,768]{1,0:T(8,128)(2,1)} %get-tuple-element.41), channel_id=1, source_target_pairs={{0,1},{1,0},{2,3},{3,2},{4,5},{5,4},{6,7},{7,6},{8,9},{9,8},{10,11... | collective-permute-start | bytes 1622024 | tf_op jit(solution)/shard_map/ppermute | solution.py:854
  101.7 20.4 %collective-permute-start.14 = (bf16[256,768]{1,0:T(8,128)(2,1)}, bf16[256,768]{1,0:T(8,128)(2,1)S(1)}, u32[]{:S(2)}, u32[]{:S(2)}) collective-permute-start(bf16[256,768]{1,0:T(8,128)(2,1)} %get-tuple-element.33), channel_id=1, source_target_pairs={{0,8},{2,10},{4,12},{6,14},{8,0},{10,2},{12,4},{14,6},{16,24},{18,... | collective-permute-start | bytes 1179656 | tf_op jit(solution)/shard_map/ppermute | solution.py:848
  102.0 16.2 %collective-permute-start.17 = (bf16[352,768]{1,0:T(8,128)(2,1)}, bf16[352,768]{1,0:T(8,128)(2,1)S(1)}, u32[]{:S(2)}, u32[]{:S(2)}) collective-permute-start(bf16[352,768]{1,0:T(8,128)(2,1)} %get-tuple-element.37), channel_id=1, source_target_pairs={{0,1},{1,0},{2,3},{3,2},{4,5},{5,4},{6,7},{7,6},{8,9},{9,8},{10,11... | collective-permute-start | bytes 1622024 | tf_op jit(solution)/shard_map/ppermute | solution.py:854
  113.0 21.0 %collective-permute-start.16 = (bf16[256,768]{1,0:T(8,128)(2,1)S(1)}, bf16[256,768]{1,0:T(8,128)(2,1)S(1)}, u32[]{:S(2)}, u32[]{:S(2)}) collective-permute-start(bf16[256,768]{1,0:T(8,128)(2,1)S(1)} %add_convert_fusion.4), channel_id=1, source_target_pairs={{0,16},{2,18},{4,20},{6,22},{8,24},{10,26},{12,28},{14,30},{16,0},... | collective-permute-start | bytes 1179656 | tf_op jit(solution)/shard_map/ppermute | solution.py:848
  115.6 18.7 %collective-permute-start.19 = (bf16[352,768]{1,0:T(8,128)(2,1)S(1)}, bf16[352,768]{1,0:T(8,128)(2,1)S(1)}, u32[]{:S(2)}, u32[]{:S(2)}) collective-permute-start(bf16[352,768]{1,0:T(8,128)(2,1)S(1)} %add_convert_fusion.2), channel_id=1, source_target_pairs={{0,2},{2,0},{4,6},{6,4},{8,10},{10,8},{12,14},{14,12},{16,18},{18,... | collective-permute-start | bytes 1622024 | tf_op jit(solution)/shard_map/ppermute | solution.py:851
  116.6 25.8 %collective-permute-start.21 = (bf16[352,768]{1,0:T(8,128)(2,1)S(1)}, bf16[352,768]{1,0:T(8,128)(2,1)S(1)}, u32[]{:S(2)}, u32[]{:S(2)}) collective-permute-start(bf16[352,768]{1,0:T(8,128)(2,1)S(1)} %add_convert_fusion.1), channel_id=1, source_target_pairs={{0,4},{2,6},{4,0},{6,2},{8,12},{10,14},{12,8},{14,10},{16,20},{18,... | collective-permute-start | bytes 1622024 | tf_op jit(solution)/shard_map/ppermute | solution.py:851
  118.2 25.0 %collective-permute-start.23 = (bf16[352,768]{1,0:T(8,128)(2,1)S(1)}, bf16[352,768]{1,0:T(8,128)(2,1)}, u32[]{:S(2)}, u32[]{:S(2)}) collective-permute-start(bf16[352,768]{1,0:T(8,128)(2,1)S(1)} %add_convert_fusion), channel_id=1, source_target_pairs={{0,6},{2,4},{4,2},{6,0},{8,14},{10,12},{12,10},{14,8},{16,22},{18,... | collective-permute-start | bytes 1622024 | tf_op jit(solution)/shard_map/ppermute | solution.py:851
  146.3 12.6 %collective-permute-start.25 = (bf16[96,768]{1,0:T(8,128)(2,1)}, bf16[96,768]{1,0:T(8,128)(2,1)S(1)}, u32[]{:S(2)}, u32[]{:S(2)}) collective-permute-start(bf16[96,768]{1,0:T(8,128)(2,1)} %get-tuple-element.46), channel_id=1, source_target_pairs={{0,16},{2,18},{4,20},{6,22},{8,24},{10,26},{12,28},{14,30},{16,0},... | collective-permute-start | bytes 442376 | tf_op jit(solution)/shard_map/ppermute | solution.py:848
  148.7 10.2 %collective-permute-start.26 = (bf16[96,768]{1,0:T(8,128)(2,1)}, bf16[96,768]{1,0:T(8,128)(2,1)S(1)}, u32[]{:S(2)}, u32[]{:S(2)}) collective-permute-start(bf16[96,768]{1,0:T(8,128)(2,1)} %get-tuple-element.47), channel_id=1, source_target_pairs={{0,24},{2,26},{4,28},{6,30},{8,16},{10,18},{12,20},{14,22},{16,8},... | collective-permute-start | bytes 442376 | tf_op jit(solution)/shard_map/ppermute | solution.py:848
  (33 other events, 252.5 us)

commit v4 on v3

--- a/solution.py
+++ b/solution.py
@@ -355,73 +355,76 @@
 def spread_groups(parts, first):
     total = None
     for group, part in enumerate(parts):
-        moved = jnp.where(group_mask(group), turned(part, PART * (group - first)), 0.0)
-        total = moved if total is None else total + moved
+        moved = turned(part, PART * (group - first))
+        total = moved if total is None else jnp.where(group_mask(group), moved, total)
+    if len(parts) < PLANES:
+        total = jnp.where(lanes_of(D) < PART * len(parts), total, 0.0)
     return total
 
 
-def every(size, stride, first):
-    row = lax.broadcasted_iota(jnp.int32, (size, SPOT), 0)
-    col = lax.broadcasted_iota(jnp.int32, (size, SPOT), 1)
-    return jnp.where(col == stride * row + first, 1.0, 0.0).astype(BF)
-
-
-def permutations():
-    place = jnp.arange(D)
-    part, inner = place // PART, place % PART
-    hidden_from = SPOT * (inner // 24) + 24 * part + inner % 24
-    kind = inner // HEAD_DIM
-    head = jnp.where(
-        part < 3,
-        part + jnp.where(kind == 0, 0, jnp.where(kind == 1, 5, 9)),
-        jnp.where(kind == 0, 3, jnp.where(kind == 1, 4, 8)),
-    )
-    head_from = HEAD_DIM * head + inner % HEAD_DIM
-    rows = place[:, None]
-    return (
-        (rows == head_from[None]).astype(BF),
-        (rows == hidden_from[None]).astype(BF),
-    )
-
-
-def pack_kernel(where_ref, rows_ref, tail_ref, heads_ref, hidden_ref, *outs):
-    out_refs, spot = outs[:PLANES], outs[PLANES]
+def count_of(value, *limits):
+    return sum(jnp.where(value >= limit, 1, 0) for limit in limits)
+
+
+def pick_matrix(kinds, size):
+    row = lax.broadcasted_iota(jnp.int32, (SPOT, SPOT), 0)
+    col = lax.broadcasted_iota(jnp.int32, (SPOT, SPOT), 1)
+    kind = count_of(row, *range(size, SPOT, size))
+    return jnp.where(col == kinds * (row - size * kind) + kind, 1.0, 0.0).astype(BF)
+
+
+def order_columns(perm_ref, by_head):
+    place = lax.broadcasted_iota(jnp.int32, (8, D), 1)
+    part = count_of(place, PART, 2 * PART, 3 * PART)
+    inner = place - PART * part
+    if by_head:
+        kind = count_of(inner, HEAD_DIM, 2 * HEAD_DIM)
+        early = part + jnp.where(kind == 0, 0, jnp.where(kind == 1, 5, 9))
+        late = jnp.where(kind == 0, 3, jnp.where(kind == 1, 4, 8))
+        source = HEAD_DIM * (jnp.where(part < 3, early, late) - kind) + inner
+    else:
+        run = count_of(inner, *range(24, PART, 24))
+        source = (SPOT - 24) * run + 24 * part + inner
+    row = lax.broadcasted_iota(jnp.int32, (D, D), 0)
+    perm_ref[...] = jnp.where(row == source[0:1], 1.0, 0.0).astype(BF)
+
+
+def pack_kernel(where_ref, rows_ref, tail_ref, *refs):
+    out_refs, (spot, perm, mixed) = refs[:PLANES], refs[PLANES:]
     plane, place = where_ref[0], where_ref[1]
     device = 8 * plane + place
+    with_heads = device < 8
+    with_hidden = (device >= 10) & (device < 22)
     spot[...] = jnp.zeros_like(spot)
+    pl.when(with_heads)(lambda: order_columns(perm, True))
+    pl.when(with_hidden)(lambda: order_columns(perm, False))
+
+    @pl.when(with_heads | with_hidden)
+    def _():
+        mixed[...] = dot_nn(rows_ref[...].astype(BF), perm[...]).astype(BF)
+
+    @pl.when(with_heads)
+    def _():
+        sort = pick_matrix(3, 32)
+        for i in range(3):
+            picked = dot_nn(sort, mixed[SPOT * i : SPOT * i + SPOT, :])
+            for j in range(3):
+                parts = [picked[32 * j + 8 * g : 32 * j + 8 * g + 8] for g in range(4)]
+                for s in range(PLANES):
+                    spot[s, 24 * i + 8 * j : 24 * i + 8 * j + 8, :] = spread_groups(parts, s)
+
     for i in range(3):
         block = 3 * device + i
 
-        @pl.when(block < 24)
-        def _():
-            for j in range(3):
-                picked = dot_nn(every(32, 3, j), rows_ref[SPOT * i : SPOT * i + SPOT, :].astype(BF))
-                sorted_ = dot_nn(picked.astype(BF), heads_ref[...])
-                parts = [sorted_[8 * g : 8 * g + 8] for g in range(4)]
-                for s in range(PLANES):
-                    spot[s, 24 * i + 8 * j : 24 * i + 8 * j + 8, :] = spread_groups(parts, s)
-
         @pl.when((block >= 32) & (block < 64))
         def _():
-            source = rows_ref[SPOT * i : SPOT * i + SPOT, :].astype(BF)
-            parts = [
-                dot_nn(dot_nn(every(24, 4, j), source).astype(BF), hidden_ref[...])
-                for j in range(4)
-            ]
+            picked = dot_nn(pick_matrix(4, 24), mixed[SPOT * i : SPOT * i + SPOT, :])
+            parts = [picked[24 * j : 24 * j + 24] for j in range(4)]
+            start = 24 * i
+            if i == 2:
+                start = pl.multiple_of(jnp.where(block == 32, 0, 48), 8)
             for s in range(PLANES):
-                value = spread_groups(parts, s)
-                if i < 2:
-                    spot[s, 24 * i : 24 * i + 24, :] = value
-                else:
-                    mixed = block == 32
-
-                    @pl.when(mixed)
-                    def _():
-                        spot[s, 0:24, :] = value
-
-                    @pl.when(jnp.logical_not(mixed))
-                    def _():
-                        spot[s, 48:72, :] = value
+                spot[s, pl.ds(start, 24), :] = spread_groups(parts, s)
 
         @pl.when(block >= 64)
         def _():
@@ -451,8 +454,10 @@
     @pl.when(device == 31)
     def _():
         upper = tail_ref[0:8, :].astype(BF)
-        by_head = dot_nn(upper, heads_ref[...])
-        by_hidden = dot_nn(upper, hidden_ref[...])
+        order_columns(perm, True)
+        by_head = dot_nn(upper, perm[...])
+        order_columns(perm, False)
+        by_hidden = dot_nn(upper, perm[...])
         for s in range(PLANES):
             spot[s, 72:73, :] = spread_groups([by_hidden[4 + j : 5 + j] for j in range(4)], s)
             spot[s, 73:74, :] = spread_groups([by_head[j : j + 1] for j in range(3)], s)
@@ -464,25 +469,34 @@
 
 
 def unpack_kernel(where_ref, *refs):
-    in_refs, (heads_ref, hidden_ref, rows_ref, tail_ref, spot) = refs[:PLANES], refs[PLANES:]
+    in_refs, (rows_ref, tail_ref, spot, perm, mixed) = refs[:PLANES], refs[PLANES:]
     plane, place = where_ref[0], where_ref[1]
     device = 8 * plane + place
+    with_heads = device < 8
+    with_hidden = (device >= 10) & (device < 22)
     for r in range(PLANES):
         spot[plane ^ r] = in_refs[r][...].astype(F32)
-    for i in range(3):
-        block = 3 * device + i
-
-        @pl.when(block < 24)
-        def _():
-            total = None
+    pl.when(with_heads)(lambda: order_columns(perm, True))
+
+    @pl.when(with_heads)
+    def _():
+        sort = pick_matrix(3, 32)
+        for i in range(3):
+            sorted_ = []
             for j in range(3):
                 base = 24 * i + 8 * j
                 parts = [spot[s, base : base + 8, :] for s in range(PLANES)]
-                sorted_ = jnp.concatenate([spread_groups(parts, g) for g in range(4)], axis=0)
-                picked = dot_nt(sorted_.astype(BF), heads_ref[...]).astype(BF)
-                value = dot_tn(every(32, 3, j), picked)
-                total = value if total is None else total + value
-            rows_ref[SPOT * i : SPOT * i + SPOT, :] = total
+                sorted_.extend(spread_groups(parts, g) for g in range(4))
+            block_rows = jnp.concatenate(sorted_, axis=0).astype(BF)
+            mixed[SPOT * i : SPOT * i + SPOT, :] = dot_tn(sort, block_rows).astype(BF)
+
+    @pl.when(with_hidden)
+    def _():
+        order_columns(perm, False)
+        mixed[...] = jnp.zeros_like(mixed)
+
+    for i in range(3):
+        block = 3 * device + i
 
         @pl.when((block >= 32) & (block < 64))
         def _():
@@ -490,14 +504,18 @@
             if i == 2:
                 start = pl.multiple_of(jnp.where(block == 32, 0, 48), 8)
             parts = [spot[s, pl.ds(start, 24), :] for s in range(PLANES)]
-            total = None
-            for j in range(4):
-                picked = dot_nt(spread_groups(parts, j).astype(BF), hidden_ref[...]).astype(BF)
-                value = dot_tn(every(24, 4, j), picked)
-                total = value if total is None else total + value
-            rows_ref[SPOT * i : SPOT * i + SPOT, :] = total
-
-        @pl.when(block >= 64)
+            block_rows = jnp.concatenate([spread_groups(parts, j) for j in range(4)], axis=0)
+            mixed[SPOT * i : SPOT * i + SPOT, :] = dot_tn(
+                pick_matrix(4, 24), block_rows.astype(BF)
+            ).astype(BF)
+
+    @pl.when(with_heads | with_hidden)
+    def _():
+        rows_ref[...] = dot_nt(mixed[...], perm[...])
+
+    for i in range(3):
+
+        @pl.when(3 * device + i >= 64)
         def _():
             for s in range(PLANES):
                 rows_ref[SPOT * i + 24 * s : SPOT * i + 24 * s + 24, :] = spot[
@@ -526,14 +544,16 @@
 
     @pl.when(device == 31)
     def _():
+        order_columns(perm, False)
         whole = [spot[s, 72:73, :] for s in range(PLANES)]
         for j in range(4):
             row = jnp.broadcast_to(spread_groups(whole, j), (8, D)).astype(BF)
-            tail_ref[4 + j : 5 + j, :] = dot_nt(row, hidden_ref[...])[0:1]
+            tail_ref[4 + j : 5 + j, :] = dot_nt(row, perm[...])[0:1]
+        order_columns(perm, True)
         whole = [spot[s, 73:74, :] for s in range(PLANES)]
         for j in range(3):
             row = jnp.broadcast_to(spread_groups(whole, j), (8, D)).astype(BF)
-            tail_ref[j : j + 1, :] = dot_nt(row, heads_ref[...])[0:1]
+            tail_ref[j : j + 1, :] = dot_nt(row, perm[...])[0:1]
         tail_ref[3:4, :] = sum(spot[s, 74:75, :] for s in range(PLANES))
         tail_ref[8:16, :] = sum(spot[s, 80:88, :] for s in range(PLANES))
 
@@ -563,10 +583,10 @@
 
 
 def layer_kernel(where_ref, *refs):
-    act_refs, slab_refs = refs[:4], refs[4:12]
-    grad_refs, back_refs = refs[12:20], refs[20:24]
+    act_refs, cot_refs, slab_refs = refs[:4], refs[4:8], refs[8:16]
+    grad_refs, back_refs = refs[16:24], refs[24:28]
     (w_up, w_down, w_out, packed, w_qkv, tails, bf_up, bf_down, bf_out, bf_qkv, normed, grad_y,
-     qkv, attn, g_qkv, g_attn, up, slab) = refs[24:]
+     qkv, attn, g_qkv, g_attn, up, slab) = refs[28:]
     plane, spot, core = where_ref[0], where_ref[1], where_ref[2]
     lane = lanes_of(D)
 
@@ -636,7 +656,7 @@
 
     for r in range(4):
         normed[128 * r : 128 * r + 128, :] = act_refs[r][0:128, :]
-        grad_y[128 * r : 128 * r + 128, :] = act_refs[r][128:256, :]
+        grad_y[128 * r : 128 * r + 128, :] = cot_refs[r][...]
     bias_up = tails[0:1, :]
     flat_bias = tails[1:2, :]
     bias_qkv = jnp.zeros((1, D), F32)
@@ -663,7 +683,7 @@
     low_half = lanes_of(128) < 64
     for r in range(4):
         span = slice(128 * r, 128 * r + 128)
-        seg_row = jnp.broadcast_to(act_refs[r][256:272, 0:128].astype(F32)[0:1], (128, 128))
+        seg_row = jnp.broadcast_to(act_refs[r][128:144, 0:128].astype(F32)[0:1], (128, 128))
         seg_col = jnp.sum(jnp.where(eye, seg_row, 0.0), axis=1, keepdims=True)
         same = (seg_col == seg_row) & same_block
         allowed = same & (cols <= rows) & ((seg_col >= 0.0) | eye)
@@ -863,18 +883,24 @@
     valid = (seg_ids >= 0).astype(F32).reshape(tokens, 1)
     grad_y = out_grad.reshape(tokens, D) * valid
     seg_rows = jnp.pad(seg_ids.reshape(1, tokens).astype(BF), ((0, 15), (0, D - tokens)))
-    sent_acts = jnp.concatenate([normed.astype(BF), grad_y.astype(BF), seg_rows])
+    sent_acts = jnp.concatenate([normed.astype(BF), seg_rows])
     acts = [to_plane(sent_acts, r) for r in range(3)]
     acts.append(to_plane(acts[2], 1))
-
-    heads, hidden = permutations()
+    cots = [to_plane(grad_y.astype(BF), r) for r in range(3)]
+    cots.append(to_plane(cots[2], 1))
+
     rows, tail = rows_from_flat(params, spread, count)
     tail = jnp.pad(tail, ((0, 3), (0, 0)))
     spot_shape = jax.ShapeDtypeStruct((SPOT, D), BF)
     slab_shape = jax.ShapeDtypeStruct((SLAB, D), BF)
+    sort_scratch = [
+        pltpu.VMEM((planes, SPOT, D), F32),
+        pltpu.VMEM((D, D), BF),
+        pltpu.VMEM(rows.shape, BF),
+    ]
     spots = local_call(
-        pack_kernel, [spot_shape] * planes, [pltpu.VMEM((planes, SPOT, D), F32)],
-        where_owner, rows, tail, heads, hidden,
+        pack_kernel, [spot_shape] * planes, sort_scratch,
+        where_owner, rows, tail,
     )
     spots = [to_plane(spots[r], r) for r in range(planes)]
     slab = local_call(slab_kernel, slab_shape, [], where_owner, *spots)
@@ -905,7 +931,7 @@
             pltpu.VMEM((total, D), F32),
             pltpu.VMEM((SLAB, D), F32),
         ],
-        where_spot, *acts, *slabs,
+        where_spot, *acts, *cots, *slabs,
     )
     grads, backs = outs[:8], outs[8:]
     paired = [
@@ -928,8 +954,8 @@
             jax.ShapeDtypeStruct(rows.shape, F32),
             jax.ShapeDtypeStruct((16, D), F32),
         ],
-        [pltpu.VMEM((planes, SPOT, D), F32)],
-        where_owner, *spots, heads, hidden,
+        sort_scratch,
+        where_owner, *spots,
     )
     back = sum(b.astype(F32) for b in backs)
     result = flat_x + back[:tokens]

time: 177 us -> 175 us (0.989)
  Pallas kernels: 38.3 us -> 31.8 us
  waiting for transfers between devices: 79.1 us -> 85.1 us
  other arithmetic: 15.4 us -> 12.1 us
    ppermute x12 -> x15, waiting for transfers between devices: 70 us -> 58.6 us  [to_plane(): return lax.ppermute(value, 'dp', across[r]) if r else value]
    ppermute x6, waiting for transfers between devices: 8.52 us -> 18.8 us  [to_spot(): return lax.ppermute(value, 'dp', within[r]) if r else value]
    ppermute x1, waiting for transfers between devices: 0.55 us -> 7.69 us  [rows_from_flat(): lax.ppermute(tail, AXES, [(i, (i + 1) % count) for i in range(count)])]
    pallas_call x5, Pallas kernels: 38.3 us -> 31.8 us  [local_call(): pl.pallas_call(kernel, out_shape=outs, in_specs=[pl.BlockSpec(memory_spac...]
    ppermute x12 -> x15, starting transfers between devices: 22.8 us -> 25.3 us  [to_plane(): return lax.ppermute(value, 'dp', across[r]) if r else value]
    unnamed x58 -> x60, local copies, waits for them, and re-layouts: 5.16 us -> 5.88 us
  transfers between devices with their start and end apart: 28 -> 31, of which waited for: 12 -> 13; matrix products, arithmetic and copies ran while one was open for 7% -> 5% of each run, Pallas kernels for 0% -> 3%
where the time goes in v4:
time: 175 us; the launch traced here: 173 us
  waiting for transfers between devices  85.1 us (49%)
  starting transfers between devices  33.6 us (19%)
  Pallas kernels  31.8 us (18%)
  other arithmetic  12.1 us (7%)
  local copies, waits for them, and re-layouts  9.67 us (6%)
    ppermute x15, waiting for transfers between devices, to_plane(): return lax.ppermute(value, 'dp', across[r]) if r else value  58.6 us
    pallas_call x5, Pallas kernels, local_call(): pl.pallas_call(kernel, out_shape=outs, in_specs=[pl.BlockSpec(memory_spac...  31.8 us
    ppermute x15, starting transfers between devices, to_plane(): return lax.ppermute(value, 'dp', across[r]) if r else value  25.3 us
    ppermute x6, waiting for transfers between devices, to_spot(): return lax.ppermute(value, 'dp', within[r]) if r else value  18.8 us
    ppermute x1, waiting for transfers between devices, rows_from_flat(): lax.ppermute(tail, AXES, [(i, (i + 1) % count) for i in range(count)])  7.69 us
    ppermute x6, starting transfers between devices, to_spot(): return lax.ppermute(value, 'dp', within[r]) if r else value  7.18 us
    unnamed x60, local copies, waits for them, and re-layouts  5.88 us
    sub x1, other arithmetic, adam_update(): params - LEARN_RATE * (first_hat / (jnp.sqrt(second_hat) + ADAM_EPS) + WE...  4.4 us
  transfers between devices with their start and end apart: 31, of which 13 were waited for; matrix products, arithmetic and copies ran while one was open for 5% of the time, Pallas kernels for 3%

profile of v4, /device:TPU:0, one launch (start us, length us, event | category | flops | bytes accessed | tf_op | source)
XLA Modules:
  0.0 173.2 jit_solution(17745112856542919241)
XLA Ops:
  2.6 4.1 %collective-permute-start.4 = (bf16[128,768]{1,0:T(8,128)(2,1)S(1)}, bf16[128,768]{1,0:T(8,128)(2,1)S(1)}, u32[]{:S(2)}, u32[]{:S(2)}) collective-permute-start(bf16[128,768]{1,0:T(8,128)(2,1)S(1)} %fusion.5.refs_4_), channel_id=1, source_target_pairs={{0,16},{2,18},{4,20},{6,22},{8,24},{10,26},{12,28},{14,30},{16,0},... | collective-permute-start | bytes 589832 | tf_op jit(solution)/shard_map/ppermute | solution.py:868
  10.9 7.7 %collective-permute-done.6 = f32[9984]{0:T(1024)S(1)} collective-permute-done((f32[9984]{0:T(1024)S(1)}, f32[9984]{0:T(1024)S(1)}, u32[]{:S(2)}, u32[]{:S(2)}) %collective-permute-start.6) | collective-permute-done | bytes 39968 | tf_op jit(solution)/shard_map/ppermute | solution.py:284
  20.1 3.3 %shard_map.109 = (bf16[96,768]{1,0:T(8,128)(2,1)}, bf16[96,768]{1,0:T(8,128)(2,1)}, bf16[96,768]{1,0:T(8,128)(2,1)}, bf16[96,768]{1,0:T(8,128)(2,1)}) custom-call(s32[2]{0:T(128)} %pad_add_fusion.1.where_ref, f32[288,768]{1,0:T(8,128)} %reshape.96.rows_ref, f32[16,768]{1,0:T(8,128)} %pad.9.tail_ref), custom_call_target="tpu_custom_call" | custom-call | tf_op jit(solution)/shard_map/pallas_call | solution.py:838
  23.4 2.7 %collective-permute-start.8 = (bf16[96,768]{1,0:T(8,128)(2,1)}, bf16[96,768]{1,0:T(8,128)(2,1)S(1)}, u32[]{:S(2)}, u32[]{:S(2)}) collective-permute-start(bf16[96,768]{1,0:T(8,128)(2,1)} %get-tuple-element.30), channel_id=1, source_target_pairs={{0,16},{2,18},{4,20},{6,22},{8,24},{10,26},{12,28},{14,30},{16,0},... | collective-permute-start | bytes 442376 | tf_op jit(solution)/shard_map/ppermute | solution.py:868
  27.9 2.5 %collective-permute-done.7.b_ref = bf16[96,768]{1,0:T(8,128)(2,1)S(1)} collective-permute-done((bf16[96,768]{1,0:T(8,128)(2,1)}, bf16[96,768]{1,0:T(8,128)(2,1)S(1)}, u32[]{:S(2)}, u32[]{:S(2)}) %collective-permute-start.7) | collective-permute-done | bytes 147488 | tf_op jit(solution)/shard_map/ppermute | solution.py:868
  30.4 3.7 %collective-permute-done.9.d_ref = bf16[96,768]{1,0:T(8,128)(2,1)S(1)} collective-permute-done((bf16[96,768]{1,0:T(8,128)(2,1)}, bf16[96,768]{1,0:T(8,128)(2,1)S(1)}, u32[]{:S(2)}, u32[]{:S(2)}) %collective-permute-start.9) | collective-permute-done | bytes 147488 | tf_op jit(solution)/shard_map/ppermute | solution.py:868
  37.6 2.7 %collective-permute-start.10 = (bf16[352,768]{1,0:T(8,128)(2,1)}, bf16[352,768]{1,0:T(8,128)(2,1)}, u32[]{:S(2)}, u32[]{:S(2)}) collective-permute-start(bf16[352,768]{1,0:T(8,128)(2,1)} %shard_map.110.refs_8_), channel_id=1, source_target_pairs={{0,2},{2,0},{4,6},{6,4},{8,10},{10,8},{12,14},{14,12},{16,18},{18,... | collective-permute-start | bytes 1622024 | tf_op jit(solution)/shard_map/ppermute | solution.py:871
  40.5 3.1 %collective-permute-start.1 = (bf16[144,768]{1,0:T(8,128)(2,1)S(1)}, bf16[144,768]{1,0:T(8,128)(2,1)S(1)}, u32[]{:S(2)}, u32[]{:S(2)}) collective-permute-start(bf16[144,768]{1,0:T(8,128)(2,1)S(1)} %fusion.7.refs_0_), channel_id=1, source_target_pairs={{0,16},{2,18},{4,20},{6,22},{8,24},{10,26},{12,28},{14,30},{16,0},... | collective-permute-start | bytes 663560 | tf_op jit(solution)/shard_map/ppermute | solution.py:868
  43.6 8.0 %collective-permute-done.1.refs_2_ = bf16[144,768]{1,0:T(8,128)(2,1)S(1)} collective-permute-done((bf16[144,768]{1,0:T(8,128)(2,1)S(1)}, bf16[144,768]{1,0:T(8,128)(2,1)S(1)}, u32[]{:S(2)}, u32[]{:S(2)}) %collective-permute-start.1) | collective-permute-done | bytes 221216 | tf_op jit(solution)/shard_map/ppermute | solution.py:868
  53.1 9.5 %collective-permute-done.11.refs_10_ = bf16[352,768]{1,0:T(8,128)(2,1)} collective-permute-done((bf16[352,768]{1,0:T(8,128)(2,1)}, bf16[352,768]{1,0:T(8,128)(2,1)}, u32[]{:S(2)}, u32[]{:S(2)}) %collective-permute-start.11) | collective-permute-done | bytes 540704 | tf_op jit(solution)/shard_map/ppermute | solution.py:871
  63.1 3.0 %collective-permute-start.5 = (bf16[128,768]{1,0:T(8,128)(2,1)S(1)}, bf16[128,768]{1,0:T(8,128)(2,1)}, u32[]{:S(2)}, u32[]{:S(2)}) collective-permute-start(bf16[128,768]{1,0:T(8,128)(2,1)S(1)} %collective-permute-done.4.refs_6_), channel_id=1, source_target_pairs={{0,8},{2,10},{4,12},{6,14},{8,0},{10,2},{12,4},{14,6},{16,24},{18,... | collective-permute-start | bytes 589832 | tf_op jit(solution)/shard_map/ppermute | solution.py:868
  66.0 5.2 %collective-permute-done.5.refs_7_ = bf16[128,768]{1,0:T(8,128)(2,1)} collective-permute-done((bf16[128,768]{1,0:T(8,128)(2,1)S(1)}, bf16[128,768]{1,0:T(8,128)(2,1)}, u32[]{:S(2)}, u32[]{:S(2)}) %collective-permute-start.5) | collective-permute-done | bytes 196640 | tf_op jit(solution)/shard_map/ppermute | solution.py:868
  73.7 4.5 %collective-permute-done.2.refs_3_ = bf16[144,768]{1,0:T(8,128)(2,1)S(1)} collective-permute-done((bf16[144,768]{1,0:T(8,128)(2,1)S(1)}, bf16[144,768]{1,0:T(8,128)(2,1)S(1)}, u32[]{:S(2)}, u32[]{:S(2)}) %collective-permute-start.2) | collective-permute-done | bytes 221216 | tf_op jit(solution)/shard_map/ppermute | solution.py:868
  80.6 20.0 %shard_map.111 = (bf16[352,768]{1,0:T(8,128)(2,1)}, bf16[352,768]{1,0:T(8,128)(2,1)}, bf16[352,768]{1,0:T(8,128)(2,1)}, bf16[352,768]{1,0:T(8,128)(2,1)}, bf16[3...) custom-call(s32[3]{0:T(128)} %pad_add_fusion.where_ref, ...), custom_call_target="tpu_custom_call" | custom-call | tf_op jit(solution)/shard_map/pallas_call | solution.py:838
  103.3 9.7 %collective-permute-done.18 = bf16[256,768]{1,0:T(8,128)(2,1)S(1)} collective-permute-done((bf16[256,768]{1,0:T(8,128)(2,1)}, bf16[256,768]{1,0:T(8,128)(2,1)S(1)}, u32[]{:S(2)}, u32[]{:S(2)}) %collective-permute-start.18) | collective-permute-done | bytes 393248 | tf_op jit(solution)/shard_map/ppermute | solution.py:868
  115.2 2.1 %collective-permute-start.22 = (bf16[352,768]{1,0:T(8,128)(2,1)S(1)}, bf16[352,768]{1,0:T(8,128)(2,1)S(1)}, u32[]{:S(2)}, u32[]{:S(2)}) collective-permute-start(bf16[352,768]{1,0:T(8,128)(2,1)S(1)} %add_convert_fusion.2), channel_id=1, source_target_pairs={{0,2},{2,0},{4,6},{6,4},{8,10},{10,8},{12,14},{14,12},{16,18},{18,... | collective-permute-start | bytes 1622024 | tf_op jit(solution)/shard_map/ppermute | solution.py:871
  120.1 14.9 %collective-permute-done.19 = bf16[256,768]{1,0:T(8,128)(2,1)S(1)} collective-permute-done((bf16[256,768]{1,0:T(8,128)(2,1)S(1)}, bf16[256,768]{1,0:T(8,128)(2,1)S(1)}, u32[]{:S(2)}, u32[]{:S(2)}) %collective-permute-start.19) | collective-permute-done | bytes 393248 | tf_op jit(solution)/shard_map/ppermute | solution.py:868
  135.4 7.8 %collective-permute-done.24.c_ref = bf16[352,768]{1,0:T(8,128)(2,1)S(1)} collective-permute-done((bf16[352,768]{1,0:T(8,128)(2,1)S(1)}, bf16[352,768]{1,0:T(8,128)(2,1)S(1)}, u32[]{:S(2)}, u32[]{:S(2)}) %collective-permute-start.24) | collective-permute-done | bytes 540704 | tf_op jit(solution)/shard_map/ppermute | solution.py:871
  144.0 2.8 %shard_map.112 = (bf16[96,768]{1,0:T(8,128)(2,1)}, bf16[96,768]{1,0:T(8,128)(2,1)}, bf16[96,768]{1,0:T(8,128)(2,1)}, bf16[96,768]{1,0:T(8,128)(2,1)}) custom-call(s32[2]{0:T(128)} %pad_add_fusion.1.where_ref, bf16[352,768]{1,0:T(8,128)(2,1)} %add_convert_fusion.3.a_ref, bf16[352,768]{1,0:T(8,128)(2,1)} %copy-done.15, bf16[352,768]{1,0:T(8,128)(2,1)} %copy-done.16, ...), custom_call_target="tpu_custom_call" | custom-call | tf_op jit(solution)/shard_map/pallas_call | solution.py:838
  147.7 2.6 %collective-permute-start.28 = (bf16[96,768]{1,0:T(8,128)(2,1)}, bf16[96,768]{1,0:T(8,128)(2,1)S(1)}, u32[]{:S(2)}, u32[]{:S(2)}) collective-permute-start(bf16[96,768]{1,0:T(8,128)(2,1)} %get-tuple-element.46), channel_id=1, source_target_pairs={{0,16},{2,18},{4,20},{6,22},{8,24},{10,26},{12,28},{14,30},{16,0},... | collective-permute-start | bytes 442376 | tf_op jit(solution)/shard_map/ppermute | solution.py:868
  151.2 2.9 %collective-permute-done.27.refs_1_ = bf16[96,768]{1,0:T(8,128)(2,1)S(1)} collective-permute-done((bf16[96,768]{1,0:T(8,128)(2,1)}, bf16[96,768]{1,0:T(8,128)(2,1)S(1)}, u32[]{:S(2)}, u32[]{:S(2)}) %collective-permute-start.27) | collective-permute-done | bytes 147488 | tf_op jit(solution)/shard_map/ppermute | solution.py:868
  154.1 7.3 %collective-permute-done.28.refs_2_ = bf16[96,768]{1,0:T(8,128)(2,1)S(1)} collective-permute-done((bf16[96,768]{1,0:T(8,128)(2,1)}, bf16[96,768]{1,0:T(8,128)(2,1)S(1)}, u32[]{:S(2)}, u32[]{:S(2)}) %collective-permute-start.28) | collective-permute-done | bytes 147488 | tf_op jit(solution)/shard_map/ppermute | solution.py:868
  162.1 3.6 %shard_map.113 = (f32[288,768]{1,0:T(8,128)}, f32[16,768]{1,0:T(8,128)}) custom-call(s32[2]{0:T(128)} %pad_add_fusion.1.where_ref, bf16[96,768]{1,0:T(8,128)(2,1)} %get-tuple-element.44.refs_0_, bf16[96,768]{1,0:T(8,128)(2,1)} %copy-done.22, bf16[96,768]{1,0:T(8,128)(2,1)} %copy-done.23, bf16[96,768]{1,0:T(8,128)(2,1)} %copy-done.25), custom_call_target="tpu_custom_call" | custom-call | tf_op jit(solution)/shard_map/pallas_call | solution.py:838
  168.8 4.4 %multiply_subtract_fusion = (f32[221496]{0:T(1024)}, f32[221496]{0:T(1024)}, f32[221496]{0:T(1024)}, f32[221496]{0:T(1024)}) fusion(f32[221496]{0:T(1024)S(1)} %copy-done.1, f32[221496]{0:T(1024)} %param.10, f32[221496]{0:T(1024)} %param.11, s32[]{:T(128)S(6)} %select_n.30, f32[9984]{0:T(1024)S(1)} %broadcast_select_fusion, f32[221184]{0:T(1024)S(1)} %reshape.100), kind=kLoop, calls=%fused_computation.11 | loop fusion | flops 3543936 | bytes 7126564 | tf_op jit(solution)/shard_map/sub | solution.py:271
  (138 shorter events, 34.2 us)
Async XLA Ops:
  2.6 37.9 %collective-permute-start.4 = (bf16[128,768]{1,0:T(8,128)(2,1)S(1)}, bf16[128,768]{1,0:T(8,128)(2,1)S(1)}, u32[]{:S(2)}, u32[]{:S(2)}) collective-permute-start(bf16[128,768]{1,0:T(8,128)(2,1)S(1)} %fusion.5.refs_4_), channel_id=1, source_target_pairs={{0,16},{2,18},{4,20},{6,22},{8,24},{10,26},{12,28},{14,30},{16,0},... | collective-permute-start | bytes 589832 | tf_op jit(solution)/shard_map/ppermute | solution.py:868
  6.7 36.8 %collective-permute-start.3 = (bf16[128,768]{1,0:T(8,128)(2,1)S(1)}, bf16[128,768]{1,0:T(8,128)(2,1)}, u32[]{:S(2)}, u32[]{:S(2)}) collective-permute-start(bf16[128,768]{1,0:T(8,128)(2,1)S(1)} %fusion.5.refs_4_), channel_id=1, source_target_pairs={{0,8},{2,10},{4,12},{6,14},{8,0},{10,2},{12,4},{14,6},{16,24},{18,... | collective-permute-start | bytes 589832 | tf_op jit(solution)/shard_map/ppermute | solution.py:868
  9.2 9.4 %collective-permute-start.6 = (f32[9984]{0:T(1024)S(1)}, f32[9984]{0:T(1024)S(1)}, u32[]{:S(2)}, u32[]{:S(2)}) collective-permute-start(f32[9984]{0:T(1024)S(1)} %slice.18), channel_id=1, source_target_pairs={{0,1},{1,2},{2,3},{3,4},{4,5},{5,6},{6,7},{7,8},{8,9},{9,10},{10,1... | collective-permute-start | bytes 119816 | tf_op jit(solution)/shard_map/ppermute | solution.py:284
  36.8 16.3 %collective-permute-start.12 = (bf16[352,768]{1,0:T(8,128)(2,1)}, bf16[352,768]{1,0:T(8,128)(2,1)S(1)}, u32[]{:S(2)}, u32[]{:S(2)}) collective-permute-start(bf16[352,768]{1,0:T(8,128)(2,1)} %shard_map.110.refs_8_), channel_id=1, source_target_pairs={{0,6},{2,4},{4,2},{6,0},{8,14},{10,12},{12,10},{14,8},{16,22},{18,... | collective-permute-start | bytes 1622024 | tf_op jit(solution)/shard_map/ppermute | solution.py:871
  36.9 25.6 %collective-permute-start.11 = (bf16[352,768]{1,0:T(8,128)(2,1)}, bf16[352,768]{1,0:T(8,128)(2,1)}, u32[]{:S(2)}, u32[]{:S(2)}) collective-permute-start(bf16[352,768]{1,0:T(8,128)(2,1)} %shard_map.110.refs_8_), channel_id=1, source_target_pairs={{0,4},{2,6},{4,0},{6,2},{8,12},{10,14},{12,8},{14,10},{16,20},{18,... | collective-permute-start | bytes 1622024 | tf_op jit(solution)/shard_map/ppermute | solution.py:871
  37.6 25.1 %collective-permute-start.10 = (bf16[352,768]{1,0:T(8,128)(2,1)}, bf16[352,768]{1,0:T(8,128)(2,1)}, u32[]{:S(2)}, u32[]{:S(2)}) collective-permute-start(bf16[352,768]{1,0:T(8,128)(2,1)} %shard_map.110.refs_8_), channel_id=1, source_target_pairs={{0,2},{2,0},{4,6},{6,4},{8,10},{10,8},{12,14},{14,12},{16,18},{18,... | collective-permute-start | bytes 1622024 | tf_op jit(solution)/shard_map/ppermute | solution.py:871
  40.5 11.1 %collective-permute-start.1 = (bf16[144,768]{1,0:T(8,128)(2,1)S(1)}, bf16[144,768]{1,0:T(8,128)(2,1)S(1)}, u32[]{:S(2)}, u32[]{:S(2)}) collective-permute-start(bf16[144,768]{1,0:T(8,128)(2,1)S(1)} %fusion.7.refs_0_), channel_id=1, source_target_pairs={{0,16},{2,18},{4,20},{6,22},{8,24},{10,26},{12,28},{14,30},{16,0},... | collective-permute-start | bytes 663560 | tf_op jit(solution)/shard_map/ppermute | solution.py:868
  43.6 19.5 %collective-permute-start = (bf16[144,768]{1,0:T(8,128)(2,1)S(1)}, bf16[144,768]{1,0:T(8,128)(2,1)S(1)}, u32[]{:S(2)}, u32[]{:S(2)}) collective-permute-start(bf16[144,768]{1,0:T(8,128)(2,1)S(1)} %fusion.7.refs_0_), channel_id=1, source_target_pairs={{0,8},{2,10},{4,12},{6,14},{8,0},{10,2},{12,4},{14,6},{16,24},{18,... | collective-permute-start | bytes 663560 | tf_op jit(solution)/shard_map/ppermute | solution.py:868
  51.6 26.5 %collective-permute-start.13 = (bf16[352,768]{1,0:T(8,128)(2,1)S(1)}, bf16[352,768]{1,0:T(8,128)(2,1)S(1)}, u32[]{:S(2)}, u32[]{:S(2)}) collective-permute-start(bf16[352,768]{1,0:T(8,128)(2,1)S(1)} %copy-done.2), channel_id=1, source_target_pairs={{0,1},{1,0},{2,3},{3,2},{4,5},{5,4},{6,7},{7,6},{8,9},{9,8},{10,11... | collective-permute-start | bytes 1622024 | tf_op jit(solution)/shard_map/ppermute | solution.py:874
  53.1 25.1 %collective-permute-start.16 = (bf16[352,768]{1,0:T(8,128)(2,1)S(1)}, bf16[352,768]{1,0:T(8,128)(2,1)S(1)}, u32[]{:S(2)}, u32[]{:S(2)}) collective-permute-start(bf16[352,768]{1,0:T(8,128)(2,1)S(1)} %collective-permute-done.12.refs_11_), channel_id=1, source_target_pairs={{0,1},{1,0},{2,3},{3,2},{4,5},{5,4},{6,7},{7,6},{8,9},{9,8},{10,11... | collective-permute-start | bytes 1622024 | tf_op jit(solution)/shard_map/ppermute | solution.py:874
  62.5 16.5 %collective-permute-start.15 = (bf16[352,768]{1,0:T(8,128)(2,1)}, bf16[352,768]{1,0:T(8,128)(2,1)S(1)}, u32[]{:S(2)}, u32[]{:S(2)}) collective-permute-start(bf16[352,768]{1,0:T(8,128)(2,1)} %collective-permute-done.11.refs_10_), channel_id=1, source_target_pairs={{0,1},{1,0},{2,3},{3,2},{4,5},{5,4},{6,7},{7,6},{8,9},{9,8},{10,11... | collective-permute-start | bytes 1622024 | tf_op jit(solution)/shard_map/ppermute | solution.py:874
  62.6 17.9 %collective-permute-start.14 = (bf16[352,768]{1,0:T(8,128)(2,1)}, bf16[352,768]{1,0:T(8,128)(2,1)}, u32[]{:S(2)}, u32[]{:S(2)}) collective-permute-start(bf16[352,768]{1,0:T(8,128)(2,1)} %collective-permute-done.10.refs_9_), channel_id=1, source_target_pairs={{0,1},{1,0},{2,3},{3,2},{4,5},{5,4},{6,7},{7,6},{8,9},{9,8},{10,11... | collective-permute-start | bytes 1622024 | tf_op jit(solution)/shard_map/ppermute | solution.py:874
  63.1 8.2 %collective-permute-start.5 = (bf16[128,768]{1,0:T(8,128)(2,1)S(1)}, bf16[128,768]{1,0:T(8,128)(2,1)}, u32[]{:S(2)}, u32[]{:S(2)}) collective-permute-start(bf16[128,768]{1,0:T(8,128)(2,1)S(1)} %collective-permute-done.4.refs_6_), channel_id=1, source_target_pairs={{0,8},{2,10},{4,12},{6,14},{8,0},{10,2},{12,4},{14,6},{16,24},{18,... | collective-permute-start | bytes 589832 | tf_op jit(solution)/shard_map/ppermute | solution.py:868
  100.7 12.3 %collective-permute-start.18 = (bf16[256,768]{1,0:T(8,128)(2,1)}, bf16[256,768]{1,0:T(8,128)(2,1)S(1)}, u32[]{:S(2)}, u32[]{:S(2)}) collective-permute-start(bf16[256,768]{1,0:T(8,128)(2,1)} %get-tuple-element.35), channel_id=1, source_target_pairs={{0,8},{2,10},{4,12},{6,14},{8,0},{10,2},{12,4},{14,6},{16,24},{18,... | collective-permute-start | bytes 1179656 | tf_op jit(solution)/shard_map/ppermute | solution.py:868
  102.2 11.9 %collective-permute-start.21 = (bf16[352,768]{1,0:T(8,128)(2,1)}, bf16[352,768]{1,0:T(8,128)(2,1)S(1)}, u32[]{:S(2)}, u32[]{:S(2)}) collective-permute-start(bf16[352,768]{1,0:T(8,128)(2,1)} %get-tuple-element.39), channel_id=1, source_target_pairs={{0,1},{1,0},{2,3},{3,2},{4,5},{5,4},{6,7},{7,6},{8,9},{9,8},{10,11... | collective-permute-start | bytes 1622024 | tf_op jit(solution)/shard_map/ppermute | solution.py:874
  102.2 13.0 %collective-permute-start.23 = (bf16[352,768]{1,0:T(8,128)(2,1)}, bf16[352,768]{1,0:T(8,128)(2,1)S(1)}, u32[]{:S(2)}, u32[]{:S(2)}) collective-permute-start(bf16[352,768]{1,0:T(8,128)(2,1)} %get-tuple-element.41), channel_id=1, source_target_pairs={{0,1},{1,0},{2,3},{3,2},{4,5},{5,4},{6,7},{7,6},{8,9},{9,8},{10,11... | collective-permute-start | bytes 1622024 | tf_op jit(solution)/shard_map/ppermute | solution.py:874
  102.7 17.4 %collective-permute-start.17 = (bf16[256,768]{1,0:T(8,128)(2,1)}, bf16[256,768]{1,0:T(8,128)(2,1)S(1)}, u32[]{:S(2)}, u32[]{:S(2)}) collective-permute-start(bf16[256,768]{1,0:T(8,128)(2,1)} %get-tuple-element.33), channel_id=1, source_target_pairs={{0,8},{2,10},{4,12},{6,14},{8,0},{10,2},{12,4},{14,6},{16,24},{18,... | collective-permute-start | bytes 1179656 | tf_op jit(solution)/shard_map/ppermute | solution.py:868
  103.3 14.6 %collective-permute-start.20 = (bf16[352,768]{1,0:T(8,128)(2,1)}, bf16[352,768]{1,0:T(8,128)(2,1)S(1)}, u32[]{:S(2)}, u32[]{:S(2)}) collective-permute-start(bf16[352,768]{1,0:T(8,128)(2,1)} %get-tuple-element.37), channel_id=1, source_target_pairs={{0,1},{1,0},{2,3},{3,2},{4,5},{5,4},{6,7},{7,6},{8,9},{9,8},{10,11... | collective-permute-start | bytes 1622024 | tf_op jit(solution)/shard_map/ppermute | solution.py:874
  114.1 20.9 %collective-permute-start.19 = (bf16[256,768]{1,0:T(8,128)(2,1)S(1)}, bf16[256,768]{1,0:T(8,128)(2,1)S(1)}, u32[]{:S(2)}, u32[]{:S(2)}) collective-permute-start(bf16[256,768]{1,0:T(8,128)(2,1)S(1)} %add_convert_fusion.4), channel_id=1, source_target_pairs={{0,16},{2,18},{4,20},{6,22},{8,24},{10,26},{12,28},{14,30},{16,0},... | collective-permute-start | bytes 1179656 | tf_op jit(solution)/shard_map/ppermute | solution.py:868
  115.2 20.1 %collective-permute-start.22 = (bf16[352,768]{1,0:T(8,128)(2,1)S(1)}, bf16[352,768]{1,0:T(8,128)(2,1)S(1)}, u32[]{:S(2)}, u32[]{:S(2)}) collective-permute-start(bf16[352,768]{1,0:T(8,128)(2,1)S(1)} %add_convert_fusion.2), channel_id=1, source_target_pairs={{0,2},{2,0},{4,6},{6,4},{8,10},{10,8},{12,14},{14,12},{16,18},{18,... | collective-permute-start | bytes 1622024 | tf_op jit(solution)/shard_map/ppermute | solution.py:871
  117.4 25.8 %collective-permute-start.24 = (bf16[352,768]{1,0:T(8,128)(2,1)S(1)}, bf16[352,768]{1,0:T(8,128)(2,1)S(1)}, u32[]{:S(2)}, u32[]{:S(2)}) collective-permute-start(bf16[352,768]{1,0:T(8,128)(2,1)S(1)} %add_convert_fusion.1), channel_id=1, source_target_pairs={{0,4},{2,6},{4,0},{6,2},{8,12},{10,14},{12,8},{14,10},{16,20},{18,... | collective-permute-start | bytes 1622024 | tf_op jit(solution)/shard_map/ppermute | solution.py:871
  117.9 25.3 %collective-permute-start.26 = (bf16[352,768]{1,0:T(8,128)(2,1)S(1)}, bf16[352,768]{1,0:T(8,128)(2,1)}, u32[]{:S(2)}, u32[]{:S(2)}) collective-permute-start(bf16[352,768]{1,0:T(8,128)(2,1)S(1)} %add_convert_fusion), channel_id=1, source_target_pairs={{0,6},{2,4},{4,2},{6,0},{8,14},{10,12},{12,10},{14,8},{16,22},{18,... | collective-permute-start | bytes 1622024 | tf_op jit(solution)/shard_map/ppermute | solution.py:871
  147.7 13.7 %collective-permute-start.28 = (bf16[96,768]{1,0:T(8,128)(2,1)}, bf16[96,768]{1,0:T(8,128)(2,1)S(1)}, u32[]{:S(2)}, u32[]{:S(2)}) collective-permute-start(bf16[96,768]{1,0:T(8,128)(2,1)} %get-tuple-element.46), channel_id=1, source_target_pairs={{0,16},{2,18},{4,20},{6,22},{8,24},{10,26},{12,28},{14,30},{16,0},... | collective-permute-start | bytes 442376 | tf_op jit(solution)/shard_map/ppermute | solution.py:868
  150.3 11.1 %collective-permute-start.29 = (bf16[96,768]{1,0:T(8,128)(2,1)}, bf16[96,768]{1,0:T(8,128)(2,1)S(1)}, u32[]{:S(2)}, u32[]{:S(2)}) collective-permute-start(bf16[96,768]{1,0:T(8,128)(2,1)} %get-tuple-element.47), channel_id=1, source_target_pairs={{0,24},{2,26},{4,28},{6,30},{8,16},{10,18},{12,20},{14,22},{16,8},... | collective-permute-start | bytes 442376 | tf_op jit(solution)/shard_map/ppermute | solution.py:868
  (37 other events, 363.2 us)

commit v5 on v4

--- a/solution.py
+++ b/solution.py
@@ -833,15 +833,20 @@
         ref[...] = slab[...].astype(BF)
 
 
-def local_call(kernel, outs, scratch, *operands):
+def local_call(kernel, outs, scratch, limit, kept_out, where, *operands):
     vmem = pl.BlockSpec(memory_space=pltpu.VMEM)
+    operands = [pltpu.with_memory_space_constraint(x, pltpu.VMEM) for x in operands]
+    out_specs = jax.tree.map(lambda _: vmem, outs)
+    if kept_out:
+        outs = jax.tree.map(lambda x: pltpu.VMEM(x.shape, x.dtype), outs)
     return pl.pallas_call(
         kernel,
         out_shape=outs,
-        in_specs=[pl.BlockSpec(memory_space=pltpu.SMEM)] + [vmem] * (len(operands) - 1),
-        out_specs=jax.tree.map(lambda _: vmem, outs),
+        in_specs=[pl.BlockSpec(memory_space=pltpu.SMEM)] + [vmem] * len(operands),
+        out_specs=out_specs,
         scratch_shapes=scratch,
-    )(*operands)
+        compiler_params=pltpu.CompilerParams(vmem_limit_bytes=limit << 20),
+    )(where, *operands)
 
 
 def sliced_step(planes, places, *args):
@@ -899,11 +904,11 @@
         pltpu.VMEM(rows.shape, BF),
     ]
     spots = local_call(
-        pack_kernel, [spot_shape] * planes, sort_scratch,
+        pack_kernel, [spot_shape] * planes, sort_scratch, 12, True,
         where_owner, rows, tail,
     )
     spots = [to_plane(spots[r], r) for r in range(planes)]
-    slab = local_call(slab_kernel, slab_shape, [], where_owner, *spots)
+    slab = local_call(slab_kernel, slab_shape, [], 8, True, where_owner, *spots)
     slabs = [to_spot(slab, r) for r in range(places)]
     slabs = slabs + [to_core(s) for s in slabs]
 
@@ -931,7 +936,7 @@
             pltpu.VMEM((total, D), F32),
             pltpu.VMEM((SLAB, D), F32),
         ],
-        where_spot, *acts, *cots, *slabs,
+        44, True, where_spot, *acts, *cots, *slabs,
     )
     grads, backs = outs[:8], outs[8:]
     paired = [
@@ -945,7 +950,7 @@
         to_plane((backs[2].astype(F32) + passed.astype(F32)).astype(BF), 2),
     ]
     spots = local_call(
-        split_kernel, [spot_shape] * planes, [pltpu.VMEM((SLAB, D), F32)], where_owner, *arrived
+        split_kernel, [spot_shape] * planes, [pltpu.VMEM((SLAB, D), F32)], 12, True, where_owner, *arrived
     )
     spots = [to_plane(spots[r], r) for r in range(planes)]
     grad_rows, grad_tail = local_call(
@@ -954,7 +959,7 @@
             jax.ShapeDtypeStruct(rows.shape, F32),
             jax.ShapeDtypeStruct((16, D), F32),
         ],
-        sort_scratch,
+        sort_scratch, 12, True,
         where_owner, *spots,
     )
     back = sum(b.astype(F32) for b in backs)

time: 175 us -> 166 us (0.949)
  Pallas kernels: 31.8 us -> 22.2 us
    pallas_call x5, Pallas kernels: 31.8 us -> 22.2 us  [local_call(): pl.pallas_call(kernel, out_shape=outs, in_specs=[pl.BlockSpec(memory_spac...]
    unnamed x60 -> x38, local copies, waits for them, and re-layouts: 5.88 us -> 8.37 us
  transfers between devices with their start and end apart: 31 -> 31, of which waited for: 13 -> 14; matrix products, arithmetic and copies ran while one was open for 5% -> 4% of each run, Pallas kernels for 3% -> 2%
where the time goes in v5:
time: 166 us; the launch traced here: 165 us
  waiting for transfers between devices  86.2 us (52%)
  starting transfers between devices  34.1 us (21%)
  Pallas kernels  22.2 us (13%)
  other arithmetic  11.7 us (7%)
  local copies, waits for them, and re-layouts  9.84 us (6%)
    ppermute x15, waiting for transfers between devices, to_plane(): return lax.ppermute(value, 'dp', across[r]) if r else value  57.1 us
    ppermute x15, starting transfers between devices, to_plane(): return lax.ppermute(value, 'dp', across[r]) if r else value  25.5 us
    pallas_call x5, Pallas kernels, local_call(): pl.pallas_call(kernel, out_shape=outs, in_specs=[pl.BlockSpec(memory_spac...  22.2 us
    ppermute x6, waiting for transfers between devices, to_spot(): return lax.ppermute(value, 'dp', within[r]) if r else value  19.5 us
    ppermute x1, waiting for transfers between devices, rows_from_flat(): lax.ppermute(tail, AXES, [(i, (i + 1) % count) for i in range(count)])  8.88 us
    unnamed x38, local copies, waits for them, and re-layouts  8.37 us
    ppermute x6, starting transfers between devices, to_spot(): return lax.ppermute(value, 'dp', within[r]) if r else value  7.38 us
    sub x1, other arithmetic, adam_update(): params - LEARN_RATE * (first_hat / (jnp.sqrt(second_hat) + ADAM_EPS) + WE...  4.39 us
  transfers between devices with their start and end apart: 31, of which 14 were waited for; matrix products, arithmetic and copies ran while one was open for 4% of the time, Pallas kernels for 2%

profile of v5, /device:TPU:0, one launch (start us, length us, event | category | flops | bytes accessed | tf_op | source)
XLA Modules:
  0.0 165.1 jit_solution(13281682353071013795)
XLA Ops:
  2.6 4.1 %collective-permute-start.4 = (bf16[128,768]{1,0:T(8,128)(2,1)S(1)}, bf16[128,768]{1,0:T(8,128)(2,1)S(1)}, u32[]{:S(2)}, u32[]{:S(2)}) collective-permute-start(bf16[128,768]{1,0:T(8,128)(2,1)S(1)} %fusion.5.refs_4_), channel_id=1, source_target_pairs={{0,16},{2,18},{4,20},{6,22},{8,24},{10,26},{12,28},{14,30},{16,0},... | collective-permute-start | bytes 589832 | tf_op jit(solution)/shard_map/ppermute | solution.py:873
  9.8 8.9 %collective-permute-done.6 = f32[9984]{0:T(1024)S(1)} collective-permute-done((f32[9984]{0:T(1024)S(1)}, f32[9984]{0:T(1024)S(1)}, u32[]{:S(2)}, u32[]{:S(2)}) %collective-permute-start.6) | collective-permute-done | bytes 39968 | tf_op jit(solution)/shard_map/ppermute | solution.py:284
  19.2 1.9 %shard_map.109 = (bf16[96,768]{1,0:T(8,128)(2,1)S(1)}, bf16[96,768]{1,0:T(8,128)(2,1)S(1)}, bf16[96,768]{1,0:T(8,128)(2,1)S(1)}, bf16[96,768]{1,0:T(8,128)(2,1)S(1)}) custom-call(s32[2]{0:T(128)S(1)} %pad_add_fusion.1.where_ref, f32[288,768]{1,0:T(8,128)S(1)} %reshape.96.rows_ref, f32[16,768]{1,0:T(8,128)S(1)} %pad.9.tail_ref), custom_call_target="tpu_custom_call" | custom-call | tf_op jit(solution)/shard_map/pallas_call | solution.py:842
  21.2 2.7 %collective-permute-start.8 = (bf16[96,768]{1,0:T(8,128)(2,1)S(1)}, bf16[96,768]{1,0:T(8,128)(2,1)S(1)}, u32[]{:S(2)}, u32[]{:S(2)}) collective-permute-start(bf16[96,768]{1,0:T(8,128)(2,1)S(1)} %get-tuple-element.30), channel_id=1, source_target_pairs={{0,16},{2,18},{4,20},{6,22},{8,24},{10,26},{12,28},{14,30},{16,0},... | collective-permute-start | bytes 442376 | tf_op jit(solution)/shard_map/ppermute | solution.py:873
  25.6 2.2 %collective-permute-done.7.b_ref = bf16[96,768]{1,0:T(8,128)(2,1)S(1)} collective-permute-done((bf16[96,768]{1,0:T(8,128)(2,1)S(1)}, bf16[96,768]{1,0:T(8,128)(2,1)S(1)}, u32[]{:S(2)}, u32[]{:S(2)}) %collective-permute-start.7) | collective-permute-done | bytes 147488 | tf_op jit(solution)/shard_map/ppermute | solution.py:873
  27.9 3.7 %collective-permute-done.9.d_ref = bf16[96,768]{1,0:T(8,128)(2,1)S(1)} collective-permute-done((bf16[96,768]{1,0:T(8,128)(2,1)S(1)}, bf16[96,768]{1,0:T(8,128)(2,1)S(1)}, u32[]{:S(2)}, u32[]{:S(2)}) %collective-permute-start.9) | collective-permute-done | bytes 147488 | tf_op jit(solution)/shard_map/ppermute | solution.py:873
  32.7 3.1 %collective-permute-start.10 = (bf16[352,768]{1,0:T(8,128)(2,1)S(1)}, bf16[352,768]{1,0:T(8,128)(2,1)S(1)}, u32[]{:S(2)}, u32[]{:S(2)}) collective-permute-start(bf16[352,768]{1,0:T(8,128)(2,1)S(1)} %shard_map.110.refs_8_), channel_id=1, source_target_pairs={{0,2},{2,0},{4,6},{6,4},{8,10},{10,8},{12,14},{14,12},{16,18},{18,... | collective-permute-start | bytes 1622024 | tf_op jit(solution)/shard_map/ppermute | solution.py:876
  36.0 3.1 %collective-permute-start.1 = (bf16[144,768]{1,0:T(8,128)(2,1)S(1)}, bf16[144,768]{1,0:T(8,128)(2,1)S(1)}, u32[]{:S(2)}, u32[]{:S(2)}) collective-permute-start(bf16[144,768]{1,0:T(8,128)(2,1)S(1)} %fusion.7.refs_0_), channel_id=1, source_target_pairs={{0,16},{2,18},{4,20},{6,22},{8,24},{10,26},{12,28},{14,30},{16,0},... | collective-permute-start | bytes 663560 | tf_op jit(solution)/shard_map/ppermute | solution.py:873
  39.8 7.4 %collective-permute-done.1.refs_2_ = bf16[144,768]{1,0:T(8,128)(2,1)S(1)} collective-permute-done((bf16[144,768]{1,0:T(8,128)(2,1)S(1)}, bf16[144,768]{1,0:T(8,128)(2,1)S(1)}, u32[]{:S(2)}, u32[]{:S(2)}) %collective-permute-start.1) | collective-permute-done | bytes 221216 | tf_op jit(solution)/shard_map/ppermute | solution.py:873
  48.4 9.3 %collective-permute-done.11.refs_10_ = bf16[352,768]{1,0:T(8,128)(2,1)S(1)} collective-permute-done((bf16[352,768]{1,0:T(8,128)(2,1)S(1)}, bf16[352,768]{1,0:T(8,128)(2,1)S(1)}, u32[]{:S(2)}, u32[]{:S(2)}) %collective-permute-start.11) | collective-permute-done | bytes 540704 | tf_op jit(solution)/shard_map/ppermute | solution.py:876
  58.2 3.0 %collective-permute-start.5 = (bf16[128,768]{1,0:T(8,128)(2,1)S(1)}, bf16[128,768]{1,0:T(8,128)(2,1)S(1)}, u32[]{:S(2)}, u32[]{:S(2)}) collective-permute-start(bf16[128,768]{1,0:T(8,128)(2,1)S(1)} %collective-permute-done.4.refs_6_), channel_id=1, source_target_pairs={{0,8},{2,10},{4,12},{6,14},{8,0},{10,2},{12,4},{14,6},{16,24},{18,... | collective-permute-start | bytes 589832 | tf_op jit(solution)/shard_map/ppermute | solution.py:873
  61.2 5.1 %collective-permute-done.5.refs_7_ = bf16[128,768]{1,0:T(8,128)(2,1)S(1)} collective-permute-done((bf16[128,768]{1,0:T(8,128)(2,1)S(1)}, bf16[128,768]{1,0:T(8,128)(2,1)S(1)}, u32[]{:S(2)}, u32[]{:S(2)}) %collective-permute-start.5) | collective-permute-done | bytes 196640 | tf_op jit(solution)/shard_map/ppermute | solution.py:873
  66.3 1.7 %collective-permute-start.2 = (bf16[144,768]{1,0:T(8,128)(2,1)S(1)}, bf16[144,768]{1,0:T(8,128)(2,1)S(1)}, u32[]{:S(2)}, u32[]{:S(2)}) collective-permute-start(bf16[144,768]{1,0:T(8,128)(2,1)S(1)} %collective-permute-done.1.refs_2_), channel_id=1, source_target_pairs={{0,8},{2,10},{4,12},{6,14},{8,0},{10,2},{12,4},{14,6},{16,24},{18,... | collective-permute-start | bytes 663560 | tf_op jit(solution)/shard_map/ppermute | solution.py:873
  68.7 4.5 %collective-permute-done.2.refs_3_ = bf16[144,768]{1,0:T(8,128)(2,1)S(1)} collective-permute-done((bf16[144,768]{1,0:T(8,128)(2,1)S(1)}, bf16[144,768]{1,0:T(8,128)(2,1)S(1)}, u32[]{:S(2)}, u32[]{:S(2)}) %collective-permute-start.2) | collective-permute-done | bytes 221216 | tf_op jit(solution)/shard_map/ppermute | solution.py:873
  74.1 16.6 %shard_map.111 = (bf16[352,768]{1,0:T(8,128)(2,1)S(1)}, bf16[352,768]{1,0:T(8,128)(2,1)S(1)}, bf16[352,768]{1,0:T(8,128)(2,1)S(1)}, bf16[352,768]{1,0:T(8,128)(2...) custom-call(s32[3]{0:T(128)} %pad_add_fusion.where_ref, ...), custom_call_target="tpu_custom_call" | custom-call | tf_op jit(solution)/shard_map/pallas_call | solution.py:842
  99.5 9.7 %collective-permute-done.18 = bf16[256,768]{1,0:T(8,128)(2,1)S(1)} collective-permute-done((bf16[256,768]{1,0:T(8,128)(2,1)}, bf16[256,768]{1,0:T(8,128)(2,1)S(1)}, u32[]{:S(2)}, u32[]{:S(2)}) %collective-permute-start.18) | collective-permute-done | bytes 393248 | tf_op jit(solution)/shard_map/ppermute | solution.py:873
  112.5 2.2 %collective-permute-start.22 = (bf16[352,768]{1,0:T(8,128)(2,1)S(1)}, bf16[352,768]{1,0:T(8,128)(2,1)S(1)}, u32[]{:S(2)}, u32[]{:S(2)}) collective-permute-start(bf16[352,768]{1,0:T(8,128)(2,1)S(1)} %add_convert_fusion.2), channel_id=1, source_target_pairs={{0,2},{2,0},{4,6},{6,4},{8,10},{10,8},{12,14},{14,12},{16,18},{18,... | collective-permute-start | bytes 1622024 | tf_op jit(solution)/shard_map/ppermute | solution.py:876
  116.8 14.5 %collective-permute-done.19 = bf16[256,768]{1,0:T(8,128)(2,1)S(1)} collective-permute-done((bf16[256,768]{1,0:T(8,128)(2,1)S(1)}, bf16[256,768]{1,0:T(8,128)(2,1)S(1)}, u32[]{:S(2)}, u32[]{:S(2)}) %collective-permute-start.19) | collective-permute-done | bytes 393248 | tf_op jit(solution)/shard_map/ppermute | solution.py:873
  131.6 9.1 %collective-permute-done.24.c_ref = bf16[352,768]{1,0:T(8,128)(2,1)S(1)} collective-permute-done((bf16[352,768]{1,0:T(8,128)(2,1)S(1)}, bf16[352,768]{1,0:T(8,128)(2,1)S(1)}, u32[]{:S(2)}, u32[]{:S(2)}) %collective-permute-start.24) | collective-permute-done | bytes 540704 | tf_op jit(solution)/shard_map/ppermute | solution.py:876
  142.8 2.6 %collective-permute-start.28 = (bf16[96,768]{1,0:T(8,128)(2,1)S(1)}, bf16[96,768]{1,0:T(8,128)(2,1)S(1)}, u32[]{:S(2)}, u32[]{:S(2)}) collective-permute-start(bf16[96,768]{1,0:T(8,128)(2,1)S(1)} %get-tuple-element.46), channel_id=1, source_target_pairs={{0,16},{2,18},{4,20},{6,22},{8,24},{10,26},{12,28},{14,30},{16,0},... | collective-permute-start | bytes 442376 | tf_op jit(solution)/shard_map/ppermute | solution.py:873
  146.2 2.7 %collective-permute-done.27.refs_1_ = bf16[96,768]{1,0:T(8,128)(2,1)S(1)} collective-permute-done((bf16[96,768]{1,0:T(8,128)(2,1)S(1)}, bf16[96,768]{1,0:T(8,128)(2,1)S(1)}, u32[]{:S(2)}, u32[]{:S(2)}) %collective-permute-start.27) | collective-permute-done | bytes 147488 | tf_op jit(solution)/shard_map/ppermute | solution.py:873
  148.9 7.3 %collective-permute-done.28.refs_2_ = bf16[96,768]{1,0:T(8,128)(2,1)S(1)} collective-permute-done((bf16[96,768]{1,0:T(8,128)(2,1)S(1)}, bf16[96,768]{1,0:T(8,128)(2,1)S(1)}, u32[]{:S(2)}, u32[]{:S(2)}) %collective-permute-start.28) | collective-permute-done | bytes 147488 | tf_op jit(solution)/shard_map/ppermute | solution.py:873
  156.2 2.1 %shard_map.113 = (f32[288,768]{1,0:T(8,128)S(1)}, f32[16,768]{1,0:T(8,128)S(1)}) custom-call(s32[2]{0:T(128)S(1)} %pad_add_fusion.1.where_ref, bf16[96,768]{1,0:T(8,128)(2,1)S(1)} %get-tuple-element.44.refs_0_, bf16[96,768]{1,0:T(8,128)(2,1)S(1)} %collective-permute-done.27.refs_1_, bf16[96,768]{1,0:T(8,128)(2,1)S(1)} %collective-permute-done.28.refs_2_, ...), custom_call_target="tpu_custom_call" | custom-call | tf_op jit(solution)/shard_map/pallas_call | solution.py:842
  160.7 4.4 %multiply_subtract_fusion = (f32[221496]{0:T(1024)}, f32[221496]{0:T(1024)}, f32[221496]{0:T(1024)}, f32[221496]{0:T(1024)}) fusion(f32[221496]{0:T(1024)S(1)} %copy-done.16, f32[221496]{0:T(1024)} %param.10, f32[221496]{0:T(1024)} %param.11, s32[]{:T(128)S(6)} %select_n.30, f32[9984]{0:T(1024)S(1)} %broadcast_select_fusion, f32[221184]{0:T(1024)S(1)} %reshape.100), kind=kLoop, calls=%fused_computation.11 | loop fusion | flops 3543936 | bytes 7126564 | tf_op jit(solution)/shard_map/sub | solution.py:271
  (116 shorter events, 32.3 us)
Async XLA Ops:
  2.6 33.4 %collective-permute-start.4 = (bf16[128,768]{1,0:T(8,128)(2,1)S(1)}, bf16[128,768]{1,0:T(8,128)(2,1)S(1)}, u32[]{:S(2)}, u32[]{:S(2)}) collective-permute-start(bf16[128,768]{1,0:T(8,128)(2,1)S(1)} %fusion.5.refs_4_), channel_id=1, source_target_pairs={{0,16},{2,18},{4,20},{6,22},{8,24},{10,26},{12,28},{14,30},{16,0},... | collective-permute-start | bytes 589832 | tf_op jit(solution)/shard_map/ppermute | solution.py:873
  6.7 32.4 %collective-permute-start.3 = (bf16[128,768]{1,0:T(8,128)(2,1)S(1)}, bf16[128,768]{1,0:T(8,128)(2,1)S(1)}, u32[]{:S(2)}, u32[]{:S(2)}) collective-permute-start(bf16[128,768]{1,0:T(8,128)(2,1)S(1)} %fusion.5.refs_4_), channel_id=1, source_target_pairs={{0,8},{2,10},{4,12},{6,14},{8,0},{10,2},{12,4},{14,6},{16,24},{18,... | collective-permute-start | bytes 589832 | tf_op jit(solution)/shard_map/ppermute | solution.py:873
  9.2 9.4 %collective-permute-start.6 = (f32[9984]{0:T(1024)S(1)}, f32[9984]{0:T(1024)S(1)}, u32[]{:S(2)}, u32[]{:S(2)}) collective-permute-start(f32[9984]{0:T(1024)S(1)} %slice.18), channel_id=1, source_target_pairs={{0,1},{1,2},{2,3},{3,4},{4,5},{5,6},{6,7},{7,8},{8,9},{9,10},{10,1... | collective-permute-start | bytes 119816 | tf_op jit(solution)/shard_map/ppermute | solution.py:284
  32.2 16.2 %collective-permute-start.12 = (bf16[352,768]{1,0:T(8,128)(2,1)S(1)}, bf16[352,768]{1,0:T(8,128)(2,1)S(1)}, u32[]{:S(2)}, u32[]{:S(2)}) collective-permute-start(bf16[352,768]{1,0:T(8,128)(2,1)S(1)} %shard_map.110.refs_8_), channel_id=1, source_target_pairs={{0,6},{2,4},{4,2},{6,0},{8,14},{10,12},{12,10},{14,8},{16,22},{18,... | collective-permute-start | bytes 1622024 | tf_op jit(solution)/shard_map/ppermute | solution.py:876
  32.4 25.2 %collective-permute-start.11 = (bf16[352,768]{1,0:T(8,128)(2,1)S(1)}, bf16[352,768]{1,0:T(8,128)(2,1)S(1)}, u32[]{:S(2)}, u32[]{:S(2)}) collective-permute-start(bf16[352,768]{1,0:T(8,128)(2,1)S(1)} %shard_map.110.refs_8_), channel_id=1, source_target_pairs={{0,4},{2,6},{4,0},{6,2},{8,12},{10,14},{12,8},{14,10},{16,20},{18,... | collective-permute-start | bytes 1622024 | tf_op jit(solution)/shard_map/ppermute | solution.py:876
  32.7 25.1 %collective-permute-start.10 = (bf16[352,768]{1,0:T(8,128)(2,1)S(1)}, bf16[352,768]{1,0:T(8,128)(2,1)S(1)}, u32[]{:S(2)}, u32[]{:S(2)}) collective-permute-start(bf16[352,768]{1,0:T(8,128)(2,1)S(1)} %shard_map.110.refs_8_), channel_id=1, source_target_pairs={{0,2},{2,0},{4,6},{6,4},{8,10},{10,8},{12,14},{14,12},{16,18},{18,... | collective-permute-start | bytes 1622024 | tf_op jit(solution)/shard_map/ppermute | solution.py:876
  36.0 11.2 %collective-permute-start.1 = (bf16[144,768]{1,0:T(8,128)(2,1)S(1)}, bf16[144,768]{1,0:T(8,128)(2,1)S(1)}, u32[]{:S(2)}, u32[]{:S(2)}) collective-permute-start(bf16[144,768]{1,0:T(8,128)(2,1)S(1)} %fusion.7.refs_0_), channel_id=1, source_target_pairs={{0,16},{2,18},{4,20},{6,22},{8,24},{10,26},{12,28},{14,30},{16,0},... | collective-permute-start | bytes 663560 | tf_op jit(solution)/shard_map/ppermute | solution.py:873
  39.8 18.4 %collective-permute-start = (bf16[144,768]{1,0:T(8,128)(2,1)S(1)}, bf16[144,768]{1,0:T(8,128)(2,1)S(1)}, u32[]{:S(2)}, u32[]{:S(2)}) collective-permute-start(bf16[144,768]{1,0:T(8,128)(2,1)S(1)} %fusion.7.refs_0_), channel_id=1, source_target_pairs={{0,8},{2,10},{4,12},{6,14},{8,0},{10,2},{12,4},{14,6},{16,24},{18,... | collective-permute-start | bytes 663560 | tf_op jit(solution)/shard_map/ppermute | solution.py:873
  47.2 26.0 %collective-permute-start.13 = (bf16[352,768]{1,0:T(8,128)(2,1)S(1)}, bf16[352,768]{1,0:T(8,128)(2,1)S(1)}, u32[]{:S(2)}, u32[]{:S(2)}) collective-permute-start(bf16[352,768]{1,0:T(8,128)(2,1)S(1)} %shard_map.110.refs_8_), channel_id=1, source_target_pairs={{0,1},{1,0},{2,3},{3,2},{4,5},{5,4},{6,7},{7,6},{8,9},{9,8},{10,11... | collective-permute-start | bytes 1622024 | tf_op jit(solution)/shard_map/ppermute | solution.py:879
  48.4 24.8 %collective-permute-start.16 = (bf16[352,768]{1,0:T(8,128)(2,1)S(1)}, bf16[352,768]{1,0:T(8,128)(2,1)S(1)}, u32[]{:S(2)}, u32[]{:S(2)}) collective-permute-start(bf16[352,768]{1,0:T(8,128)(2,1)S(1)} %collective-permute-done.12.refs_11_), channel_id=1, source_target_pairs={{0,1},{1,0},{2,3},{3,2},{4,5},{5,4},{6,7},{7,6},{8,9},{9,8},{10,11... | collective-permute-start | bytes 1622024 | tf_op jit(solution)/shard_map/ppermute | solution.py:879
  57.6 15.5 %collective-permute-start.15 = (bf16[352,768]{1,0:T(8,128)(2,1)S(1)}, bf16[352,768]{1,0:T(8,128)(2,1)S(1)}, u32[]{:S(2)}, u32[]{:S(2)}) collective-permute-start(bf16[352,768]{1,0:T(8,128)(2,1)S(1)} %collective-permute-done.11.refs_10_), channel_id=1, source_target_pairs={{0,1},{1,0},{2,3},{3,2},{4,5},{5,4},{6,7},{7,6},{8,9},{9,8},{10,11... | collective-permute-start | bytes 1622024 | tf_op jit(solution)/shard_map/ppermute | solution.py:879
  57.8 15.4 %collective-permute-start.14 = (bf16[352,768]{1,0:T(8,128)(2,1)S(1)}, bf16[352,768]{1,0:T(8,128)(2,1)S(1)}, u32[]{:S(2)}, u32[]{:S(2)}) collective-permute-start(bf16[352,768]{1,0:T(8,128)(2,1)S(1)} %collective-permute-done.10.refs_9_), channel_id=1, source_target_pairs={{0,1},{1,0},{2,3},{3,2},{4,5},{5,4},{6,7},{7,6},{8,9},{9,8},{10,11... | collective-permute-start | bytes 1622024 | tf_op jit(solution)/shard_map/ppermute | solution.py:879
  58.2 8.2 %collective-permute-start.5 = (bf16[128,768]{1,0:T(8,128)(2,1)S(1)}, bf16[128,768]{1,0:T(8,128)(2,1)S(1)}, u32[]{:S(2)}, u32[]{:S(2)}) collective-permute-start(bf16[128,768]{1,0:T(8,128)(2,1)S(1)} %collective-permute-done.4.refs_6_), channel_id=1, source_target_pairs={{0,8},{2,10},{4,12},{6,14},{8,0},{10,2},{12,4},{14,6},{16,24},{18,... | collective-permute-start | bytes 589832 | tf_op jit(solution)/shard_map/ppermute | solution.py:873
  97.0 12.2 %collective-permute-start.18 = (bf16[256,768]{1,0:T(8,128)(2,1)}, bf16[256,768]{1,0:T(8,128)(2,1)S(1)}, u32[]{:S(2)}, u32[]{:S(2)}) collective-permute-start(bf16[256,768]{1,0:T(8,128)(2,1)} %get-tuple-element.35), channel_id=1, source_target_pairs={{0,8},{2,10},{4,12},{6,14},{8,0},{10,2},{12,4},{14,6},{16,24},{18,... | collective-permute-start | bytes 1179656 | tf_op jit(solution)/shard_map/ppermute | solution.py:873
  98.4 11.9 %collective-permute-start.21 = (bf16[352,768]{1,0:T(8,128)(2,1)}, bf16[352,768]{1,0:T(8,128)(2,1)}, u32[]{:S(2)}, u32[]{:S(2)}) collective-permute-start(bf16[352,768]{1,0:T(8,128)(2,1)} %get-tuple-element.39), channel_id=1, source_target_pairs={{0,1},{1,0},{2,3},{3,2},{4,5},{5,4},{6,7},{7,6},{8,9},{9,8},{10,11... | collective-permute-start | bytes 1622024 | tf_op jit(solution)/shard_map/ppermute | solution.py:879
  98.4 14.1 %collective-permute-start.23 = (bf16[352,768]{1,0:T(8,128)(2,1)}, bf16[352,768]{1,0:T(8,128)(2,1)S(1)}, u32[]{:S(2)}, u32[]{:S(2)}) collective-permute-start(bf16[352,768]{1,0:T(8,128)(2,1)} %get-tuple-element.41), channel_id=1, source_target_pairs={{0,1},{1,0},{2,3},{3,2},{4,5},{5,4},{6,7},{7,6},{8,9},{9,8},{10,11... | collective-permute-start | bytes 1622024 | tf_op jit(solution)/shard_map/ppermute | solution.py:879
  99.0 17.8 %collective-permute-start.17 = (bf16[256,768]{1,0:T(8,128)(2,1)}, bf16[256,768]{1,0:T(8,128)(2,1)S(1)}, u32[]{:S(2)}, u32[]{:S(2)}) collective-permute-start(bf16[256,768]{1,0:T(8,128)(2,1)} %copy-done.13), channel_id=1, source_target_pairs={{0,8},{2,10},{4,12},{6,14},{8,0},{10,2},{12,4},{14,6},{16,24},{18,... | collective-permute-start | bytes 1179656 | tf_op jit(solution)/shard_map/ppermute | solution.py:873
  99.5 15.8 %collective-permute-start.20 = (bf16[352,768]{1,0:T(8,128)(2,1)}, bf16[352,768]{1,0:T(8,128)(2,1)S(1)}, u32[]{:S(2)}, u32[]{:S(2)}) collective-permute-start(bf16[352,768]{1,0:T(8,128)(2,1)} %copy-done.11), channel_id=1, source_target_pairs={{0,1},{1,0},{2,3},{3,2},{4,5},{5,4},{6,7},{7,6},{8,9},{9,8},{10,11... | collective-permute-start | bytes 1622024 | tf_op jit(solution)/shard_map/ppermute | solution.py:879
  110.3 20.9 %collective-permute-start.19 = (bf16[256,768]{1,0:T(8,128)(2,1)S(1)}, bf16[256,768]{1,0:T(8,128)(2,1)S(1)}, u32[]{:S(2)}, u32[]{:S(2)}) collective-permute-start(bf16[256,768]{1,0:T(8,128)(2,1)S(1)} %add_convert_fusion.4), channel_id=1, source_target_pairs={{0,16},{2,18},{4,20},{6,22},{8,24},{10,26},{12,28},{14,30},{16,0},... | collective-permute-start | bytes 1179656 | tf_op jit(solution)/shard_map/ppermute | solution.py:873
  112.5 19.1 %collective-permute-start.22 = (bf16[352,768]{1,0:T(8,128)(2,1)S(1)}, bf16[352,768]{1,0:T(8,128)(2,1)S(1)}, u32[]{:S(2)}, u32[]{:S(2)}) collective-permute-start(bf16[352,768]{1,0:T(8,128)(2,1)S(1)} %add_convert_fusion.2), channel_id=1, source_target_pairs={{0,2},{2,0},{4,6},{6,4},{8,10},{10,8},{12,14},{14,12},{16,18},{18,... | collective-permute-start | bytes 1622024 | tf_op jit(solution)/shard_map/ppermute | solution.py:876
  114.9 25.8 %collective-permute-start.24 = (bf16[352,768]{1,0:T(8,128)(2,1)S(1)}, bf16[352,768]{1,0:T(8,128)(2,1)S(1)}, u32[]{:S(2)}, u32[]{:S(2)}) collective-permute-start(bf16[352,768]{1,0:T(8,128)(2,1)S(1)} %add_convert_fusion.1), channel_id=1, source_target_pairs={{0,4},{2,6},{4,0},{6,2},{8,12},{10,14},{12,8},{14,10},{16,20},{18,... | collective-permute-start | bytes 1622024 | tf_op jit(solution)/shard_map/ppermute | solution.py:876
  115.3 25.3 %collective-permute-start.26 = (bf16[352,768]{1,0:T(8,128)(2,1)S(1)}, bf16[352,768]{1,0:T(8,128)(2,1)S(1)}, u32[]{:S(2)}, u32[]{:S(2)}) collective-permute-start(bf16[352,768]{1,0:T(8,128)(2,1)S(1)} %add_convert_fusion), channel_id=1, source_target_pairs={{0,6},{2,4},{4,2},{6,0},{8,14},{10,12},{12,10},{14,8},{16,22},{18,... | collective-permute-start | bytes 1622024 | tf_op jit(solution)/shard_map/ppermute | solution.py:876
  142.8 13.5 %collective-permute-start.28 = (bf16[96,768]{1,0:T(8,128)(2,1)S(1)}, bf16[96,768]{1,0:T(8,128)(2,1)S(1)}, u32[]{:S(2)}, u32[]{:S(2)}) collective-permute-start(bf16[96,768]{1,0:T(8,128)(2,1)S(1)} %get-tuple-element.46), channel_id=1, source_target_pairs={{0,16},{2,18},{4,20},{6,22},{8,24},{10,26},{12,28},{14,30},{16,0},... | collective-permute-start | bytes 442376 | tf_op jit(solution)/shard_map/ppermute | solution.py:873
  145.3 10.9 %collective-permute-start.29 = (bf16[96,768]{1,0:T(8,128)(2,1)S(1)}, bf16[96,768]{1,0:T(8,128)(2,1)S(1)}, u32[]{:S(2)}, u32[]{:S(2)}) collective-permute-start(bf16[96,768]{1,0:T(8,128)(2,1)S(1)} %get-tuple-element.47), channel_id=1, source_target_pairs={{0,24},{2,26},{4,28},{6,30},{8,16},{10,18},{12,20},{14,22},{16,8},... | collective-permute-start | bytes 442376 | tf_op jit(solution)/shard_map/ppermute | solution.py:873
  (26 other events, 147.5 us)

commit v6 on v5

--- a/solution.py
+++ b/solution.py
@@ -323,6 +323,7 @@
 PART = D // PLANES
 SPOT = 96
 SLAB = 352
+EARLY = 80
 STARTS = (0, 80, 176, 256)
 
 
@@ -459,10 +460,10 @@
         order_columns(perm, False)
         by_hidden = dot_nn(upper, perm[...])
         for s in range(PLANES):
-            spot[s, 72:73, :] = spread_groups([by_hidden[4 + j : 5 + j] for j in range(4)], s)
-            spot[s, 73:74, :] = spread_groups([by_head[j : j + 1] for j in range(3)], s)
-            spot[s, 74:75, :] = tail_ref[3:4, :]
-            spot[s, 80:88, :] = tail_ref[8:16, :]
+            spot[s, 80:81, :] = spread_groups([by_hidden[4 + j : 5 + j] for j in range(4)], s)
+            spot[s, 81:82, :] = spread_groups([by_head[j : j + 1] for j in range(3)], s)
+            spot[s, 82:83, :] = tail_ref[3:4, :]
+            spot[s, 88:96, :] = tail_ref[8:16, :]
 
     for r in range(PLANES):
         out_refs[r][...] = spot[plane ^ r].astype(BF)
@@ -545,17 +546,17 @@
     @pl.when(device == 31)
     def _():
         order_columns(perm, False)
-        whole = [spot[s, 72:73, :] for s in range(PLANES)]
+        whole = [spot[s, 80:81, :] for s in range(PLANES)]
         for j in range(4):
             row = jnp.broadcast_to(spread_groups(whole, j), (8, D)).astype(BF)
             tail_ref[4 + j : 5 + j, :] = dot_nt(row, perm[...])[0:1]
         order_columns(perm, True)
-        whole = [spot[s, 73:74, :] for s in range(PLANES)]
+        whole = [spot[s, 81:82, :] for s in range(PLANES)]
         for j in range(3):
             row = jnp.broadcast_to(spread_groups(whole, j), (8, D)).astype(BF)
             tail_ref[j : j + 1, :] = dot_nt(row, perm[...])[0:1]
-        tail_ref[3:4, :] = sum(spot[s, 74:75, :] for s in range(PLANES))
-        tail_ref[8:16, :] = sum(spot[s, 80:88, :] for s in range(PLANES))
+        tail_ref[3:4, :] = sum(spot[s, 82:83, :] for s in range(PLANES))
+        tail_ref[8:16, :] = sum(spot[s, 88:96, :] for s in range(PLANES))
 
 
 def slab_start(plane):
@@ -563,55 +564,74 @@
     return pl.multiple_of(jnp.where(plane == 0, 0, start), 16)
 
 
-def slab_kernel(where_ref, a_ref, b_ref, c_ref, d_ref, out_ref):
-    for r, ref in enumerate((a_ref, b_ref, c_ref, d_ref)):
+def slab_kernel(where_ref, *refs):
+    in_refs, (first, second) = refs[:PLANES], refs[PLANES:]
+    for r, ref in enumerate(in_refs):
         source = where_ref[0] ^ r
-        out_ref[pl.ds(slab_start(source), 80), :] = ref[0:80, :]
-
-        @pl.when((source == 1) | (source == 3))
-        def _():
-            out_ref[pl.ds(slab_start(source) + 80, 16), :] = ref[80:96, :]
-
-
-def split_kernel(where_ref, a_ref, b_ref, c_ref, d_ref, *outs):
-    out_refs, total = outs[:PLANES], outs[PLANES]
-    total[...] = (a_ref[...].astype(F32) + b_ref[...].astype(F32)) + (
-        c_ref[...].astype(F32) + d_ref[...].astype(F32)
-    )
+
+        @pl.when(source == 0)
+        def _():
+            first[0:80, :] = ref[0:80, :]
+
+        @pl.when(source == 1)
+        def _():
+            first[80:176, :] = ref[...]
+
+        @pl.when(source == 2)
+        def _():
+            second[0:80, :] = ref[0:80, :]
+
+        @pl.when(source == 3)
+        def _():
+            second[80:160, :] = ref[0:80, :]
+            first[176:192, :] = ref[80:96, :]
+
+
+def split_kernel(where_ref, *refs):
+    early, late, out_refs, total = refs[:4], refs[4:8], refs[8:12], refs[12]
+
+    def sum_of(parts):
+        a, b, c, d = (part[...].astype(F32) for part in parts)
+        return (a + b) + (c + d)
+
+    total[0:EARLY, :] = sum_of(early)
+    total[EARLY:SLAB, :] = sum_of(late)
     for r in range(PLANES):
         out_refs[r][...] = total[pl.ds(slab_start(where_ref[0] ^ r), SPOT), :].astype(BF)
 
 
-def layer_kernel(where_ref, *refs):
-    act_refs, cot_refs, slab_refs = refs[:4], refs[4:8], refs[8:16]
-    grad_refs, back_refs = refs[16:24], refs[24:28]
-    (w_up, w_down, w_out, packed, w_qkv, tails, bf_up, bf_down, bf_out, bf_qkv, normed, grad_y,
-     qkv, attn, g_qkv, g_attn, up, slab) = refs[28:]
+def place_of(index, spot, core):
+    return 2 * (spot ^ (index % 4)) + (core if index < 4 else 1 - core)
+
+
+def row_sum(x):
+    return jnp.sum(x, axis=0, keepdims=True)
+
+
+def attention_kernel(where_ref, *refs):
+    act_refs, cot_refs, slab_refs, grad_refs = refs[:4], refs[4:8], refs[8:16], refs[16:24]
+    (y_ref, dn_ref, g_out_ref, up_low, tails, g_tails, normed, grad_y,
+     w_out, packed, w_qkv, bf_out, bf_qkv, qkv, attn, g_qkv, g_attn) = refs[24:]
     plane, spot, core = where_ref[0], where_ref[1], where_ref[2]
     lane = lanes_of(D)
 
-    def place_of(index):
-        return 2 * (spot ^ (index % 4)) + (core if index < 4 else 1 - core)
-
     w_out[...] = jnp.zeros_like(w_out)
     for index, ref in enumerate(slab_refs):
-        q = place_of(index)
+        q = place_of(index, spot, core)
         for i in range(3):
             for j in range(3):
                 packed[j, pl.ds(pl.multiple_of(24 * q + 8 * i, 8), 8), :] = ref[0:80, :][
                     24 * i + 8 * j : 24 * i + 8 * j + 8
                 ].astype(F32)
         one = ref[80:176, :].astype(F32)
-        two = ref[176:256, :].astype(F32)
-        three = ref[256:352, :].astype(F32)
 
         @pl.when(q >= 3)
         def _():
-            w_up[pl.ds(pl.multiple_of(72 * q - 192, 8), 72), :] = one[0:72]
+            up_low[pl.ds(pl.multiple_of(72 * q - 192, 8), 72), :] = one[0:72]
 
         @pl.when(q == 2)
         def _():
-            w_up[0:24, :] = one[0:24]
+            up_low[0:24, :] = one[0:24]
 
             @pl.when(plane < 3)
             def _():
@@ -625,39 +645,21 @@
         def _():
             w_out[pl.ds(pl.multiple_of(96 * q, 8), 96), :] = one[0:96]
 
-        @pl.when(q < 5)
-        def _():
-            w_up[pl.ds(pl.multiple_of(384 + 72 * q, 8), 72), :] = two[0:72]
-
-        @pl.when(q == 5)
-        def _():
-            w_up[744:768, :] = two[0:24]
-            w_down[0:48, :] = two[24:72]
-
-        @pl.when(q > 5)
-        def _():
-            w_down[pl.ds(pl.multiple_of(72 * q - 384, 8), 72), :] = two[0:72]
-
-        w_down[pl.ds(pl.multiple_of(192 + 72 * q, 8), 72), :] = three[0:72]
-
         @pl.when(q == 7)
         def _():
-            tails[...] = three[72:88]
+            tails[...] = ref[176:192, :].astype(F32)
 
     for j in range(3):
         for i in range(4):
             moved = turned(packed[j], -PART * i)[:, 0:256]
             moved = jnp.where(lanes_of(256) < PART, moved, 0.0)
             w_qkv[:, i, :, 256 * j : 256 * j + 256] = moved.reshape(24, 8, 256)
-    bf_up[...] = w_up[...].astype(BF)
-    bf_down[...] = w_down[...].astype(BF)
     bf_out[...] = w_out[...].astype(BF)
     bf_qkv[...] = w_qkv[...].reshape(D, D).astype(BF)
 
     for r in range(4):
         normed[128 * r : 128 * r + 128, :] = act_refs[r][0:128, :]
         grad_y[128 * r : 128 * r + 128, :] = cot_refs[r][...]
-    bias_up = tails[0:1, :]
     flat_bias = tails[1:2, :]
     bias_qkv = jnp.zeros((1, D), F32)
     for j in range(3):
@@ -665,12 +667,8 @@
         bias_qkv = jnp.where(keep, turned(flat_bias, 64 * j), bias_qkv)
     bias_y = jnp.where(plane == 0, tails[2:3, :] + tails[8:9, :], 0.0)
     gain_one, shift_one = tails[9:10, :], tails[10:11, :]
-    gain_two, shift_two = tails[11:12, :], tails[12:13, :]
-
-    def act_of(gain, shift):
-        return (normed[...].astype(F32) * gain + shift).astype(BF)
-
-    act_one = act_of(gain_one, shift_one)
+    wide = normed[...].astype(F32)
+    act_one = (wide * gain_one + shift_one).astype(BF)
     qkv[...] = dot_nn(act_one, bf_qkv[...]) + bias_qkv
     g_attn[...] = dot_nt(grad_y[...], bf_out[...]).astype(BF)
 
@@ -736,51 +734,24 @@
             g_qkv[span, at[0] : at[0] + 128] = unrotated(gq)
             g_qkv[span, at[1] : at[1] + 128] = unrotated(gk)
             g_qkv[span, at[2] : at[2] + 128] = gv
-    y = dot_nn(attn[...], bf_out[...]) + bias_y
-    grad_out = dot_tn(attn[...], grad_y[...])
+    y_ref[...] = dot_nn(attn[...], bf_out[...]) + bias_y
+    g_out_ref[...] = dot_tn(attn[...], grad_y[...])
     g_bias_qkv = jnp.sum(g_qkv[...], axis=0, keepdims=True)
     g_qkv_bf = g_qkv[...].astype(BF)
     w_qkv[...] = dot_tn(act_one, g_qkv_bf).reshape(24, 4, 8, D)
     g_act_one = dot_nt(g_qkv_bf, bf_qkv[...])
-    w_out[...] = grad_out
-
-    act_two = act_of(gain_two, shift_two)
-    up[...] = dot_nn(act_two, bf_up[...]) + bias_up
-    cdf = 0.5 * (1.0 + lax.erf(up[...] * 0.7071067811865476))
-    hidden = (up[...] * cdf).astype(BF)
-    y = y + dot_nn(hidden, bf_down[...])
-    for r in range(4):
-        back_refs[r][0:128, :] = y[128 * r : 128 * r + 128].astype(BF)
-    w_down[...] = dot_tn(hidden, grad_y[...])
-    pdf = jnp.exp(-0.5 * up[...] * up[...]) * 0.3989422804014327
-    g_up = dot_nt(grad_y[...], bf_down[...]) * (cdf + up[...] * pdf)
-    g_bias_up = jnp.sum(g_up, axis=0, keepdims=True)
-    g_up_bf = g_up.astype(BF)
-    w_up[...] = dot_tn(act_two, g_up_bf)
-    g_act_two = dot_nt(g_up_bf, bf_up[...])
-    wide = normed[...].astype(F32)
-    for r in range(4):
-        span = slice(128 * r, 128 * r + 128)
-        back_refs[r][128:256, :] = (g_act_one[span] * gain_one + g_act_two[span] * gain_two).astype(BF)
-
-    def row_sum(x):
-        return jnp.sum(x, axis=0, keepdims=True)
-
-    g_bias_y = row_sum(grad_y[0:128, :].astype(F32))
+    dn_ref[...] = g_act_one * gain_one
     flat_bias = jnp.zeros((1, D), F32)
     for j in range(3):
         keep = (lane >= PART * j) & (lane < PART * (j + 1))
         flat_bias = jnp.where(keep, turned(g_bias_qkv, -64 * j), flat_bias)
-    tails[...] = jnp.zeros_like(tails)
-    tails[0:1, :] = g_bias_up
-    tails[1:2, :] = flat_bias
-    tails[2:3, :] = g_bias_y
-    tails[8:9, :] = g_bias_y
-    tails[9:10, :] = row_sum(g_act_one * wide)
-    tails[10:11, :] = row_sum(g_act_one)
-    tails[11:12, :] = row_sum(g_act_two * wide)
-    tails[12:13, :] = row_sum(g_act_two)
-
+    g_bias_y = row_sum(grad_y[0:128, :].astype(F32))
+    g_tails[...] = jnp.zeros_like(g_tails)
+    g_tails[1:2, :] = flat_bias
+    g_tails[2:3, :] = g_bias_y
+    g_tails[8:9, :] = g_bias_y
+    g_tails[9:10, :] = row_sum(g_act_one * wide)
+    g_tails[10:11, :] = row_sum(g_act_one)
     for j in range(3):
         total = None
         for i in range(4):
@@ -791,45 +762,102 @@
             total = piece if total is None else total + piece
         packed[j] = total
     for index, ref in enumerate(grad_refs):
-        q = place_of(index)
-        for i in range(3):
-            for j in range(3):
-                slab[24 * i + 8 * j : 24 * i + 8 * j + 8, :] = packed[
-                    j, pl.ds(pl.multiple_of(24 * q + 8 * i, 8), 8), :
-                ]
+        q = place_of(index, spot, core)
+        pieces = [
+            packed[j, pl.ds(pl.multiple_of(24 * q + 8 * i, 8), 8), :]
+            for i in range(3)
+            for j in range(3)
+        ]
+        pieces.append(jnp.zeros((8, D), F32))
+        ref[...] = jnp.concatenate(pieces, axis=0).astype(BF)
+
+
+def feed_forward_kernel(where_ref, *refs):
+    (y_ref, dn_ref, g_out_ref, up_low, tails, g_tails, normed, grad_y) = refs[:8]
+    slab_refs, grad_refs, back_refs = refs[8:16], refs[16:24], refs[24:28]
+    w_up, w_down, bf_up, bf_down, up, slab = refs[28:]
+    plane, spot, core = where_ref[0], where_ref[1], where_ref[2]
+    w_up[0:384, :] = up_low[...]
+    for index, ref in enumerate(slab_refs):
+        q = place_of(index, spot, core)
+        two = ref[0:80, :].astype(F32)
+        three = ref[80:160, :].astype(F32)
+
+        @pl.when(q < 5)
+        def _():
+            w_up[pl.ds(pl.multiple_of(384 + 72 * q, 8), 72), :] = two[0:72]
+
+        @pl.when(q == 5)
+        def _():
+            w_up[744:768, :] = two[0:24]
+            w_down[0:48, :] = two[24:72]
+
+        @pl.when(q > 5)
+        def _():
+            w_down[pl.ds(pl.multiple_of(72 * q - 384, 8), 72), :] = two[0:72]
+
+        w_down[pl.ds(pl.multiple_of(192 + 72 * q, 8), 72), :] = three[0:72]
+
+    bf_up[...] = w_up[...].astype(BF)
+    bf_down[...] = w_down[...].astype(BF)
+    bias_up = tails[0:1, :]
+    gain_two, shift_two = tails[11:12, :], tails[12:13, :]
+    wide = normed[...].astype(F32)
+    act_two = (wide * gain_two + shift_two).astype(BF)
+    up[...] = dot_nn(act_two, bf_up[...]) + bias_up
+    cdf = 0.5 * (1.0 + lax.erf(up[...] * 0.7071067811865476))
+    hidden = (up[...] * cdf).astype(BF)
+    y = y_ref[...] + dot_nn(hidden, bf_down[...])
+    for r in range(4):
+        back_refs[r][0:128, :] = y[128 * r : 128 * r + 128].astype(BF)
+    w_down[...] = dot_tn(hidden, grad_y[...])
+    pdf = jnp.exp(-0.5 * up[...] * up[...]) * 0.3989422804014327
+    g_up = dot_nt(grad_y[...], bf_down[...]) * (cdf + up[...] * pdf)
+    g_bias_up = row_sum(g_up)
+    g_up_bf = g_up.astype(BF)
+    w_up[...] = dot_tn(act_two, g_up_bf)
+    g_act_two = dot_nt(g_up_bf, bf_up[...])
+    dn = dn_ref[...] + g_act_two * gain_two
+    for r in range(4):
+        back_refs[r][128:256, :] = dn[128 * r : 128 * r + 128].astype(BF)
+    slab[256:272, :] = g_tails[...]
+    slab[256:257, :] = g_bias_up
+    slab[267:268, :] = row_sum(g_act_two * wide)
+    slab[268:269, :] = row_sum(g_act_two)
+    for index, ref in enumerate(grad_refs):
+        q = place_of(index, spot, core)
 
         @pl.when(q >= 3)
         def _():
-            slab[80:152, :] = w_up[pl.ds(pl.multiple_of(72 * q - 192, 8), 72), :]
+            slab[0:72, :] = w_up[pl.ds(pl.multiple_of(72 * q - 192, 8), 72), :]
 
         @pl.when(q == 2)
         def _():
-            slab[80:104, :] = w_up[0:24, :]
-            slab[104:168, :] = w_out[128:192, :]
+            slab[0:24, :] = w_up[0:24, :]
+            slab[24:88, :] = g_out_ref[128:192, :]
 
         @pl.when((q < 2) & (plane < 3))
         def _():
-            slab[80:144, :] = w_out[pl.ds(pl.multiple_of(64 * q, 8), 64), :]
+            slab[0:64, :] = g_out_ref[pl.ds(pl.multiple_of(64 * q, 8), 64), :]
 
         @pl.when((q < 2) & (plane == 3))
         def _():
-            slab[80:176, :] = w_out[pl.ds(pl.multiple_of(96 * q, 8), 96), :]
+            slab[0:96, :] = g_out_ref[pl.ds(pl.multiple_of(96 * q, 8), 96), :]
 
         @pl.when(q < 5)
         def _():
-            slab[176:248, :] = w_up[pl.ds(pl.multiple_of(384 + 72 * q, 8), 72), :]
+            slab[96:168, :] = w_up[pl.ds(pl.multiple_of(384 + 72 * q, 8), 72), :]
 
         @pl.when(q == 5)
         def _():
-            slab[176:200, :] = w_up[744:768, :]
-            slab[200:248, :] = w_down[0:48, :]
+            slab[96:120, :] = w_up[744:768, :]
+            slab[120:168, :] = w_down[0:48, :]
 
         @pl.when(q > 5)
         def _():
-            slab[176:248, :] = w_down[pl.ds(pl.multiple_of(72 * q - 384, 8), 72), :]
-
-        slab[256:328, :] = w_down[pl.ds(pl.multiple_of(192 + 72 * q, 8), 72), :]
-        slab[328:344, :] = tails[...]
+            slab[96:168, :] = w_down[pl.ds(pl.multiple_of(72 * q - 384, 8), 72), :]
+
+        slab[176:248, :] = w_down[pl.ds(pl.multiple_of(192 + 72 * q, 8), 72), :]
         ref[...] = slab[...].astype(BF)
 
 
@@ -897,52 +925,78 @@
     rows, tail = rows_from_flat(params, spread, count)
     tail = jnp.pad(tail, ((0, 3), (0, 0)))
     spot_shape = jax.ShapeDtypeStruct((SPOT, D), BF)
-    slab_shape = jax.ShapeDtypeStruct((SLAB, D), BF)
+
+    def shaped(rows, kind=BF):
+        return jax.ShapeDtypeStruct((rows, D), kind)
+
     sort_scratch = [
         pltpu.VMEM((planes, SPOT, D), F32),
         pltpu.VMEM((D, D), BF),
         pltpu.VMEM(rows.shape, BF),
     ]
     spots = local_call(
-        pack_kernel, [spot_shape] * planes, sort_scratch, 12, True,
+        pack_kernel, [spot_shape] * planes, sort_scratch, 8, True,
         where_owner, rows, tail,
     )
     spots = [to_plane(spots[r], r) for r in range(planes)]
-    slab = local_call(slab_kernel, slab_shape, [], 8, True, where_owner, *spots)
-    slabs = [to_spot(slab, r) for r in range(places)]
-    slabs = slabs + [to_core(s) for s in slabs]
-
+    first, second = local_call(
+        slab_kernel, [shaped(192), shaped(160)], [], 8, True, where_owner, *spots
+    )
+    firsts = [to_spot(first, r) for r in range(places)]
+    seconds = [to_spot(second, r) for r in range(places)]
+    firsts = firsts + [to_core(x) for x in firsts]
     total = planes * tokens
     outs = local_call(
-        layer_kernel,
-        [slab_shape] * 8 + [jax.ShapeDtypeStruct((2 * tokens, D), BF)] * planes,
+        attention_kernel,
+        [shaped(EARLY)] * 8
+        + [
+            shaped(total, F32),
+            shaped(total, F32),
+            shaped(256, F32),
+            shaped(384, F32),
+            shaped(16, F32),
+            shaped(16, F32),
+            shaped(total),
+            shaped(total),
+        ],
         [
-            pltpu.VMEM((D, D), F32),
-            pltpu.VMEM((D, D), F32),
             pltpu.VMEM((256, D), F32),
             pltpu.VMEM((3, PART, D), F32),
             pltpu.VMEM((24, 4, 8, D), F32),
-            pltpu.VMEM((16, D), F32),
-            pltpu.VMEM((D, D), BF),
-            pltpu.VMEM((D, D), BF),
             pltpu.VMEM((256, D), BF),
             pltpu.VMEM((D, D), BF),
-            pltpu.VMEM((total, D), BF),
-            pltpu.VMEM((total, D), BF),
             pltpu.VMEM((total, D), F32),
             pltpu.VMEM((total, 256), BF),
             pltpu.VMEM((total, D), F32),
             pltpu.VMEM((total, 256), BF),
+        ],
+        28, True, where_spot, *acts, *cots, *firsts,
+    )
+    early, kept = outs[:8], outs[8:]
+
+    def summed(parts):
+        paired = [
+            (parts[r].astype(F32) + to_core(parts[4 + r]).astype(F32)).astype(BF)
+            for r in range(places)
+        ]
+        return [to_spot(paired[r], r) for r in range(places)]
+
+    early = summed(early)
+    seconds = seconds + [to_core(x) for x in seconds]
+    outs = local_call(
+        feed_forward_kernel,
+        [shaped(SLAB - EARLY)] * 8 + [shaped(2 * tokens)] * planes,
+        [
+            pltpu.VMEM((D, D), F32),
+            pltpu.VMEM((D, D), F32),
+            pltpu.VMEM((D, D), BF),
+            pltpu.VMEM((D, D), BF),
             pltpu.VMEM((total, D), F32),
-            pltpu.VMEM((SLAB, D), F32),
+            pltpu.VMEM((SLAB - EARLY, D), F32),
         ],
-        44, True, where_spot, *acts, *cots, *slabs,
-    )
-    grads, backs = outs[:8], outs[8:]
-    paired = [
-        (grads[r].astype(F32) + to_core(grads[4 + r]).astype(F32)).astype(BF) for r in range(places)
-    ]
-    arrived = [to_spot(paired[r], r) for r in range(places)]
+        28, True, where_spot, *kept, *seconds,
+    )
+    late, backs = summed(outs[:8]), outs[8:]
     passed = to_plane(backs[3], 1)
     backs = [
         backs[0],
@@ -950,7 +1004,7 @@
         to_plane((backs[2].astype(F32) + passed.astype(F32)).astype(BF), 2),
     ]
     spots = local_call(
-        split_kernel, [spot_shape] * planes, [pltpu.VMEM((SLAB, D), F32)], 12, True, where_owner, *arrived
+        split_kernel, [spot_shape] * planes, [pltpu.VMEM((SLAB, D), F32)], 12, True, where_owner, *early, *late
     )
     spots = [to_plane(spots[r], r) for r in range(planes)]
     grad_rows, grad_tail = local_call(

time: 166 us -> 189 us (1.14)
  starting transfers between devices: 34.1 us -> 48.8 us
  local copies, waits for them, and re-layouts: 9.84 us -> 17.8 us
  Pallas kernels: 22.2 us -> 24.1 us
    ppermute x6 -> x12, starting transfers between devices: 7.38 us -> 19.2 us  [to_spot(): return lax.ppermute(value, 'dp', within[r]) if r else value]
    ppermute x1, waiting for transfers between devices: 8.88 us -> 0.01 us  [rows_from_flat(): lax.ppermute(tail, AXES, [(i, (i + 1) % count) for i in range(count)])]
    unnamed x38 -> x62, local copies, waits for them, and re-layouts: 8.37 us -> 16.2 us
    ppermute x15, waiting for transfers between devices: 57.1 us -> 63.3 us  [to_plane(): return lax.ppermute(value, 'dp', across[r]) if r else value]
    ppermute x8 -> x16, starting transfers between devices: 1.03 us -> 3.5 us  [to_core(): return lax.ppermute(value, 'fsdp', [(0, 1), (1, 0)])]
    pallas_call x5 -> x6, Pallas kernels: 22.2 us -> 24.1 us  [local_call(): pl.pallas_call(kernel, out_shape=outs, in_specs=[pl.BlockSpec(memory_spac...]
    ppermute x6 -> x12, waiting for transfers between devices: 19.5 us -> 21 us  [to_spot(): return lax.ppermute(value, 'dp', within[r]) if r else value]
  transfers between devices with their start and end apart: 31 -> 45, of which waited for: 14 -> 12; matrix products, arithmetic and copies ran while one was open for 4% -> 4% of each run, Pallas kernels for 2% -> 11%
where the time goes in v6:
time: 189 us; the launch traced here: 188 us
  waiting for transfers between devices  85 us (45%)
  starting transfers between devices  48.8 us (26%)
  Pallas kernels  24.1 us (13%)
  local copies, waits for them, and re-layouts  17.8 us (9%)
  other arithmetic  11.1 us (6%)
    ppermute x15, waiting for transfers between devices, to_plane(): return lax.ppermute(value, 'dp', across[r]) if r else value  63.3 us
    ppermute x15, starting transfers between devices, to_plane(): return lax.ppermute(value, 'dp', across[r]) if r else value  25.5 us
    pallas_call x6, Pallas kernels, local_call(): pl.pallas_call(kernel, out_shape=outs, in_specs=[pl.BlockSpec(memory_spac...  24.1 us
    ppermute x12, waiting for transfers between devices, to_spot(): return lax.ppermute(value, 'dp', within[r]) if r else value  21 us
    ppermute x12, starting transfers between devices, to_spot(): return lax.ppermute(value, 'dp', within[r]) if r else value  19.2 us
    unnamed x62, local copies, waits for them, and re-layouts  16.2 us
    sub x1, other arithmetic, adam_update(): params - LEARN_RATE * (first_hat / (jnp.sqrt(second_hat) + ADAM_EPS) + WE...  4.39 us
  transfers between devices with their start and end apart: 45, of which 12 were waited for; matrix products, arithmetic and copies ran while one was open for 4% of the time, Pallas kernels for 11%

profile of v6, /device:TPU:0, one launch (start us, length us, event | category | flops | bytes accessed | tf_op | source)
XLA Modules:
  0.0 187.8 jit_solution(17159488662804103373)
XLA Ops:
  4.0 3.7 %collective-permute-start.4 = (bf16[128,768]{1,0:T(8,128)(2,1)S(1)}, bf16[128,768]{1,0:T(8,128)(2,1)S(1)}, u32[]{:S(2)}, u32[]{:S(2)}) collective-permute-start(bf16[128,768]{1,0:T(8,128)(2,1)S(1)} %fusion.5.refs_4_), channel_id=1, source_target_pairs={{0,16},{2,18},{4,20},{6,22},{8,24},{10,26},{12,28},{14,30},{16,0},... | collective-permute-start | bytes 589832 | tf_op jit(solution)/shard_map/ppermute | solution.py:901
  14.1 3.2 %collective-permute-start.9 = (bf16[96,768]{1,0:T(8,128)(2,1)S(1)}, bf16[96,768]{1,0:T(8,128)(2,1)S(1)}, u32[]{:S(2)}, u32[]{:S(2)}) collective-permute-start(bf16[96,768]{1,0:T(8,128)(2,1)S(1)} %get-tuple-element.49), channel_id=1, source_target_pairs={{0,24},{2,26},{4,28},{6,30},{8,16},{10,18},{12,20},{14,22},{16,8},... | collective-permute-start | bytes 442376 | tf_op jit(solution)/shard_map/ppermute | solution.py:901
  17.7 5.2 %collective-permute-done.7.refs_1_ = bf16[96,768]{1,0:T(8,128)(2,1)S(1)} collective-permute-done((bf16[96,768]{1,0:T(8,128)(2,1)S(1)}, bf16[96,768]{1,0:T(8,128)(2,1)S(1)}, u32[]{:S(2)}, u32[]{:S(2)}) %collective-permute-start.7) | collective-permute-done | bytes 147488 | tf_op jit(solution)/shard_map/ppermute | solution.py:901
  22.9 9.2 %collective-permute-done.8.refs_2_ = bf16[96,768]{1,0:T(8,128)(2,1)S(1)} collective-permute-done((bf16[96,768]{1,0:T(8,128)(2,1)S(1)}, bf16[96,768]{1,0:T(8,128)(2,1)S(1)}, u32[]{:S(2)}, u32[]{:S(2)}) %collective-permute-start.8) | collective-permute-done | bytes 147488 | tf_op jit(solution)/shard_map/ppermute | solution.py:901
  34.1 2.9 %collective-permute-start.19 = (bf16[160,768]{1,0:T(8,128)(2,1)}, bf16[160,768]{1,0:T(8,128)(2,1)}, u32[]{:S(2)}, u32[]{:S(2)}) collective-permute-start(bf16[160,768]{1,0:T(8,128)(2,1)} %get-tuple-element.59.refs_8_), channel_id=1, source_target_pairs={{0,6},{2,4},{4,2},{6,0},{8,14},{10,12},{12,10},{14,8},{16,22},{18,... | collective-permute-start | bytes 737288 | tf_op jit(solution)/shard_map/ppermute | solution.py:904
  37.0 3.7 %collective-permute-start.5 = (bf16[128,768]{1,0:T(8,128)(2,1)S(1)}, bf16[128,768]{1,0:T(8,128)(2,1)S(1)}, u32[]{:S(2)}, u32[]{:S(2)}) collective-permute-start(bf16[128,768]{1,0:T(8,128)(2,1)S(1)} %collective-permute-done.4.refs_6_), channel_id=1, source_target_pairs={{0,8},{2,10},{4,12},{6,14},{8,0},{10,2},{12,4},{14,6},{16,24},{18,... | collective-permute-start | bytes 589832 | tf_op jit(solution)/shard_map/ppermute | solution.py:901
  40.8 2.4 %collective-permute-start.11 = (bf16[192,768]{1,0:T(8,128)(2,1)S(1)}, bf16[192,768]{1,0:T(8,128)(2,1)S(1)}, u32[]{:S(2)}, u32[]{:S(2)}) collective-permute-start(bf16[192,768]{1,0:T(8,128)(2,1)S(1)} %get-tuple-element.50.refs_8_), channel_id=1, source_target_pairs={{0,4},{2,6},{4,0},{6,2},{8,12},{10,14},{12,8},{14,10},{16,20},{18,... | collective-permute-start | bytes 884744 | tf_op jit(solution)/shard_map/ppermute | solution.py:904
  44.9 3.0 %collective-permute-start.18 = (bf16[160,768]{1,0:T(8,128)(2,1)}, bf16[160,768]{1,0:T(8,128)(2,1)}, u32[]{:S(2)}, u32[]{:S(2)}) collective-permute-start(bf16[160,768]{1,0:T(8,128)(2,1)} %get-tuple-element.59.refs_8_), channel_id=1, source_target_pairs={{0,4},{2,6},{4,0},{6,2},{8,12},{10,14},{12,8},{14,10},{16,20},{18,... | collective-permute-start | bytes 737288 | tf_op jit(solution)/shard_map/ppermute | solution.py:904
  48.5 2.6 %collective-permute-start.17 = (bf16[160,768]{1,0:T(8,128)(2,1)}, bf16[160,768]{1,0:T(8,128)(2,1)}, u32[]{:S(2)}, u32[]{:S(2)}) collective-permute-start(bf16[160,768]{1,0:T(8,128)(2,1)} %get-tuple-element.59.refs_8_), channel_id=1, source_target_pairs={{0,2},{2,0},{4,6},{6,4},{8,10},{10,8},{12,14},{14,12},{16,18},{18,... | collective-permute-start | bytes 737288 | tf_op jit(solution)/shard_map/ppermute | solution.py:904
  51.1 9.9 %collective-permute-done.18.refs_10_ = bf16[160,768]{1,0:T(8,128)(2,1)} collective-permute-done((bf16[160,768]{1,0:T(8,128)(2,1)}, bf16[160,768]{1,0:T(8,128)(2,1)}, u32[]{:S(2)}, u32[]{:S(2)}) %collective-permute-start.18) | collective-permute-done | bytes 245792 | tf_op jit(solution)/shard_map/ppermute | solution.py:904
  61.7 3.8 %collective-permute-start.2 = (bf16[144,768]{1,0:T(8,128)(2,1)S(1)}, bf16[144,768]{1,0:T(8,128)(2,1)S(1)}, u32[]{:S(2)}, u32[]{:S(2)}) collective-permute-start(bf16[144,768]{1,0:T(8,128)(2,1)S(1)} %collective-permute-done.1.refs_2_), channel_id=1, source_target_pairs={{0,8},{2,10},{4,12},{6,14},{8,0},{10,2},{12,4},{14,6},{16,24},{18,... | collective-permute-start | bytes 663560 | tf_op jit(solution)/shard_map/ppermute | solution.py:901
  65.6 5.9 %collective-permute-done.2.refs_3_ = bf16[144,768]{1,0:T(8,128)(2,1)S(1)} collective-permute-done((bf16[144,768]{1,0:T(8,128)(2,1)S(1)}, bf16[144,768]{1,0:T(8,128)(2,1)S(1)}, u32[]{:S(2)}, u32[]{:S(2)}) %collective-permute-start.2) | collective-permute-done | bytes 221216 | tf_op jit(solution)/shard_map/ppermute | solution.py:901
  72.6 10.3 %shard_map.111 = (bf16[80,768]{1,0:T(8,128)(2,1)S(1)}, bf16[80,768]{1,0:T(8,128)(2,1)S(1)}, bf16[80,768]{1,0:T(8,128)(2,1)S(1)}, bf16[80,768]{1,0:T(8,128)(2,1)S...) custom-call(s32[3]{0:T(128)S(1)} %pad_add_fusion.where_ref, ...), custom_call_target="tpu_custom_call" | custom-call | tf_op jit(solution)/shard_map/pallas_call | solution.py:870
  99.7 7.4 %shard_map.112 = (bf16[272,768]{1,0:T(8,128)(2,1)S(1)}, bf16[272,768]{1,0:T(8,128)(2,1)S(1)}, bf16[272,768]{1,0:T(8,128)(2,1)S(1)}, bf16[272,768]{1,0:T(8,128)(2...) custom-call(s32[3]{0:T(128)S(1)} %pad_add_fusion.where_ref, ...), custom_call_target="tpu_custom_call" | custom-call | tf_op jit(solution)/shard_map/pallas_call | solution.py:870
  110.1 16.6 %collective-permute-done.25 = bf16[256,768]{1,0:T(8,128)(2,1)S(1)} collective-permute-done((bf16[256,768]{1,0:T(8,128)(2,1)S(1)}, bf16[256,768]{1,0:T(8,128)(2,1)S(1)}, u32[]{:S(2)}, u32[]{:S(2)}) %collective-permute-start.25) | collective-permute-done | bytes 393248 | tf_op jit(solution)/shard_map/ppermute | solution.py:901
  126.8 2.4 %collective-permute-start.29 = (bf16[80,768]{1,0:T(8,128)(2,1)S(1)}, bf16[80,768]{1,0:T(8,128)(2,1)S(1)}, u32[]{:S(2)}, u32[]{:S(2)}) collective-permute-start(bf16[80,768]{1,0:T(8,128)(2,1)S(1)} %add_convert_fusion.7), channel_id=1, source_target_pairs={{0,2},{2,0},{4,6},{6,4},{8,10},{10,8},{12,14},{14,12},{16,18},{18,... | collective-permute-start | bytes 368648 | tf_op jit(solution)/shard_map/ppermute | solution.py:904
  129.7 2.4 %collective-permute-start.26 = (bf16[256,768]{1,0:T(8,128)(2,1)S(1)}, bf16[256,768]{1,0:T(8,128)(2,1)S(1)}, u32[]{:S(2)}, u32[]{:S(2)}) collective-permute-start(bf16[256,768]{1,0:T(8,128)(2,1)S(1)} %add_convert_fusion.4), channel_id=1, source_target_pairs={{0,16},{2,18},{4,20},{6,22},{8,24},{10,26},{12,28},{14,30},{16,0},... | collective-permute-start | bytes 1179656 | tf_op jit(solution)/shard_map/ppermute | solution.py:901
  132.2 2.1 %collective-permute-start.36 = (bf16[272,768]{1,0:T(8,128)(2,1)S(1)}, bf16[272,768]{1,0:T(8,128)(2,1)S(1)}, u32[]{:S(2)}, u32[]{:S(2)}) collective-permute-start(bf16[272,768]{1,0:T(8,128)(2,1)S(1)} %add_convert_fusion.2), channel_id=1, source_target_pairs={{0,2},{2,0},{4,6},{6,4},{8,10},{10,8},{12,14},{14,12},{16,18},{18,... | collective-permute-start | bytes 1253384 | tf_op jit(solution)/shard_map/ppermute | solution.py:904
  135.0 15.3 %collective-permute-done.26 = bf16[256,768]{1,0:T(8,128)(2,1)S(1)} collective-permute-done((bf16[256,768]{1,0:T(8,128)(2,1)S(1)}, bf16[256,768]{1,0:T(8,128)(2,1)S(1)}, u32[]{:S(2)}, u32[]{:S(2)}) %collective-permute-start.26) | collective-permute-done | bytes 393248 | tf_op jit(solution)/shard_map/ppermute | solution.py:901
  153.7 11.0 %collective-permute-done.33.refs_3_ = bf16[80,768]{1,0:T(8,128)(2,1)S(1)} collective-permute-done((bf16[80,768]{1,0:T(8,128)(2,1)S(1)}, bf16[80,768]{1,0:T(8,128)(2,1)S(1)}, u32[]{:S(2)}, u32[]{:S(2)}) %collective-permute-start.33) | collective-permute-done | bytes 122912 | tf_op jit(solution)/shard_map/ppermute | solution.py:904
  166.0 2.6 %collective-permute-start.42 = (bf16[96,768]{1,0:T(8,128)(2,1)S(1)}, bf16[96,768]{1,0:T(8,128)(2,1)S(1)}, u32[]{:S(2)}, u32[]{:S(2)}) collective-permute-start(bf16[96,768]{1,0:T(8,128)(2,1)S(1)} %get-tuple-element.82), channel_id=1, source_target_pairs={{0,16},{2,18},{4,20},{6,22},{8,24},{10,26},{12,28},{14,30},{16,0},... | collective-permute-start | bytes 442376 | tf_op jit(solution)/shard_map/ppermute | solution.py:901
  170.4 2.5 %collective-permute-done.41.refs_1_ = bf16[96,768]{1,0:T(8,128)(2,1)S(1)} collective-permute-done((bf16[96,768]{1,0:T(8,128)(2,1)S(1)}, bf16[96,768]{1,0:T(8,128)(2,1)S(1)}, u32[]{:S(2)}, u32[]{:S(2)}) %collective-permute-start.41) | collective-permute-done | bytes 147488 | tf_op jit(solution)/shard_map/ppermute | solution.py:901
  172.9 6.2 %collective-permute-done.42.refs_2_ = bf16[96,768]{1,0:T(8,128)(2,1)S(1)} collective-permute-done((bf16[96,768]{1,0:T(8,128)(2,1)S(1)}, bf16[96,768]{1,0:T(8,128)(2,1)S(1)}, u32[]{:S(2)}, u32[]{:S(2)}) %collective-permute-start.42) | collective-permute-done | bytes 147488 | tf_op jit(solution)/shard_map/ppermute | solution.py:901
  183.4 4.4 %multiply_subtract_fusion = (f32[221496]{0:T(1024)}, f32[221496]{0:T(1024)}, f32[221496]{0:T(1024)}, f32[221496]{0:T(1024)}) fusion(f32[221496]{0:T(1024)S(1)} %copy-done.26, f32[221496]{0:T(1024)} %param.10, f32[221496]{0:T(1024)} %param.11, s32[]{:T(128)S(6)} %select_n.30, f32[9984]{0:T(1024)S(1)} %broadcast_select_fusion, f32[221184]{0:T(1024)S(1)} %reshape.100), kind=kLoop, calls=%fused_computation.7 | loop fusion | flops 3543936 | bytes 7126564 | tf_op jit(solution)/shard_map/sub | solution.py:271
  (173 shorter events, 48.0 us)
Async XLA Ops:
  4.0 33.1 %collective-permute-start.4 = (bf16[128,768]{1,0:T(8,128)(2,1)S(1)}, bf16[128,768]{1,0:T(8,128)(2,1)S(1)}, u32[]{:S(2)}, u32[]{:S(2)}) collective-permute-start(bf16[128,768]{1,0:T(8,128)(2,1)S(1)} %fusion.5.refs_4_), channel_id=1, source_target_pairs={{0,16},{2,18},{4,20},{6,22},{8,24},{10,26},{12,28},{14,30},{16,0},... | collective-permute-start | bytes 589832 | tf_op jit(solution)/shard_map/ppermute | solution.py:901
  13.5 18.6 %collective-permute-start.8 = (bf16[96,768]{1,0:T(8,128)(2,1)S(1)}, bf16[96,768]{1,0:T(8,128)(2,1)S(1)}, u32[]{:S(2)}, u32[]{:S(2)}) collective-permute-start(bf16[96,768]{1,0:T(8,128)(2,1)S(1)} %get-tuple-element.48), channel_id=1, source_target_pairs={{0,16},{2,18},{4,20},{6,22},{8,24},{10,26},{12,28},{14,30},{16,0},... | collective-permute-start | bytes 442376 | tf_op jit(solution)/shard_map/ppermute | solution.py:901
  14.1 18.7 %collective-permute-start.9 = (bf16[96,768]{1,0:T(8,128)(2,1)S(1)}, bf16[96,768]{1,0:T(8,128)(2,1)S(1)}, u32[]{:S(2)}, u32[]{:S(2)}) collective-permute-start(bf16[96,768]{1,0:T(8,128)(2,1)S(1)} %get-tuple-element.49), channel_id=1, source_target_pairs={{0,24},{2,26},{4,28},{6,30},{8,16},{10,18},{12,20},{14,22},{16,8},... | collective-permute-start | bytes 442376 | tf_op jit(solution)/shard_map/ppermute | solution.py:901
  17.4 23.4 %collective-permute-start.1 = (bf16[144,768]{1,0:T(8,128)(2,1)S(1)}, bf16[144,768]{1,0:T(8,128)(2,1)S(1)}, u32[]{:S(2)}, u32[]{:S(2)}) collective-permute-start(bf16[144,768]{1,0:T(8,128)(2,1)S(1)} %fusion.7.refs_0_), channel_id=1, source_target_pairs={{0,16},{2,18},{4,20},{6,22},{8,24},{10,26},{12,28},{14,30},{16,0},... | collective-permute-start | bytes 663560 | tf_op jit(solution)/shard_map/ppermute | solution.py:901
  22.9 17.8 %collective-permute-start.3 = (bf16[128,768]{1,0:T(8,128)(2,1)S(1)}, bf16[128,768]{1,0:T(8,128)(2,1)S(1)}, u32[]{:S(2)}, u32[]{:S(2)}) collective-permute-start(bf16[128,768]{1,0:T(8,128)(2,1)S(1)} %fusion.5.refs_4_), channel_id=1, source_target_pairs={{0,8},{2,10},{4,12},{6,14},{8,0},{10,2},{12,4},{14,6},{16,24},{18,... | collective-permute-start | bytes 589832 | tf_op jit(solution)/shard_map/ppermute | solution.py:901
  34.1 17.0 %collective-permute-start.19 = (bf16[160,768]{1,0:T(8,128)(2,1)}, bf16[160,768]{1,0:T(8,128)(2,1)}, u32[]{:S(2)}, u32[]{:S(2)}) collective-permute-start(bf16[160,768]{1,0:T(8,128)(2,1)} %get-tuple-element.59.refs_8_), channel_id=1, source_target_pairs={{0,6},{2,4},{4,2},{6,0},{8,14},{10,12},{12,10},{14,8},{16,22},{18,... | collective-permute-start | bytes 737288 | tf_op jit(solution)/shard_map/ppermute | solution.py:904
  40.8 20.4 %collective-permute-start.12 = (bf16[192,768]{1,0:T(8,128)(2,1)S(1)}, bf16[192,768]{1,0:T(8,128)(2,1)S(1)}, u32[]{:S(2)}, u32[]{:S(2)}) collective-permute-start(bf16[192,768]{1,0:T(8,128)(2,1)S(1)} %get-tuple-element.50.refs_8_), channel_id=1, source_target_pairs={{0,6},{2,4},{4,2},{6,0},{8,14},{10,12},{12,10},{14,8},{16,22},{18,... | collective-permute-start | bytes 884744 | tf_op jit(solution)/shard_map/ppermute | solution.py:904
  40.8 20.8 %collective-permute-start.11 = (bf16[192,768]{1,0:T(8,128)(2,1)S(1)}, bf16[192,768]{1,0:T(8,128)(2,1)S(1)}, u32[]{:S(2)}, u32[]{:S(2)}) collective-permute-start(bf16[192,768]{1,0:T(8,128)(2,1)S(1)} %get-tuple-element.50.refs_8_), channel_id=1, source_target_pairs={{0,4},{2,6},{4,0},{6,2},{8,12},{10,14},{12,8},{14,10},{16,20},{18,... | collective-permute-start | bytes 884744 | tf_op jit(solution)/shard_map/ppermute | solution.py:904
  71.5 20.9 %collective-permute-start.20 = (bf16[160,768]{1,0:T(8,128)(2,1)}, bf16[160,768]{1,0:T(8,128)(2,1)}, u32[]{:S(2)}, u32[]{:S(2)}) collective-permute-start(bf16[160,768]{1,0:T(8,128)(2,1)} %get-tuple-element.59.refs_8_), channel_id=1, source_target_pairs={{0,1},{1,0},{2,3},{3,2},{4,5},{5,4},{6,7},{7,6},{8,9},{9,8},{10,11... | collective-permute-start | bytes 737288 | tf_op jit(solution)/shard_map/ppermute | solution.py:907
  71.5 21.4 %collective-permute-start.23 = (bf16[160,768]{1,0:T(8,128)(2,1)}, bf16[160,768]{1,0:T(8,128)(2,1)}, u32[]{:S(2)}, u32[]{:S(2)}) collective-permute-start(bf16[160,768]{1,0:T(8,128)(2,1)} %collective-permute-done.19.refs_11_), channel_id=1, source_target_pairs={{0,1},{1,0},{2,3},{3,2},{4,5},{5,4},{6,7},{7,6},{8,9},{9,8},{10,11... | collective-permute-start | bytes 737288 | tf_op jit(solution)/shard_map/ppermute | solution.py:907
  72.0 20.9 %collective-permute-start.22 = (bf16[160,768]{1,0:T(8,128)(2,1)}, bf16[160,768]{1,0:T(8,128)(2,1)}, u32[]{:S(2)}, u32[]{:S(2)}) collective-permute-start(bf16[160,768]{1,0:T(8,128)(2,1)} %collective-permute-done.18.refs_10_), channel_id=1, source_target_pairs={{0,1},{1,0},{2,3},{3,2},{4,5},{5,4},{6,7},{7,6},{8,9},{9,8},{10,11... | collective-permute-start | bytes 737288 | tf_op jit(solution)/shard_map/ppermute | solution.py:907
  72.1 21.3 %collective-permute-start.21 = (bf16[160,768]{1,0:T(8,128)(2,1)}, bf16[160,768]{1,0:T(8,128)(2,1)}, u32[]{:S(2)}, u32[]{:S(2)}) collective-permute-start(bf16[160,768]{1,0:T(8,128)(2,1)} %collective-permute-done.17.refs_9_), channel_id=1, source_target_pairs={{0,1},{1,0},{2,3},{3,2},{4,5},{5,4},{6,7},{7,6},{8,9},{9,8},{10,11... | collective-permute-start | bytes 737288 | tf_op jit(solution)/shard_map/ppermute | solution.py:907
  92.4 16.8 %collective-permute-start.28 = (bf16[80,768]{1,0:T(8,128)(2,1)}, bf16[80,768]{1,0:T(8,128)(2,1)S(1)}, u32[]{:S(2)}, u32[]{:S(2)}) collective-permute-start(bf16[80,768]{1,0:T(8,128)(2,1)} %copy-done.22), channel_id=1, source_target_pairs={{0,1},{1,0},{2,3},{3,2},{4,5},{5,4},{6,7},{7,6},{8,9},{9,8},{10,11... | collective-permute-start | bytes 368648 | tf_op jit(solution)/shard_map/ppermute | solution.py:907
  92.9 17.0 %collective-permute-start.32 = (bf16[80,768]{1,0:T(8,128)(2,1)}, bf16[80,768]{1,0:T(8,128)(2,1)S(1)}, u32[]{:S(2)}, u32[]{:S(2)}) collective-permute-start(bf16[80,768]{1,0:T(8,128)(2,1)} %copy-done.20), channel_id=1, source_target_pairs={{0,1},{1,0},{2,3},{3,2},{4,5},{5,4},{6,7},{7,6},{8,9},{9,8},{10,11... | collective-permute-start | bytes 368648 | tf_op jit(solution)/shard_map/ppermute | solution.py:907
  107.1 27.3 %collective-permute-start.24 = (bf16[256,768]{1,0:T(8,128)(2,1)S(1)}, bf16[256,768]{1,0:T(8,128)(2,1)S(1)}, u32[]{:S(2)}, u32[]{:S(2)}) collective-permute-start(bf16[256,768]{1,0:T(8,128)(2,1)S(1)} %get-tuple-element.61), channel_id=1, source_target_pairs={{0,8},{2,10},{4,12},{6,14},{8,0},{10,2},{12,4},{14,6},{16,24},{18,... | collective-permute-start | bytes 1179656 | tf_op jit(solution)/shard_map/ppermute | solution.py:901
  108.9 17.8 %collective-permute-start.25 = (bf16[256,768]{1,0:T(8,128)(2,1)S(1)}, bf16[256,768]{1,0:T(8,128)(2,1)S(1)}, u32[]{:S(2)}, u32[]{:S(2)}) collective-permute-start(bf16[256,768]{1,0:T(8,128)(2,1)S(1)} %get-tuple-element.63), channel_id=1, source_target_pairs={{0,8},{2,10},{4,12},{6,14},{8,0},{10,2},{12,4},{14,6},{16,24},{18,... | collective-permute-start | bytes 1179656 | tf_op jit(solution)/shard_map/ppermute | solution.py:901
  109.3 17.6 %collective-permute-start.34 = (bf16[272,768]{1,0:T(8,128)(2,1)S(1)}, bf16[272,768]{1,0:T(8,128)(2,1)S(1)}, u32[]{:S(2)}, u32[]{:S(2)}) collective-permute-start(bf16[272,768]{1,0:T(8,128)(2,1)S(1)} %get-tuple-element.73), channel_id=1, source_target_pairs={{0,1},{1,0},{2,3},{3,2},{4,5},{5,4},{6,7},{7,6},{8,9},{9,8},{10,11... | collective-permute-start | bytes 1253384 | tf_op jit(solution)/shard_map/ppermute | solution.py:907
  109.4 19.9 %collective-permute-start.35 = (bf16[272,768]{1,0:T(8,128)(2,1)S(1)}, bf16[272,768]{1,0:T(8,128)(2,1)S(1)}, u32[]{:S(2)}, u32[]{:S(2)}) collective-permute-start(bf16[272,768]{1,0:T(8,128)(2,1)S(1)} %get-tuple-element.75), channel_id=1, source_target_pairs={{0,1},{1,0},{2,3},{3,2},{4,5},{5,4},{6,7},{7,6},{8,9},{9,8},{10,11... | collective-permute-start | bytes 1253384 | tf_op jit(solution)/shard_map/ppermute | solution.py:907
  110.0 19.7 %collective-permute-start.37 = (bf16[272,768]{1,0:T(8,128)(2,1)S(1)}, bf16[272,768]{1,0:T(8,128)(2,1)S(1)}, u32[]{:S(2)}, u32[]{:S(2)}) collective-permute-start(bf16[272,768]{1,0:T(8,128)(2,1)S(1)} %get-tuple-element.77), channel_id=1, source_target_pairs={{0,1},{1,0},{2,3},{3,2},{4,5},{5,4},{6,7},{7,6},{8,9},{9,8},{10,11... | collective-permute-start | bytes 1253384 | tf_op jit(solution)/shard_map/ppermute | solution.py:907
  126.8 25.1 %collective-permute-start.29 = (bf16[80,768]{1,0:T(8,128)(2,1)S(1)}, bf16[80,768]{1,0:T(8,128)(2,1)S(1)}, u32[]{:S(2)}, u32[]{:S(2)}) collective-permute-start(bf16[80,768]{1,0:T(8,128)(2,1)S(1)} %add_convert_fusion.7), channel_id=1, source_target_pairs={{0,2},{2,0},{4,6},{6,4},{8,10},{10,8},{12,14},{14,12},{16,18},{18,... | collective-permute-start | bytes 368648 | tf_op jit(solution)/shard_map/ppermute | solution.py:904
  129.3 24.4 %collective-permute-start.31 = (bf16[80,768]{1,0:T(8,128)(2,1)S(1)}, bf16[80,768]{1,0:T(8,128)(2,1)S(1)}, u32[]{:S(2)}, u32[]{:S(2)}) collective-permute-start(bf16[80,768]{1,0:T(8,128)(2,1)S(1)} %add_convert_fusion.6), channel_id=1, source_target_pairs={{0,4},{2,6},{4,0},{6,2},{8,12},{10,14},{12,8},{14,10},{16,20},{18,... | collective-permute-start | bytes 368648 | tf_op jit(solution)/shard_map/ppermute | solution.py:904
  129.7 20.6 %collective-permute-start.26 = (bf16[256,768]{1,0:T(8,128)(2,1)S(1)}, bf16[256,768]{1,0:T(8,128)(2,1)S(1)}, u32[]{:S(2)}, u32[]{:S(2)}) collective-permute-start(bf16[256,768]{1,0:T(8,128)(2,1)S(1)} %add_convert_fusion.4), channel_id=1, source_target_pairs={{0,16},{2,18},{4,20},{6,22},{8,24},{10,26},{12,28},{14,30},{16,0},... | collective-permute-start | bytes 1179656 | tf_op jit(solution)/shard_map/ppermute | solution.py:901
  132.2 32.6 %collective-permute-start.36 = (bf16[272,768]{1,0:T(8,128)(2,1)S(1)}, bf16[272,768]{1,0:T(8,128)(2,1)S(1)}, u32[]{:S(2)}, u32[]{:S(2)}) collective-permute-start(bf16[272,768]{1,0:T(8,128)(2,1)S(1)} %add_convert_fusion.2), channel_id=1, source_target_pairs={{0,2},{2,0},{4,6},{6,4},{8,10},{10,8},{12,14},{14,12},{16,18},{18,... | collective-permute-start | bytes 1253384 | tf_op jit(solution)/shard_map/ppermute | solution.py:904
  134.4 30.4 %collective-permute-start.38 = (bf16[272,768]{1,0:T(8,128)(2,1)S(1)}, bf16[272,768]{1,0:T(8,128)(2,1)S(1)}, u32[]{:S(2)}, u32[]{:S(2)}) collective-permute-start(bf16[272,768]{1,0:T(8,128)(2,1)S(1)} %add_convert_fusion.1), channel_id=1, source_target_pairs={{0,4},{2,6},{4,0},{6,2},{8,12},{10,14},{12,8},{14,10},{16,20},{18,... | collective-permute-start | bytes 1253384 | tf_op jit(solution)/shard_map/ppermute | solution.py:904
  (52 other events, 384.6 us)

commit v7 on v6

--- a/solution.py
+++ b/solution.py
@@ -390,8 +390,12 @@
     perm_ref[...] = jnp.where(row == source[0:1], 1.0, 0.0).astype(BF)
 
 
-def pack_kernel(where_ref, rows_ref, tail_ref, *refs):
-    out_refs, (spot, perm, mixed) = refs[:PLANES], refs[PLANES:]
+def pack_kernel(where_ref, lines_ref, tail_ref, *refs):
+    out_refs, (spot, perm, mixed, rows_ref) = refs[:PLANES], refs[PLANES:]
+    for j in range(D // 128):
+        rows_ref[:, 128 * j : 128 * j + 128] = lines_ref[
+            pl.ds(j, rows_ref.shape[0], stride=D // 128), :
+        ]
     plane, place = where_ref[0], where_ref[1]
     device = 8 * plane + place
     with_heads = device < 8
@@ -470,7 +474,7 @@
 
 
 def unpack_kernel(where_ref, *refs):
-    in_refs, (rows_ref, tail_ref, spot, perm, mixed) = refs[:PLANES], refs[PLANES:]
+    in_refs, (lines_ref, tail_ref, spot, perm, mixed, rows_ref) = refs[:PLANES], refs[PLANES:]
     plane, place = where_ref[0], where_ref[1]
     device = 8 * plane + place
     with_heads = device < 8
@@ -541,6 +545,10 @@
         for s in range(3):
             rows_ref[64 * s : 64 * s + 64, :] = spot[s, 24:88, :]
 
+    for j in range(D // 128):
+        lines_ref[pl.ds(j, rows_ref.shape[0], stride=D // 128), :] = rows_ref[
+            :, 128 * j : 128 * j + 128
+        ]
     tail_ref[...] = jnp.zeros_like(tail_ref)
 
     @pl.when(device == 31)
@@ -598,6 +606,31 @@
     total[EARLY:SLAB, :] = sum_of(late)
     for r in range(PLANES):
         out_refs[r][...] = total[pl.ds(slab_start(where_ref[0] ^ r), SPOT), :].astype(BF)
+
+
+def norm_kernel(seg_ref, x_ref, g_ref, act_ref, cot_ref, normed_ref, g_y_ref, inv_ref, segs):
+    micro, row_count = seg_ref.shape
+    segs[...] = jnp.zeros_like(segs)
+    segs[0:micro, 0:row_count] = seg_ref[...].astype(F32)
+    x = x_ref[...]
+    centred = x - jnp.mean(x, axis=1, keepdims=True)
+    inv = lax.rsqrt(jnp.mean(centred * centred, axis=1, keepdims=True) + NORM_EPS)
+    normed = centred * inv
+    normed_ref[...] = normed
+    inv_ref[...] = jnp.broadcast_to(inv, inv_ref.shape)
+    tokens = micro * row_count
+    act_ref[0:tokens, :] = normed.astype(BF)
+    act_ref[tokens:, :] = jnp.zeros((16, D), BF)
+    act_ref[tokens:, 0:128] = segs[...].astype(BF)
+    rows = lax.broadcasted_iota(jnp.int32, (row_count, 128), 0)
+    cols = lax.broadcasted_iota(jnp.int32, (row_count, 128), 1)
+    for m in range(micro):
+        own = jnp.where(rows == cols, jnp.broadcast_to(segs[m : m + 1, :], rows.shape), 0.0)
+        valid = jnp.sum(own, axis=1, keepdims=True) >= 0.0
+        span = slice(row_count * m, row_count * (m + 1))
+        g_y = jnp.where(valid, g_ref[span, :], 0.0)
+        g_y_ref[span, :] = g_y
+        cot_ref[span, :] = g_y.astype(BF)
 
 
 def place_of(index, spot, core):
@@ -681,7 +714,9 @@
     low_half = lanes_of(128) < 64
     for r in range(4):
         span = slice(128 * r, 128 * r + 128)
-        seg_row = jnp.broadcast_to(act_refs[r][128:144, 0:128].astype(F32)[0:1], (128, 128))
+        ids = act_refs[r][128:144, 0:128].astype(F32)
+        ids = jnp.where(low_half, ids[0:1], turned(ids[1:2], 64))
+        seg_row = jnp.broadcast_to(ids, (128, 128))
         seg_col = jnp.sum(jnp.where(eye, seg_row, 0.0), axis=1, keepdims=True)
         same = (seg_col == seg_row) & same_block
         allowed = same & (cols <= rows) & ((seg_col >= 0.0) | eye)
@@ -909,17 +944,31 @@
     micro, row_count, _ = block_input.shape
     tokens = micro * row_count
     flat_x = block_input.reshape(tokens, D)
-    mean = jnp.mean(flat_x, axis=-1, keepdims=True)
-    centred = flat_x - mean
-    inv_std = lax.rsqrt(jnp.mean(centred * centred, axis=-1, keepdims=True) + NORM_EPS)
-    normed = centred * inv_std
-    valid = (seg_ids >= 0).astype(F32).reshape(tokens, 1)
-    grad_y = out_grad.reshape(tokens, D) * valid
-    seg_rows = jnp.pad(seg_ids.reshape(1, tokens).astype(BF), ((0, 15), (0, D - tokens)))
-    sent_acts = jnp.concatenate([normed.astype(BF), seg_rows])
+    vmem = pl.BlockSpec(memory_space=pltpu.VMEM)
+    sent_acts, sent_cots, normed, grad_y, inv_std = pl.pallas_call(
+        norm_kernel,
+        out_shape=[
+            pltpu.VMEM((tokens + 16, D), BF),
+            pltpu.VMEM((tokens, D), BF),
+            jax.ShapeDtypeStruct((tokens, D), F32),
+            jax.ShapeDtypeStruct((tokens, D), F32),
+            jax.ShapeDtypeStruct((tokens, 128), F32),
+        ],
+        in_specs=[vmem] * 3,
+        out_specs=[vmem] * 5,
+        scratch_shapes=[pltpu.VMEM((16, 128), F32)],
+        compiler_params=pltpu.CompilerParams(vmem_limit_bytes=8 << 20),
+        name="norm",
+    )(
+        *(
+            pltpu.with_memory_space_constraint(x, pltpu.HBM)
+            for x in (seg_ids, flat_x, out_grad.reshape(tokens, D))
+        )
+    )
+    inv_std = inv_std[:, 0:1]
     acts = [to_plane(sent_acts, r) for r in range(3)]
     acts.append(to_plane(acts[2], 1))
-    cots = [to_plane(grad_y.astype(BF), r) for r in range(3)]
+    cots = [to_plane(sent_cots, r) for r in range(3)]
     cots.append(to_plane(cots[2], 1))
 
     rows, tail = rows_from_flat(params, spread, count)
@@ -933,10 +982,11 @@
         pltpu.VMEM((planes, SPOT, D), F32),
         pltpu.VMEM((D, D), BF),
         pltpu.VMEM(rows.shape, BF),
+        pltpu.VMEM(rows.shape, F32),
     ]
     spots = local_call(
-        pack_kernel, [spot_shape] * planes, sort_scratch, 8, True,
-        where_owner, rows, tail,
+        pack_kernel, [spot_shape] * planes, sort_scratch, 10, True,
+        where_owner, rows.reshape(-1, 128), tail,
     )
     spots = [to_plane(spots[r], r) for r in range(planes)]
     first, second = local_call(
@@ -1010,7 +1060,7 @@
     grad_rows, grad_tail = local_call(
         unpack_kernel,
         [
-            jax.ShapeDtypeStruct(rows.shape, F32),
+            jax.ShapeDtypeStruct((rows.size // 128, 128), F32),
             jax.ShapeDtypeStruct((16, D), F32),
         ],
         sort_scratch, 12, True,

time: 189 us -> 187 us (0.989)
  waiting for transfers between devices: 85 us -> 82.2 us
  other arithmetic: 11.1 us -> 8.66 us
    ppermute x15, waiting for transfers between devices: 63.3 us -> 54.1 us  [to_plane(): return lax.ppermute(value, 'dp', across[r]) if r else value]
    ppermute x1, waiting for transfers between devices: 0.01 us -> 7.49 us  [rows_from_flat(): lax.ppermute(tail, AXES, [(i, (i + 1) % count) for i in range(count)])]
    ppermute x12, starting transfers between devices: 19.2 us -> 16.2 us  [to_spot(): return lax.ppermute(value, 'dp', within[r]) if r else value]
    ppermute x15, starting transfers between devices: 25.5 us -> 28.4 us  [to_plane(): return lax.ppermute(value, 'dp', across[r]) if r else value]
    reduce_sum x2 -> x0, other arithmetic: 2.28 us -> none  [the longest x1 1.18 us: sliced_body(): jnp.mean(centred * centred, axis=-1, keepdims=True) + NORM_EPS]
    unnamed x62 -> x58, local copies, waits for them, and re-layouts: 16.2 us -> 17.1 us
  transfers between devices with their start and end apart: 45 -> 45, of which waited for: 12 -> 13; matrix products, arithmetic and copies ran while one was open for 4% -> 2% of each run, Pallas kernels for 11% -> 11%
where the time goes in v7:
time: 187 us; the launch traced here: 185 us
  waiting for transfers between devices  82.2 us (44%)
  starting transfers between devices  48.7 us (26%)
  Pallas kernels  25.8 us (14%)
  local copies, waits for them, and re-layouts  18.9 us (10%)
  other arithmetic  8.66 us (5%)
    ppermute x15, waiting for transfers between devices, to_plane(): return lax.ppermute(value, 'dp', across[r]) if r else value  54.1 us
    ppermute x15, starting transfers between devices, to_plane(): return lax.ppermute(value, 'dp', across[r]) if r else value  28.4 us
    pallas_call x6, Pallas kernels, local_call(): pl.pallas_call(kernel, out_shape=outs, in_specs=[pl.BlockSpec(memory_spac...  24.4 us
    ppermute x12, waiting for transfers between devices, to_spot(): return lax.ppermute(value, 'dp', within[r]) if r else value  20 us
    unnamed x58, local copies, waits for them, and re-layouts  17.1 us
    ppermute x12, starting transfers between devices, to_spot(): return lax.ppermute(value, 'dp', within[r]) if r else value  16.2 us
    ppermute x1, waiting for transfers between devices, rows_from_flat(): lax.ppermute(tail, AXES, [(i, (i + 1) % count) for i in range(count)])  7.49 us
    sub x1, other arithmetic, adam_update(): params - LEARN_RATE * (first_hat / (jnp.sqrt(second_hat) + ADAM_EPS) + WE...  4.14 us
  transfers between devices with their start and end apart: 45, of which 13 were waited for; matrix products, arithmetic and copies ran while one was open for 2% of the time, Pallas kernels for 11%

profile of v7, /device:TPU:0, one launch (start us, length us, event | category | flops | bytes accessed | tf_op | source)
XLA Modules:
  0.0 185.3 jit_solution(945760309976220739)
XLA Ops:
  2.1 7.5 %collective-permute-done.6 = f32[9984]{0:T(1024)S(1)} collective-permute-done((f32[9984]{0:T(1024)S(1)}, f32[9984]{0:T(1024)S(1)}, u32[]{:S(2)}, u32[]{:S(2)}) %collective-permute-start.6) | collective-permute-done | bytes 39968 | tf_op jit(solution)/shard_map/ppermute | solution.py:284
  11.1 1.9 %shard_map.109 = (bf16[96,768]{1,0:T(8,128)(2,1)S(1)}, bf16[96,768]{1,0:T(8,128)(2,1)S(1)}, bf16[96,768]{1,0:T(8,128)(2,1)S(1)}, bf16[96,768]{1,0:T(8,128)(2,1)S(1)}) custom-call(s32[2]{0:T(128)S(1)} %pad_add_fusion.1.where_ref, f32[1728,128]{1,0:T(8,128)S(1)} %fusion.3.lines_ref, f32[16,768]{1,0:T(8,128)S(1)} %pad.4.tail_ref), custom_call_target="tpu_custom_call" | custom-call | tf_op jit(solution)/shard_map/pallas_call | solution.py:905
  18.9 3.0 %collective-permute-start.9 = (bf16[96,768]{1,0:T(8,128)(2,1)S(1)}, bf16[96,768]{1,0:T(8,128)(2,1)S(1)}, u32[]{:S(2)}, u32[]{:S(2)}) collective-permute-start(bf16[96,768]{1,0:T(8,128)(2,1)S(1)} %get-tuple-element.56), channel_id=1, source_target_pairs={{0,24},{2,26},{4,28},{6,30},{8,16},{10,18},{12,20},{14,22},{16,8},... | collective-permute-start | bytes 442376 | tf_op jit(solution)/shard_map/ppermute | solution.py:936
  23.3 9.2 %collective-permute-done.8.refs_2_ = bf16[96,768]{1,0:T(8,128)(2,1)S(1)} collective-permute-done((bf16[96,768]{1,0:T(8,128)(2,1)S(1)}, bf16[96,768]{1,0:T(8,128)(2,1)S(1)}, u32[]{:S(2)}, u32[]{:S(2)}) %collective-permute-start.8) | collective-permute-done | bytes 147488 | tf_op jit(solution)/shard_map/ppermute | solution.py:936
  35.3 2.2 %collective-permute-start.19 = (bf16[160,768]{1,0:T(8,128)(2,1)}, bf16[160,768]{1,0:T(8,128)(2,1)}, u32[]{:S(2)}, u32[]{:S(2)}) collective-permute-start(bf16[160,768]{1,0:T(8,128)(2,1)} %get-tuple-element.66.refs_8_), channel_id=1, source_target_pairs={{0,6},{2,4},{4,2},{6,0},{8,14},{10,12},{12,10},{14,8},{16,22},{18,... | collective-permute-start | bytes 737288 | tf_op jit(solution)/shard_map/ppermute | solution.py:939
  38.2 7.3 %collective-permute-start.5 = (bf16[128,768]{1,0:T(8,128)(2,1)S(1)}, bf16[128,768]{1,0:T(8,128)(2,1)S(1)}, u32[]{:S(2)}, u32[]{:S(2)}) collective-permute-start(bf16[128,768]{1,0:T(8,128)(2,1)S(1)} %collective-permute-done.4.refs_6_), channel_id=1, source_target_pairs={{0,8},{2,10},{4,12},{6,14},{8,0},{10,2},{12,4},{14,6},{16,24},{18,... | collective-permute-start | bytes 589832 | tf_op jit(solution)/shard_map/ppermute | solution.py:936
  51.4 13.3 %collective-permute-done.18.refs_10_ = bf16[160,768]{1,0:T(8,128)(2,1)} collective-permute-done((bf16[160,768]{1,0:T(8,128)(2,1)}, bf16[160,768]{1,0:T(8,128)(2,1)}, u32[]{:S(2)}, u32[]{:S(2)}) %collective-permute-start.18) | collective-permute-done | bytes 245792 | tf_op jit(solution)/shard_map/ppermute | solution.py:939
  65.2 3.8 %collective-permute-start.2 = (bf16[144,768]{1,0:T(8,128)(2,1)S(1)}, bf16[144,768]{1,0:T(8,128)(2,1)S(1)}, u32[]{:S(2)}, u32[]{:S(2)}) collective-permute-start(bf16[144,768]{1,0:T(8,128)(2,1)S(1)} %collective-permute-done.1.refs_2_), channel_id=1, source_target_pairs={{0,8},{2,10},{4,12},{6,14},{8,0},{10,2},{12,4},{14,6},{16,24},{18,... | collective-permute-start | bytes 663560 | tf_op jit(solution)/shard_map/ppermute | solution.py:936
  69.2 5.9 %collective-permute-done.2.refs_3_ = bf16[144,768]{1,0:T(8,128)(2,1)S(1)} collective-permute-done((bf16[144,768]{1,0:T(8,128)(2,1)S(1)}, bf16[144,768]{1,0:T(8,128)(2,1)S(1)}, u32[]{:S(2)}, u32[]{:S(2)}) %collective-permute-start.2) | collective-permute-done | bytes 221216 | tf_op jit(solution)/shard_map/ppermute | solution.py:936
  76.1 10.5 %shard_map.111 = (bf16[80,768]{1,0:T(8,128)(2,1)S(1)}, bf16[80,768]{1,0:T(8,128)(2,1)S(1)}, bf16[80,768]{1,0:T(8,128)(2,1)S(1)}, bf16[80,768]{1,0:T(8,128)(2,1)S...) custom-call(s32[3]{0:T(128)S(1)} %pad_add_fusion.where_ref, ...), custom_call_target="tpu_custom_call" | custom-call | tf_op jit(solution)/shard_map/pallas_call | solution.py:905
  104.4 7.4 %shard_map.112 = (bf16[272,768]{1,0:T(8,128)(2,1)S(1)}, bf16[272,768]{1,0:T(8,128)(2,1)S(1)}, bf16[272,768]{1,0:T(8,128)(2,1)S(1)}, bf16[272,768]{1,0:T(8,128)(2...) custom-call(s32[3]{0:T(128)S(1)} %pad_add_fusion.where_ref, ...), custom_call_target="tpu_custom_call" | custom-call | tf_op jit(solution)/shard_map/pallas_call | solution.py:905
  111.8 1.8 collective-permute-start.24
  115.7 15.7 %collective-permute-done.25 = bf16[256,768]{1,0:T(8,128)(2,1)S(1)} collective-permute-done((bf16[256,768]{1,0:T(8,128)(2,1)S(1)}, bf16[256,768]{1,0:T(8,128)(2,1)S(1)}, u32[]{:S(2)}, u32[]{:S(2)}) %collective-permute-start.25) | collective-permute-done | bytes 393248 | tf_op jit(solution)/shard_map/ppermute | solution.py:936
  133.5 2.1 %collective-permute-start.36 = (bf16[272,768]{1,0:T(8,128)(2,1)S(1)}, bf16[272,768]{1,0:T(8,128)(2,1)S(1)}, u32[]{:S(2)}, u32[]{:S(2)}) collective-permute-start(bf16[272,768]{1,0:T(8,128)(2,1)S(1)} %add_convert_fusion.2), channel_id=1, source_target_pairs={{0,2},{2,0},{4,6},{6,4},{8,10},{10,8},{12,14},{14,12},{16,18},{18,... | collective-permute-start | bytes 1253384 | tf_op jit(solution)/shard_map/ppermute | solution.py:939
  137.5 2.1 %collective-permute-start.29 = (bf16[80,768]{1,0:T(8,128)(2,1)S(1)}, bf16[80,768]{1,0:T(8,128)(2,1)S(1)}, u32[]{:S(2)}, u32[]{:S(2)}) collective-permute-start(bf16[80,768]{1,0:T(8,128)(2,1)S(1)} %add_convert_fusion.7), channel_id=1, source_target_pairs={{0,2},{2,0},{4,6},{6,4},{8,10},{10,8},{12,14},{14,12},{16,18},{18,... | collective-permute-start | bytes 368648 | tf_op jit(solution)/shard_map/ppermute | solution.py:939
  139.6 12.9 %collective-permute-done.26 = bf16[256,768]{1,0:T(8,128)(2,1)S(1)} collective-permute-done((bf16[256,768]{1,0:T(8,128)(2,1)S(1)}, bf16[256,768]{1,0:T(8,128)(2,1)S(1)}, u32[]{:S(2)}, u32[]{:S(2)}) %collective-permute-start.26) | collective-permute-done | bytes 393248 | tf_op jit(solution)/shard_map/ppermute | solution.py:936
  153.7 3.5 %collective-permute-done.29.refs_1_ = bf16[80,768]{1,0:T(8,128)(2,1)S(1)} collective-permute-done((bf16[80,768]{1,0:T(8,128)(2,1)S(1)}, bf16[80,768]{1,0:T(8,128)(2,1)S(1)}, u32[]{:S(2)}, u32[]{:S(2)}) %collective-permute-start.29) | collective-permute-done | bytes 122912 | tf_op jit(solution)/shard_map/ppermute | solution.py:939
  157.2 2.3 %collective-permute-start.33 = (bf16[80,768]{1,0:T(8,128)(2,1)S(1)}, bf16[80,768]{1,0:T(8,128)(2,1)S(1)}, u32[]{:S(2)}, u32[]{:S(2)}) collective-permute-start(bf16[80,768]{1,0:T(8,128)(2,1)S(1)} %add_convert_fusion.5), channel_id=1, source_target_pairs={{0,6},{2,4},{4,2},{6,0},{8,14},{10,12},{12,10},{14,8},{16,22},{18,... | collective-permute-start | bytes 368648 | tf_op jit(solution)/shard_map/ppermute | solution.py:939
  159.7 3.3 %collective-permute-done.33.refs_3_ = bf16[80,768]{1,0:T(8,128)(2,1)S(1)} collective-permute-done((bf16[80,768]{1,0:T(8,128)(2,1)S(1)}, bf16[80,768]{1,0:T(8,128)(2,1)S(1)}, u32[]{:S(2)}, u32[]{:S(2)}) %collective-permute-start.33) | collective-permute-done | bytes 122912 | tf_op jit(solution)/shard_map/ppermute | solution.py:939
  164.5 2.4 %collective-permute-start.42 = (bf16[96,768]{1,0:T(8,128)(2,1)S(1)}, bf16[96,768]{1,0:T(8,128)(2,1)S(1)}, u32[]{:S(2)}, u32[]{:S(2)}) collective-permute-start(bf16[96,768]{1,0:T(8,128)(2,1)S(1)} %get-tuple-element.92), channel_id=1, source_target_pairs={{0,16},{2,18},{4,20},{6,22},{8,24},{10,26},{12,28},{14,30},{16,0},... | collective-permute-start | bytes 442376 | tf_op jit(solution)/shard_map/ppermute | solution.py:936
  168.6 2.8 %collective-permute-done.41.refs_1_ = bf16[96,768]{1,0:T(8,128)(2,1)S(1)} collective-permute-done((bf16[96,768]{1,0:T(8,128)(2,1)S(1)}, bf16[96,768]{1,0:T(8,128)(2,1)S(1)}, u32[]{:S(2)}, u32[]{:S(2)}) %collective-permute-start.41) | collective-permute-done | bytes 147488 | tf_op jit(solution)/shard_map/ppermute | solution.py:936
  171.4 5.8 %collective-permute-done.42.refs_2_ = bf16[96,768]{1,0:T(8,128)(2,1)S(1)} collective-permute-done((bf16[96,768]{1,0:T(8,128)(2,1)S(1)}, bf16[96,768]{1,0:T(8,128)(2,1)S(1)}, u32[]{:S(2)}, u32[]{:S(2)}) %collective-permute-start.42) | collective-permute-done | bytes 147488 | tf_op jit(solution)/shard_map/ppermute | solution.py:936
  177.2 2.1 %shard_map.114 = (f32[1728,128]{1,0:T(8,128)S(1)}, f32[16,768]{1,0:T(8,128)S(1)}) custom-call(s32[2]{0:T(128)S(1)} %pad_add_fusion.1.where_ref, bf16[96,768]{1,0:T(8,128)(2,1)S(1)} %get-tuple-element.90.refs_0_, bf16[96,768]{1,0:T(8,128)(2,1)S(1)} %collective-permute-done.41.refs_1_, bf16[96,768]{1,0:T(8,128)(2,1)S(1)} %collective-permute-done.42.refs_2_, ...), custom_call_target="tpu_custom_call" | custom-call | tf_op jit(solution)/shard_map/pallas_call | solution.py:905
  181.2 4.1 %multiply_subtract_fusion = (f32[221496]{0:T(1024)}, f32[221496]{0:T(1024)}, f32[221496]{0:T(1024)}, f32[221496]{0:T(1024)}) fusion(f32[221496]{0:T(1024)S(1)} %copy-done.26, f32[221496]{0:T(1024)S(1)} %copy-done.28, f32[221496]{0:T(1024)} %param.11, s32[]{:T(128)S(6)} %select_n.30, f32[9984]{0:T(1024)S(1)} %broadcast_select_fusion, f32[221184]{0:T(1024)S(1)} %bitcast.15), kind=kLoop, calls=%fused_computation.7 | loop fusion | flops 3543936 | bytes 7126564 | tf_op jit(solution)/shard_map/sub | solution.py:271
  (155 shorter events, 51.5 us)
Async XLA Ops:
  13.2 19.3 %collective-permute-start.8 = (bf16[96,768]{1,0:T(8,128)(2,1)S(1)}, bf16[96,768]{1,0:T(8,128)(2,1)S(1)}, u32[]{:S(2)}, u32[]{:S(2)}) collective-permute-start(bf16[96,768]{1,0:T(8,128)(2,1)S(1)} %get-tuple-element.55), channel_id=1, source_target_pairs={{0,16},{2,18},{4,20},{6,22},{8,24},{10,26},{12,28},{14,30},{16,0},... | collective-permute-start | bytes 442376 | tf_op jit(solution)/shard_map/ppermute | solution.py:936
  17.6 20.6 %collective-permute-start.4 = (bf16[128,768]{1,0:T(8,128)(2,1)S(1)}, bf16[128,768]{1,0:T(8,128)(2,1)S(1)}, u32[]{:S(2)}, u32[]{:S(2)}) collective-permute-start(bf16[128,768]{1,0:T(8,128)(2,1)S(1)} %get-tuple-element.52.refs_4_), channel_id=1, source_target_pairs={{0,16},{2,18},{4,20},{6,22},{8,24},{10,26},{12,28},{14,30},{16,0},... | collective-permute-start | bytes 589832 | tf_op jit(solution)/shard_map/ppermute | solution.py:936
  21.9 24.3 %collective-permute-start.1 = (bf16[144,768]{1,0:T(8,128)(2,1)S(1)}, bf16[144,768]{1,0:T(8,128)(2,1)S(1)}, u32[]{:S(2)}, u32[]{:S(2)}) collective-permute-start(bf16[144,768]{1,0:T(8,128)(2,1)S(1)} %get-tuple-element.51.refs_0_), channel_id=1, source_target_pairs={{0,16},{2,18},{4,20},{6,22},{8,24},{10,26},{12,28},{14,30},{16,0},... | collective-permute-start | bytes 663560 | tf_op jit(solution)/shard_map/ppermute | solution.py:936
  22.3 23.2 %collective-permute-start.3 = (bf16[128,768]{1,0:T(8,128)(2,1)S(1)}, bf16[128,768]{1,0:T(8,128)(2,1)S(1)}, u32[]{:S(2)}, u32[]{:S(2)}) collective-permute-start(bf16[128,768]{1,0:T(8,128)(2,1)S(1)} %get-tuple-element.52.refs_4_), channel_id=1, source_target_pairs={{0,8},{2,10},{4,12},{6,14},{8,0},{10,2},{12,4},{14,6},{16,24},{18,... | collective-permute-start | bytes 589832 | tf_op jit(solution)/shard_map/ppermute | solution.py:936
  45.5 19.1 %collective-permute-start.12 = (bf16[192,768]{1,0:T(8,128)(2,1)S(1)}, bf16[192,768]{1,0:T(8,128)(2,1)S(1)}, u32[]{:S(2)}, u32[]{:S(2)}) collective-permute-start(bf16[192,768]{1,0:T(8,128)(2,1)S(1)} %get-tuple-element.57.refs_8_), channel_id=1, source_target_pairs={{0,6},{2,4},{4,2},{6,0},{8,14},{10,12},{12,10},{14,8},{16,22},{18,... | collective-permute-start | bytes 884744 | tf_op jit(solution)/shard_map/ppermute | solution.py:939
  46.2 18.9 %collective-permute-start.11 = (bf16[192,768]{1,0:T(8,128)(2,1)S(1)}, bf16[192,768]{1,0:T(8,128)(2,1)S(1)}, u32[]{:S(2)}, u32[]{:S(2)}) collective-permute-start(bf16[192,768]{1,0:T(8,128)(2,1)S(1)} %get-tuple-element.57.refs_8_), channel_id=1, source_target_pairs={{0,4},{2,6},{4,0},{6,2},{8,12},{10,14},{12,8},{14,10},{16,20},{18,... | collective-permute-start | bytes 884744 | tf_op jit(solution)/shard_map/ppermute | solution.py:939
  50.8 18.2 %collective-permute-start.10 = (bf16[192,768]{1,0:T(8,128)(2,1)S(1)}, bf16[192,768]{1,0:T(8,128)(2,1)S(1)}, u32[]{:S(2)}, u32[]{:S(2)}) collective-permute-start(bf16[192,768]{1,0:T(8,128)(2,1)S(1)} %get-tuple-element.57.refs_8_), channel_id=1, source_target_pairs={{0,2},{2,0},{4,6},{6,4},{8,10},{10,8},{12,14},{14,12},{16,18},{18,... | collective-permute-start | bytes 884744 | tf_op jit(solution)/shard_map/ppermute | solution.py:939
  75.0 22.1 %collective-permute-start.20 = (bf16[160,768]{1,0:T(8,128)(2,1)}, bf16[160,768]{1,0:T(8,128)(2,1)}, u32[]{:S(2)}, u32[]{:S(2)}) collective-permute-start(bf16[160,768]{1,0:T(8,128)(2,1)} %get-tuple-element.66.refs_8_), channel_id=1, source_target_pairs={{0,1},{1,0},{2,3},{3,2},{4,5},{5,4},{6,7},{7,6},{8,9},{9,8},{10,11... | collective-permute-start | bytes 737288 | tf_op jit(solution)/shard_map/ppermute | solution.py:942
  75.0 22.6 %collective-permute-start.23 = (bf16[160,768]{1,0:T(8,128)(2,1)}, bf16[160,768]{1,0:T(8,128)(2,1)}, u32[]{:S(2)}, u32[]{:S(2)}) collective-permute-start(bf16[160,768]{1,0:T(8,128)(2,1)} %collective-permute-done.19.refs_11_), channel_id=1, source_target_pairs={{0,1},{1,0},{2,3},{3,2},{4,5},{5,4},{6,7},{7,6},{8,9},{9,8},{10,11... | collective-permute-start | bytes 737288 | tf_op jit(solution)/shard_map/ppermute | solution.py:942
  75.5 22.2 %collective-permute-start.22 = (bf16[160,768]{1,0:T(8,128)(2,1)}, bf16[160,768]{1,0:T(8,128)(2,1)}, u32[]{:S(2)}, u32[]{:S(2)}) collective-permute-start(bf16[160,768]{1,0:T(8,128)(2,1)} %collective-permute-done.18.refs_10_), channel_id=1, source_target_pairs={{0,1},{1,0},{2,3},{3,2},{4,5},{5,4},{6,7},{7,6},{8,9},{9,8},{10,11... | collective-permute-start | bytes 737288 | tf_op jit(solution)/shard_map/ppermute | solution.py:942
  75.6 22.5 %collective-permute-start.21 = (bf16[160,768]{1,0:T(8,128)(2,1)}, bf16[160,768]{1,0:T(8,128)(2,1)}, u32[]{:S(2)}, u32[]{:S(2)}) collective-permute-start(bf16[160,768]{1,0:T(8,128)(2,1)} %collective-permute-done.17.refs_9_), channel_id=1, source_target_pairs={{0,1},{1,0},{2,3},{3,2},{4,5},{5,4},{6,7},{7,6},{8,9},{9,8},{10,11... | collective-permute-start | bytes 737288 | tf_op jit(solution)/shard_map/ppermute | solution.py:942
  96.1 17.5 %collective-permute-start.27 = (bf16[80,768]{1,0:T(8,128)(2,1)}, bf16[80,768]{1,0:T(8,128)(2,1)}, u32[]{:S(2)}, u32[]{:S(2)}) collective-permute-start(bf16[80,768]{1,0:T(8,128)(2,1)} %get-tuple-element.75), channel_id=1, source_target_pairs={{0,1},{1,0},{2,3},{3,2},{4,5},{5,4},{6,7},{7,6},{8,9},{9,8},{10,11... | collective-permute-start | bytes 368648 | tf_op jit(solution)/shard_map/ppermute | solution.py:942
  97.1 17.7 %collective-permute-start.28 = (bf16[80,768]{1,0:T(8,128)(2,1)}, bf16[80,768]{1,0:T(8,128)(2,1)S(1)}, u32[]{:S(2)}, u32[]{:S(2)}) collective-permute-start(bf16[80,768]{1,0:T(8,128)(2,1)} %copy-done.25), channel_id=1, source_target_pairs={{0,1},{1,0},{2,3},{3,2},{4,5},{5,4},{6,7},{7,6},{8,9},{9,8},{10,11... | collective-permute-start | bytes 368648 | tf_op jit(solution)/shard_map/ppermute | solution.py:942
  97.6 17.4 %collective-permute-start.30 = (bf16[80,768]{1,0:T(8,128)(2,1)}, bf16[80,768]{1,0:T(8,128)(2,1)S(1)}, u32[]{:S(2)}, u32[]{:S(2)}) collective-permute-start(bf16[80,768]{1,0:T(8,128)(2,1)} %copy-done.24), channel_id=1, source_target_pairs={{0,1},{1,0},{2,3},{3,2},{4,5},{5,4},{6,7},{7,6},{8,9},{9,8},{10,11... | collective-permute-start | bytes 368648 | tf_op jit(solution)/shard_map/ppermute | solution.py:942
  97.7 17.9 %collective-permute-start.32 = (bf16[80,768]{1,0:T(8,128)(2,1)}, bf16[80,768]{1,0:T(8,128)(2,1)S(1)}, u32[]{:S(2)}, u32[]{:S(2)}) collective-permute-start(bf16[80,768]{1,0:T(8,128)(2,1)} %copy-done.23), channel_id=1, source_target_pairs={{0,1},{1,0},{2,3},{3,2},{4,5},{5,4},{6,7},{7,6},{8,9},{9,8},{10,11... | collective-permute-start | bytes 368648 | tf_op jit(solution)/shard_map/ppermute | solution.py:942
  111.8 25.7 %collective-permute-start.24 = (bf16[256,768]{1,0:T(8,128)(2,1)S(1)}, bf16[256,768]{1,0:T(8,128)(2,1)S(1)}, u32[]{:S(2)}, u32[]{:S(2)}) collective-permute-start(bf16[256,768]{1,0:T(8,128)(2,1)S(1)} %get-tuple-element.68), channel_id=1, source_target_pairs={{0,8},{2,10},{4,12},{6,14},{8,0},{10,2},{12,4},{14,6},{16,24},{18,... | collective-permute-start | bytes 1179656 | tf_op jit(solution)/shard_map/ppermute | solution.py:936
  113.6 17.8 %collective-permute-start.25 = (bf16[256,768]{1,0:T(8,128)(2,1)S(1)}, bf16[256,768]{1,0:T(8,128)(2,1)S(1)}, u32[]{:S(2)}, u32[]{:S(2)}) collective-permute-start(bf16[256,768]{1,0:T(8,128)(2,1)S(1)} %get-tuple-element.70), channel_id=1, source_target_pairs={{0,8},{2,10},{4,12},{6,14},{8,0},{10,2},{12,4},{14,6},{16,24},{18,... | collective-permute-start | bytes 1179656 | tf_op jit(solution)/shard_map/ppermute | solution.py:936
  114.8 22.2 %collective-permute-start.34 = (bf16[272,768]{1,0:T(8,128)(2,1)S(1)}, bf16[272,768]{1,0:T(8,128)(2,1)S(1)}, u32[]{:S(2)}, u32[]{:S(2)}) collective-permute-start(bf16[272,768]{1,0:T(8,128)(2,1)S(1)} %get-tuple-element.83), channel_id=1, source_target_pairs={{0,1},{1,0},{2,3},{3,2},{4,5},{5,4},{6,7},{7,6},{8,9},{9,8},{10,11... | collective-permute-start | bytes 1253384 | tf_op jit(solution)/shard_map/ppermute | solution.py:942
  115.6 17.9 %collective-permute-start.37 = (bf16[272,768]{1,0:T(8,128)(2,1)S(1)}, bf16[272,768]{1,0:T(8,128)(2,1)S(1)}, u32[]{:S(2)}, u32[]{:S(2)}) collective-permute-start(bf16[272,768]{1,0:T(8,128)(2,1)S(1)} %get-tuple-element.87), channel_id=1, source_target_pairs={{0,1},{1,0},{2,3},{3,2},{4,5},{5,4},{6,7},{7,6},{8,9},{9,8},{10,11... | collective-permute-start | bytes 1253384 | tf_op jit(solution)/shard_map/ppermute | solution.py:942
  131.5 20.9 %collective-permute-start.26 = (bf16[256,768]{1,0:T(8,128)(2,1)S(1)}, bf16[256,768]{1,0:T(8,128)(2,1)S(1)}, u32[]{:S(2)}, u32[]{:S(2)}) collective-permute-start(bf16[256,768]{1,0:T(8,128)(2,1)S(1)} %add_convert_fusion.4), channel_id=1, source_target_pairs={{0,16},{2,18},{4,20},{6,22},{8,24},{10,26},{12,28},{14,30},{16,0},... | collective-permute-start | bytes 1179656 | tf_op jit(solution)/shard_map/ppermute | solution.py:936
  133.5 29.5 %collective-permute-start.36 = (bf16[272,768]{1,0:T(8,128)(2,1)S(1)}, bf16[272,768]{1,0:T(8,128)(2,1)S(1)}, u32[]{:S(2)}, u32[]{:S(2)}) collective-permute-start(bf16[272,768]{1,0:T(8,128)(2,1)S(1)} %add_convert_fusion.2), channel_id=1, source_target_pairs={{0,2},{2,0},{4,6},{6,4},{8,10},{10,8},{12,14},{14,12},{16,18},{18,... | collective-permute-start | bytes 1253384 | tf_op jit(solution)/shard_map/ppermute | solution.py:939
  135.6 27.3 %collective-permute-start.38 = (bf16[272,768]{1,0:T(8,128)(2,1)S(1)}, bf16[272,768]{1,0:T(8,128)(2,1)S(1)}, u32[]{:S(2)}, u32[]{:S(2)}) collective-permute-start(bf16[272,768]{1,0:T(8,128)(2,1)S(1)} %add_convert_fusion.1), channel_id=1, source_target_pairs={{0,4},{2,6},{4,0},{6,2},{8,12},{10,14},{12,8},{14,10},{16,20},{18,... | collective-permute-start | bytes 1253384 | tf_op jit(solution)/shard_map/ppermute | solution.py:939
  137.0 26.0 %collective-permute-start.40 = (bf16[272,768]{1,0:T(8,128)(2,1)S(1)}, bf16[272,768]{1,0:T(8,128)(2,1)S(1)}, u32[]{:S(2)}, u32[]{:S(2)}) collective-permute-start(bf16[272,768]{1,0:T(8,128)(2,1)S(1)} %add_convert_fusion), channel_id=1, source_target_pairs={{0,6},{2,4},{4,2},{6,0},{8,14},{10,12},{12,10},{14,8},{16,22},{18,... | collective-permute-start | bytes 1253384 | tf_op jit(solution)/shard_map/ppermute | solution.py:939
  137.5 19.7 %collective-permute-start.29 = (bf16[80,768]{1,0:T(8,128)(2,1)S(1)}, bf16[80,768]{1,0:T(8,128)(2,1)S(1)}, u32[]{:S(2)}, u32[]{:S(2)}) collective-permute-start(bf16[80,768]{1,0:T(8,128)(2,1)S(1)} %add_convert_fusion.7), channel_id=1, source_target_pairs={{0,2},{2,0},{4,6},{6,4},{8,10},{10,8},{12,14},{14,12},{16,18},{18,... | collective-permute-start | bytes 368648 | tf_op jit(solution)/shard_map/ppermute | solution.py:939
  (50 other events, 324.4 us)
